TPU v7x, 128 devices: a whole 4x4x4 slice. The times are simulated.
128 devices in a mesh: row: 16 (over z_lo, x, core), col: 8 (over y, z_hi).
Axes of the slice: x: 4, y: 4, z: 4 (z_hi: 2, z_lo: 2; z = z_hi * 2 + z_lo), core: 2. Of those that a mesh axis runs over, the one named last changes fastest.
Arguments:
- amplitudes: bfloat16 [7168, 7168], P('row', 'col'), as said below
- integrals: bfloat16 [7168, 7168], P('row', 'col'), as said below
- occ_energy: float32 [80], replicated, may hold values from -2 to -0.5
- vir_energy: float32 [1000], replicated, may hold values from 0.5 to 4
- pair_occ: int32 [7168], replicated, may hold values from 0 to 79, as said below
- pair_vir: int32 [7168], replicated, may hold values from 0 to 999, as said below
Outputs:
- updated: float32 [7168, 7168], P('row', 'col')
Inputs may be any that keep to these rules, and one draw needn't show every extreme that they name: amplitudes is exactly symmetric. integrals is exactly symmetric. pair_occ[p] mod 8 equals pair_vir[p] mod 8 (one irrep block), and no pair (pair_occ[p], pair_vir[p]) occurs twice. `pair_vir`: see pair_occ.
All inputs are finite; a program needn't handle non-finite values.
Results may differ from a plain program's by a relative error of at most 0.0003.
Values may be sent and summed in bfloat16 or wider, within the bound.
No kernel may reach another device: no remote copies, remote signals or barrier semaphores. Data moves between devices by JAX's collectives and lax.ppermute only.
A program may use at most 128 MiB of HBM per device.

v0:
```python
import jax
import jax.numpy as jnp
from jax import lax
from jax.sharding import PartitionSpec as P


def lookup(energies, orbital_index):
    labels = jnp.arange(energies.shape[0], dtype=jnp.int32)
    picked = jnp.where(orbital_index[:, None] == labels[None, :], energies[None, :], 0.0)
    return jnp.sum(picked, axis=1)


def shards(amplitudes, integrals, occ_energy, vir_energy, pair_occ, pair_vir):
    tile_rows, tile_cols = amplitudes.shape
    left_local = jnp.stack((amplitudes, integrals))
    right_local = jnp.stack((integrals, amplitudes))
    row_panels = lax.all_gather(left_local, "col", axis=2, tiled=True)
    summed = jnp.einsum(
        "lrk,lkc->rc",
        row_panels,
        lax.all_gather(right_local, "row", axis=1, tiled=True),
        preferred_element_type=jnp.float32,
    )
    row_start = lax.axis_index("row") * tile_rows
    col_start = lax.axis_index("col") * tile_cols
    row_occ = lax.dynamic_slice_in_dim(pair_occ, row_start, tile_rows)
    row_vir = lax.dynamic_slice_in_dim(pair_vir, row_start, tile_rows)
    col_occ = lax.dynamic_slice_in_dim(pair_occ, col_start, tile_cols)
    col_vir = lax.dynamic_slice_in_dim(pair_vir, col_start, tile_cols)
    row_gap = lookup(occ_energy, row_occ) - lookup(vir_energy, row_vir)
    col_gap = lookup(occ_energy, col_occ) - lookup(vir_energy, col_vir)
    return summed / (row_gap[:, None] + col_gap[None, :])


def solution(mesh):
    return jax.shard_map(
        shards,
        mesh=mesh,
        in_specs=(P("row", "col"), P("row", "col"), P(), P(), P(), P()),
        out_specs=P("row", "col"),
        check_vma=False,
    )
```

profile of v0, /device:TPU:16, one launch (start us, length us, event | category | flops | bytes accessed | tf_op | source)
XLA Modules:
  0.0 322.3 jit_solution(3779648207988396233)
XLA Ops:
  6.5 0.0 all-gather.3.cloned.1.call-start
  6.5 4.0 %pad_maximum_fusion.1 = (bf16[2,448,896]{2,1,0:T(8,128)(2,1)}, bf16[2,448,896]{2,1,0:T(8,128)(2,1)}) fusion(bf16[1,448,896]{2,1,0:T(8,128)(2,1)} %bitcast.6, bf16[1,448,896]{2,1,0:T(8,128)(2,1)} %bitcast.7), kind=kLoop, calls=%fused_computation.5 | loop fusion | flops 1605632 | bytes 4816896 | tf_op jit(solution)/shard_map/stack | solution.py:16
  10.5 0.0 copy-start.1
  10.5 0.0 copy-start
  10.5 0.0 all-gather.3.cloned.1.call-update
  10.5 0.0 all-gather.5.cloned.1.call-start
  10.6 0.7 all-gather.5.cloned.1.call-update
  11.3 0.8 dynamic_slice.14
  12.1 0.8 dynamic_slice.15
  12.9 0.8 dynamic_slice.12
  13.6 0.8 dynamic_slice.13
  14.4 0.0 copy-done.1
  14.4 0.1 select_reduce_fusion.2
  14.5 0.0 copy-done
  14.5 0.5 select_reduce_fusion
  15.0 0.1 select_reduce_fusion.3
  15.1 0.3 select_reduce_fusion.1
  15.5 144.0 %all-gather.3.cloned.1.call-done = bf16[2,448,7168]{2,1,0:T(8,128)(2,1)} async-done(((bf16[2,448,896]{2,1,0:T(8,128)(2,1)}), bf16[2,448,7168]{2,1,0:T(8,128)(2,1)}) %all-gather.3.cloned.1.call-update) | async-done | bytes 12845072 | tf_op jit(solution)/shard_map/all_gather | solution.py:17
  159.4 134.5 %all-gather.5.cloned.1.call-done = bf16[2,7168,896]{2,1,0:T(8,128)(2,1)} async-done(((bf16[2,448,896]{2,1,0:T(8,128)(2,1)}), bf16[2,7168,896]{2,1,0:T(8,128)(2,1)}) %all-gather.5.cloned.1.call-update) | async-done | bytes 25690128 | tf_op jit(solution)/shard_map/all_gather | solution.py:21
  293.9 21.5 %bitcast_divide_fusion = f32[448,896]{1,0:T(8,128)} fusion(bf16[2,448,7168]{2,1,0:T(8,128)(2,1)} %all-gather.3.cloned.1.call-done, bf16[2,7168,896]{2,1,0:T(8,128)(2,1)} %all-gather.5.cloned.1.call-done, f32[896]{0:T(1024)S(1)} %sub.15, f32[448]{0:T(512)S(1)} %sub.14), kind=kOutput, calls=%fused_computation.6 | convolution fusion | flops 11509972992 | bytes 40146176 | tf_op jit(solution)/shard_map/lrk,lkc->rc/dot_general | solution.py:18
  (2 shorter events, 0.0 us)
Async XLA Ops:
  6.5 152.9 %all-gather.3.cloned.1.call-start = ((), (), s32[]{:S(2)}) async-start(), calls=%async_computation | async-start | bytes 14450688 | tf_op jit(solution)/shard_map/all_gather | solution.py:17
  10.5 3.9 %copy-start.1 = (f32[80]{0:T(128)S(1)}, f32[80]{0:T(128)}, u32[]{:S(2)}) copy-start(f32[80]{0:T(128)} %param.8) | copy-start | bytes 964
  10.5 4.0 %copy-start = (f32[1000]{0:T(1024)S(1)}, f32[1000]{0:T(1024)}, u32[]{:S(2)}) copy-start(f32[1000]{0:T(1024)} %param.9) | copy-start | bytes 12004
  10.5 283.4 %all-gather.5.cloned.1.call-start = ((), (), s32[]{:S(2)}) async-start(), calls=%async_computation.1 | async-start | bytes 27295744 | tf_op jit(solution)/shard_map/all_gather | solution.py:21
Sparse Core Ops, SparseCore 0:
  10.7 148.7 all-gather.2
  161.1 132.7 all-gather.4
where the time goes:
time: 324 us; the launch traced here: 322 us
  waiting for transfers between devices  279 us (86%)
  matrix products  21.5 us (7%)
  between operations  13.4 us (4%)
  other arithmetic  5.01 us (2%)
    all_gather x1, waiting for transfers between devices, shards(): row_panels = lax.all_gather(left_local, 'col', axis=2, tiled=True)  144 us
    all_gather x1, waiting for transfers between devices, shards(): lax.all_gather(right_local, 'row', axis=1, tiled=True)  134 us
    dot_general x1, matrix products, shards(): jnp.einsum('lrk,lkc->rc', row_panels, lax.all_gather(right_local, 'row',...  21.5 us
  transfers between devices with their start and end apart: 2, of which 2 were waited for; matrix products, arithmetic and copies ran while one was open for 1% of the time, Pallas kernels for 0%

commit v1 on v0

v1 whole, which is shorter than its diff:
```python
import jax
import jax.numpy as jnp
from jax import lax
from jax.experimental import pallas as pl
from jax.experimental.pallas import tpu as pltpu
from jax.sharding import PartitionSpec as P

Z_LO, X, CORE, Y, Z_HI = 2, 4, 2, 4, 2
AXES = ("row", "col")
LEVELS = 15


def device_index(z_lo, x, core, y, z_hi):
    return ((z_lo * X + x) * CORE + core) * (Y * Z_HI) + y * Z_HI + z_hi


def places():
    for z_lo in range(Z_LO):
        for x in range(X):
            for core in range(CORE):
                for y in range(Y):
                    for z_hi in range(Z_HI):
                        yield z_lo, x, core, y, z_hi


def send(block, target):
    pairs = [(device_index(*place), device_index(*target(*place))) for place in places()]
    return lax.ppermute(block, AXES, pairs)


def along_x(step):
    return lambda z_lo, x, core, y, z_hi: (z_lo, (x + step) % X, core, y, z_hi)


def along_y(step):
    return lambda z_lo, x, core, y, z_hi: (z_lo, x, core, (y + step) % Y, z_hi)


def across_z_lo(z_lo, x, core, y, z_hi):
    return 1 - z_lo, x, core, y, z_hi


def across_z_hi(z_lo, x, core, y, z_hi):
    return z_lo, x, core, y, 1 - z_hi


def across_core(z_lo, x, core, y, z_hi):
    return z_lo, x, 1 - core, y, z_hi


def mirrored(flip):
    def target(z_lo, x, core, y, z_hi):
        chip_row, chip_col = z_lo * X + x, y * Z_HI + z_hi
        return chip_col // X, chip_col % X, core ^ flip, chip_row // Z_HI, chip_row % Z_HI

    return target


def ring(block, along):
    half = block.shape[0] // 2
    before = send(block, along(1))
    after = send(block, along(-1))
    top = send(before[:half], along(1))
    bottom = send(after[half:], along(-1))
    return [(block,), (after,), (top, bottom), (before,)]


def gather(block, along, across):
    return ring(block, along) + ring(send(block, across), along)


def lookup(energies, orbital_index):
    labels = jnp.arange(energies.shape[0], dtype=jnp.int32)
    picked = jnp.where(orbital_index[:, None] == labels[None, :], energies[None, :], 0.0)
    return jnp.sum(picked, axis=1)


def product_kernel(counts_a, counts_b, *refs):
    total_a, total_b = sum(counts_a), sum(counts_b)
    a_parts, b_parts, rest = refs[:total_a], refs[total_a:total_a + total_b], refs[total_a + total_b:]
    out_ref, left, right, acc, sem_a, sem_b = rest
    row, col = lax.axis_index("row"), lax.axis_index("col")
    z_lo, x, core = row // (X * CORE), (row // CORE) % X, row % CORE
    y, z_hi = col // Z_HI, col % Z_HI
    rows, depth = left.shape[1], left.shape[2]
    copies_a, copies_b = [], []
    at = 0
    for slot, count in enumerate(counts_a):
        part = rows // count
        for i in range(count):
            copies_a.append(pltpu.make_async_copy(
                a_parts[at], left.at[slot, pl.ds(i * part, part), :], sem_a.at[at]))
            at += 1
    half = depth // CORE
    at = 0
    for slot in range(len(counts_b) // 2):
        mine = []
        for other in range(CORE):
            base = pl.multiple_of((core if other == 0 else 1 - core) * half, half)
            count = counts_b[2 * slot + other]
            part = half // count
            for i in range(count):
                mine.append(pltpu.make_async_copy(
                    b_parts[at], right.at[slot, pl.ds(base + i * part, part), :], sem_b.at[at]))
                at += 1
        copies_b.append(mine)
    for copy in copies_a:
        copy.start()
    for mine in copies_b:
        for copy in mine:
            copy.start()
    for copy in copies_a:
        copy.wait()
    for slot, mine in enumerate(copies_b):
        for copy in mine:
            copy.wait()
        z_part = z_lo if slot < X else 1 - z_lo
        block = z_part * X + lax.rem(x + slot % X, X)
        other = (block % Z_HI + z_hi) % 2
        place = other * Y + lax.rem(block // Z_HI - y + Y, Y)
        term = jnp.dot(left[place], right[slot], preferred_element_type=jnp.float32)
        if slot == 0:
            acc[...] = term
        elif slot < len(copies_b) - 1:
            acc[...] += term
        else:
            out_ref[...] = acc[...] + term


def local_product(a_groups, b_groups, rows, cols):
    counts_a, counts_b = [len(g) for g in a_groups], [len(g) for g in b_groups]
    parts = [p for g in a_groups for p in g] + [p for g in b_groups for p in g]
    slots = len(a_groups)
    depth = a_groups[0][0].shape[1]
    return pl.pallas_call(
        lambda *refs: product_kernel(counts_a, counts_b, *refs),
        out_shape=jax.ShapeDtypeStruct((rows, cols), jnp.float32),
        in_specs=[pl.BlockSpec(memory_space=pl.ANY)] * len(parts),
        out_specs=pl.BlockSpec(memory_space=pltpu.VMEM),
        scratch_shapes=[
            pltpu.VMEM((slots, rows, depth), jnp.bfloat16),
            pltpu.VMEM((slots, depth, cols), jnp.bfloat16),
            pltpu.VMEM((rows, cols), jnp.float32),
            pltpu.SemaphoreType.DMA((sum(counts_a),)),
            pltpu.SemaphoreType.DMA((sum(counts_b),)),
        ],
        compiler_params=pltpu.CompilerParams(vmem_limit_bytes=36 * 2**20),
        cost_estimate=pl.CostEstimate(
            flops=2 * rows * cols * depth * slots, bytes_accessed=20 * 2**20, transcendentals=0),
        name="local_product",
    )(*parts)


def encode(product):
    top = jnp.maximum(jnp.max(jnp.abs(product), axis=0, keepdims=True), 1e-30)
    power = jnp.ceil(jnp.log2(top) + 1e-3)
    coded = jnp.round(product * jnp.exp2(LEVELS - power)).astype(jnp.int16)
    return jnp.concatenate([coded, jnp.broadcast_to(power.astype(jnp.int16), (16, product.shape[1]))])


def decode(payload):
    power = payload[-1:].astype(jnp.float32)
    return payload[:-16].astype(jnp.float32) * jnp.exp2(power - LEVELS)


def shards(amplitudes, integrals, occ_energy, vir_energy, pair_occ, pair_vir):
    tile_rows, tile_cols = amplitudes.shape
    core = lax.axis_index("row") % CORE
    a_groups = gather(amplitudes, along_y, across_z_hi)
    b_groups = []
    for group in gather(integrals, along_x, across_z_lo):
        b_groups += [group, tuple(send(part, across_core) for part in group)]
    product = local_product(a_groups, b_groups, tile_rows, tile_cols)

    payload = encode(product)
    low, high = payload[:, :tile_rows], payload[:, tile_rows:]
    same = decode(send(jnp.where(core == 0, low, high), mirrored(0))).T
    cross = decode(send(jnp.where(core == 0, high, low), mirrored(1))).T
    mirror = jnp.concatenate([jnp.where(core == 0, same, cross), jnp.where(core == 0, cross, same)], axis=1)

    row_start = lax.axis_index("row") * tile_rows
    col_start = lax.axis_index("col") * tile_cols
    row_occ = lax.dynamic_slice_in_dim(pair_occ, row_start, tile_rows)
    row_vir = lax.dynamic_slice_in_dim(pair_vir, row_start, tile_rows)
    col_occ = lax.dynamic_slice_in_dim(pair_occ, col_start, tile_cols)
    col_vir = lax.dynamic_slice_in_dim(pair_vir, col_start, tile_cols)
    row_gap = lookup(occ_energy, row_occ) - lookup(vir_energy, row_vir)
    col_gap = lookup(occ_energy, col_occ) - lookup(vir_energy, col_vir)
    return (product + mirror) / (row_gap[:, None] + col_gap[None, :])


def solution(mesh):
    return jax.shard_map(
        shards,
        mesh=mesh,
        in_specs=(P("row", "col"), P("row", "col"), P(), P(), P(), P()),
        out_specs=P("row", "col"),
        check_vma=False,
    )
```

time: 324 us -> 193 us (0.60)
  the two profiles are of different devices: /device:TPU:16 before, /device:TPU:121 now
where the time goes in v1:
time: 193 us; the launch traced here: 192 us
  waiting for transfers between devices  100 us (52%)
  starting transfers between devices  36.2 us (19%)
  local copies, waits for them, and re-layouts  35 us (18%)
  Pallas kernels  12.7 us (7%)
  other arithmetic  7.32 us (4%)
    ppermute x30, waiting for transfers between devices, send(): return lax.ppermute(block, AXES, pairs)  100 us
    ppermute x30, starting transfers between devices, send(): return lax.ppermute(block, AXES, pairs)  36.2 us
    unnamed x70, local copies, waits for them, and re-layouts  26.9 us
    pallas_call x1, Pallas kernels, local_product(): pl.pallas_call(lambda *refs: product_kernel(counts_a, counts_b, *refs), o...  12.7 us
  transfers between devices with their start and end apart: 30, of which 11 were waited for; matrix products, arithmetic and copies ran while one was open for 4% of the time, Pallas kernels for 0%

profile of v1, /device:TPU:121, one launch (start us, length us, event | category | flops | bytes accessed | tf_op | source)
XLA Modules:
  0.0 191.9 jit_solution(17791395849182348846)
XLA Ops:
  0.0 1.2 collective-permute-start.12
  1.2 1.5 collective-permute-start.10
  3.0 17.2 %collective-permute-done.12.refs_18_ = bf16[448,896]{1,0:T(8,128)(2,1)S(1)} collective-permute-done((bf16[448,896]{1,0:T(8,128)(2,1)}, bf16[448,896]{1,0:T(8,128)(2,1)S(1)}, u32[]{:S(2)}, u32[]{:S(2)}) %collective-permute-start.12) | collective-permute-done | bytes 802848 | tf_op jit(solution)/shard_map/ppermute | solution.py:28
  20.6 1.8 collective-permute-start.9
  23.2 2.3 %collective-permute-start.14 = (bf16[224,896]{1,0:T(8,128)(2,1)S(1)}, bf16[224,896]{1,0:T(8,128)(2,1)S(1)}, u32[]{:S(2)}, u32[]{:S(2)}) collective-permute-start(bf16[224,896]{1,0:T(8,128)(2,1)S(1)} %slice.61), channel_id=1, source_target_pairs={{0,48},{1,49},{2,50},{3,51},{4,52},{5,53},{6,54},{7,55},{8,56},{9,... | collective-permute-start | bytes 1204232 | tf_op jit(solution)/shard_map/ppermute | solution.py:28
  25.4 11.7 %collective-permute-done.4.refs_5_ = bf16[448,896]{1,0:T(8,128)(2,1)S(1)} collective-permute-done((bf16[448,896]{1,0:T(8,128)(2,1)}, bf16[448,896]{1,0:T(8,128)(2,1)S(1)}, u32[]{:S(2)}, u32[]{:S(2)}) %collective-permute-start.4) | collective-permute-done | bytes 802848 | tf_op jit(solution)/shard_map/ppermute | solution.py:28
  38.2 1.3 collective-permute-done.refs_1_
  40.4 2.7 %collective-permute-start.20 = (bf16[448,896]{1,0:T(8,128)(2,1)S(1)}, bf16[448,896]{1,0:T(8,128)(2,1)}, u32[]{:S(2)}, u32[]{:S(2)}) collective-permute-start(bf16[448,896]{1,0:T(8,128)(2,1)S(1)} %collective-permute-done.18.refs_20_), channel_id=1, source_target_pairs={{0,48},{1,49},{2,50},{3,51},{4,52},{5,53},{6,54},{7,55},{8,56},{9,... | collective-permute-start | bytes 2408456 | tf_op jit(solution)/shard_map/ppermute | solution.py:28
  43.2 1.4 collective-permute-start.5
  44.6 1.2 collective-permute-done.2.refs_2_
  46.6 1.2 collective-permute-start.3
  47.8 21.3 %collective-permute-done.3.refs_3_ = bf16[224,896]{1,0:T(8,128)(2,1)S(1)} collective-permute-done((bf16[224,896]{1,0:T(8,128)(2,1)S(1)}, bf16[224,896]{1,0:T(8,128)(2,1)S(1)}, u32[]{:S(2)}, u32[]{:S(2)}) %collective-permute-start.3) | collective-permute-done | bytes 401440 | tf_op jit(solution)/shard_map/ppermute | solution.py:28
  69.9 4.3 %collective-permute-start.19 = (bf16[448,896]{1,0:T(8,128)(2,1)S(1)}, bf16[448,896]{1,0:T(8,128)(2,1)S(1)}, u32[]{:S(2)}, u32[]{:S(2)}) collective-permute-start(bf16[448,896]{1,0:T(8,128)(2,1)S(1)} %collective-permute-done.18.refs_20_), channel_id=1, source_target_pairs={{0,8},{1,9},{2,10},{3,11},{4,12},{5,13},{6,14},{7,15},{8,0},{9,1},... | collective-permute-start | bytes 2408456 | tf_op jit(solution)/shard_map/ppermute | solution.py:28
  80.4 2.7 %collective-permute-start.24 = (bf16[224,896]{1,0:T(8,128)(2,1)S(1)}, bf16[224,896]{1,0:T(8,128)(2,1)}, u32[]{:S(2)}, u32[]{:S(2)}) collective-permute-start(bf16[224,896]{1,0:T(8,128)(2,1)S(1)} %slice.63), channel_id=1, source_target_pairs={{0,48},{1,49},{2,50},{3,51},{4,52},{5,53},{6,54},{7,55},{8,56},{9,... | collective-permute-start | bytes 1204232 | tf_op jit(solution)/shard_map/ppermute | solution.py:28
  86.9 4.6 %collective-permute-done.23.refs_24_ = bf16[224,896]{1,0:T(8,128)(2,1)} collective-permute-done((bf16[224,896]{1,0:T(8,128)(2,1)S(1)}, bf16[224,896]{1,0:T(8,128)(2,1)}, u32[]{:S(2)}, u32[]{:S(2)}) %collective-permute-start.23) | collective-permute-done | bytes 401440 | tf_op jit(solution)/shard_map/ppermute | solution.py:28
  91.7 1.5 collective-permute-start.25
  93.2 3.3 %collective-permute-done.7.refs_7_ = bf16[224,896]{1,0:T(8,128)(2,1)S(1)} collective-permute-done((bf16[224,896]{1,0:T(8,128)(2,1)S(1)}, bf16[224,896]{1,0:T(8,128)(2,1)S(1)}, u32[]{:S(2)}, u32[]{:S(2)}) %collective-permute-start.7) | collective-permute-done | bytes 401440 | tf_op jit(solution)/shard_map/ppermute | solution.py:28
  97.2 1.3 collective-permute-start.26
  103.8 1.1 copy-done.3
  104.9 1.1 copy-done.4
  106.1 1.1 copy-done.5
  107.2 1.1 copy-done.7
  108.3 1.1 copy-done.9
  121.0 12.7 %local_product.1 = f32[448,896]{1,0:T(8,128)} custom-call(bf16[448,896]{1,0:T(8,128)(2,1)S(1)} %copy-done.4, bf16[448,896]{1,0:T(8,128)(2,1)S(1)} %collective-permute-done.refs_1_, bf16[224,896]{1,0:T(8,128)(2,1)S(1)} %copy-done.23, bf16[224,896]{1,0:T(8,128)(2,1)S(1)} %copy-done.25, bf16[448,896]{1,0:T(8,128)(2,1)S(1)} %collective-permute-done.1.refs_4_, ...), custom_call_target="tpu_custom_call" | custom-call | flops 5754585088 | bytes 20971520 | tf_op jit(solution)/shard_map/local_product/pallas_call | solution.py:135
  133.8 1.6 abs_reduce_fusion
  135.7 1.8 copy.10
  137.5 1.8 round-nearest-even_convert_fusion
  139.8 2.1 %collective-permute-start.29 = (s16[464,448]{0,1:T(8,128)(2,1)S(1)}, s16[464,448]{0,1:T(8,128)(2,1)S(1)}, u32[]{:S(2)}, u32[]{:S(2)}) collective-permute-start(s16[464,448]{0,1:T(8,128)(2,1)S(1)} %get-tuple-element.6), channel_id=1, source_target_pairs={{0,8},{1,24},{2,40},{3,56},{4,72},{5,88},{6,104},{7,120},{8,0},{9,... | collective-permute-start | bytes 1247240 | tf_op jit(solution)/shard_map/ppermute | solution.py:28
  142.0 7.9 %collective-permute-start.28 = (s16[464,448]{0,1:T(8,128)(2,1)S(1)}, s16[464,448]{0,1:T(8,128)(2,1)S(1)}, u32[]{:S(2)}, u32[]{:S(2)}) collective-permute-start(s16[464,448]{0,1:T(8,128)(2,1)S(1)} %get-tuple-element.5), channel_id=1, source_target_pairs={{0,0},{1,16},{2,32},{3,48},{4,64},{5,80},{6,96},{7,112},{8,8},{9,2... | collective-permute-start | bytes 1247240 | tf_op jit(solution)/shard_map/ppermute | solution.py:28
  150.5 29.1 %collective-permute-done.29 = s16[464,448]{0,1:T(8,128)(2,1)S(1)} collective-permute-done((s16[464,448]{0,1:T(8,128)(2,1)S(1)}, s16[464,448]{0,1:T(8,128)(2,1)S(1)}, u32[]{:S(2)}, u32[]{:S(2)}) %collective-permute-start.29) | collective-permute-done | bytes 415776 | tf_op jit(solution)/shard_map/ppermute | solution.py:28
  179.9 9.7 %collective-permute-done.28 = s16[464,448]{0,1:T(8,128)(2,1)S(1)} collective-permute-done((s16[464,448]{0,1:T(8,128)(2,1)S(1)}, s16[464,448]{0,1:T(8,128)(2,1)S(1)}, u32[]{:S(2)}, u32[]{:S(2)}) %collective-permute-start.28) | collective-permute-done | bytes 415776 | tf_op jit(solution)/shard_map/ppermute | solution.py:28
  190.3 1.7 fusion
  (127 shorter events, 35.0 us)
Async XLA Ops:
  0.0 20.2 %collective-permute-start.12 = (bf16[448,896]{1,0:T(8,128)(2,1)}, bf16[448,896]{1,0:T(8,128)(2,1)S(1)}, u32[]{:S(2)}, u32[]{:S(2)}) collective-permute-start(bf16[448,896]{1,0:T(8,128)(2,1)} %refs_10_.1), channel_id=1, source_target_pairs={{0,16},{1,17},{2,18},{3,19},{4,20},{5,21},{6,22},{7,23},{8,24},{9,... | collective-permute-start | bytes 2408456 | tf_op jit(solution)/shard_map/ppermute | solution.py:28
  1.2 19.4 %collective-permute-start.10 = (bf16[448,896]{1,0:T(8,128)(2,1)}, bf16[448,896]{1,0:T(8,128)(2,1)S(1)}, u32[]{:S(2)}, u32[]{:S(2)}) collective-permute-start(bf16[448,896]{1,0:T(8,128)(2,1)} %refs_10_.1), channel_id=1, source_target_pairs={{0,48},{1,49},{2,50},{3,51},{4,52},{5,53},{6,54},{7,55},{8,56},{9,... | collective-permute-start | bytes 2408456 | tf_op jit(solution)/shard_map/ppermute | solution.py:28
  2.7 19.9 %collective-permute-start.1 = (bf16[448,896]{1,0:T(8,128)(2,1)}, bf16[448,896]{1,0:T(8,128)(2,1)S(1)}, u32[]{:S(2)}, u32[]{:S(2)}) collective-permute-start(bf16[448,896]{1,0:T(8,128)(2,1)} %refs_0_.1), channel_id=1, source_target_pairs={{0,2},{1,3},{2,4},{3,5},{4,6},{5,7},{6,0},{7,1},{8,10},{9,11},{10,... | collective-permute-start | bytes 2408456 | tf_op jit(solution)/shard_map/ppermute | solution.py:28
  2.7 20.5 %collective-permute-start.18 = (bf16[448,896]{1,0:T(8,128)(2,1)}, bf16[448,896]{1,0:T(8,128)(2,1)S(1)}, u32[]{:S(2)}, u32[]{:S(2)}) collective-permute-start(bf16[448,896]{1,0:T(8,128)(2,1)} %refs_10_.1), channel_id=1, source_target_pairs={{0,64},{1,65},{2,66},{3,67},{4,68},{5,69},{6,70},{7,71},{8,72},{9,... | collective-permute-start | bytes 2408456 | tf_op jit(solution)/shard_map/ppermute | solution.py:28
  2.8 34.3 %collective-permute-start.4 = (bf16[448,896]{1,0:T(8,128)(2,1)}, bf16[448,896]{1,0:T(8,128)(2,1)S(1)}, u32[]{:S(2)}, u32[]{:S(2)}) collective-permute-start(bf16[448,896]{1,0:T(8,128)(2,1)} %refs_0_.1), channel_id=1, source_target_pairs={{0,1},{1,0},{2,3},{3,2},{4,5},{5,4},{6,7},{7,6},{8,9},{9,8},{10,11... | collective-permute-start | bytes 2408456 | tf_op jit(solution)/shard_map/ppermute | solution.py:28
  20.2 19.3 %collective-permute-start = (bf16[448,896]{1,0:T(8,128)(2,1)}, bf16[448,896]{1,0:T(8,128)(2,1)S(1)}, u32[]{:S(2)}, u32[]{:S(2)}) collective-permute-start(bf16[448,896]{1,0:T(8,128)(2,1)} %refs_0_.1), channel_id=1, source_target_pairs={{0,6},{1,7},{2,0},{3,1},{4,2},{5,3},{6,4},{7,5},{8,14},{9,15},{10,... | collective-permute-start | bytes 2408456 | tf_op jit(solution)/shard_map/ppermute | solution.py:28
  20.6 18.8 %collective-permute-start.9 = (bf16[448,896]{1,0:T(8,128)(2,1)}, bf16[448,896]{1,0:T(8,128)(2,1)S(1)}, u32[]{:S(2)}, u32[]{:S(2)}) collective-permute-start(bf16[448,896]{1,0:T(8,128)(2,1)} %refs_10_.1), channel_id=1, source_target_pairs={{0,8},{1,9},{2,10},{3,11},{4,12},{5,13},{6,14},{7,15},{8,0},{9,1},... | collective-permute-start | bytes 2408456 | tf_op jit(solution)/shard_map/ppermute | solution.py:28
  22.6 20.5 %collective-permute-start.13 = (bf16[224,896]{1,0:T(8,128)(2,1)S(1)}, bf16[224,896]{1,0:T(8,128)(2,1)S(1)}, u32[]{:S(2)}, u32[]{:S(2)}) collective-permute-start(bf16[224,896]{1,0:T(8,128)(2,1)S(1)} %slice.60), channel_id=1, source_target_pairs={{0,16},{1,17},{2,18},{3,19},{4,20},{5,21},{6,22},{7,23},{8,24},{9,... | collective-permute-start | bytes 1204232 | tf_op jit(solution)/shard_map/ppermute | solution.py:28
  23.2 63.7 %copy-start.6 = (bf16[448,896]{1,0:T(8,128)(2,1)}, bf16[448,896]{1,0:T(8,128)(2,1)S(1)}, u32[]{:S(2)}) copy-start(bf16[448,896]{1,0:T(8,128)(2,1)S(1)} %collective-permute-done.18.refs_20_) | copy-start | bytes 2408452
  23.2 20.0 %collective-permute-start.14 = (bf16[224,896]{1,0:T(8,128)(2,1)S(1)}, bf16[224,896]{1,0:T(8,128)(2,1)S(1)}, u32[]{:S(2)}, u32[]{:S(2)}) collective-permute-start(bf16[224,896]{1,0:T(8,128)(2,1)S(1)} %slice.61), channel_id=1, source_target_pairs={{0,48},{1,49},{2,50},{3,51},{4,52},{5,53},{6,54},{7,55},{8,56},{9,... | collective-permute-start | bytes 1204232 | tf_op jit(solution)/shard_map/ppermute | solution.py:28
  37.2 8.7 %collective-permute-start.2 = (bf16[224,896]{1,0:T(8,128)(2,1)S(1)}, bf16[224,896]{1,0:T(8,128)(2,1)S(1)}, u32[]{:S(2)}, u32[]{:S(2)}) collective-permute-start(bf16[224,896]{1,0:T(8,128)(2,1)S(1)} %slice.56), channel_id=1, source_target_pairs={{0,2},{1,3},{2,4},{3,5},{4,6},{5,7},{6,0},{7,1},{8,10},{9,11},{10,... | collective-permute-start | bytes 1204232 | tf_op jit(solution)/shard_map/ppermute | solution.py:28
  39.4 34.7 %collective-permute-start.22 = (bf16[448,896]{1,0:T(8,128)(2,1)S(1)}, bf16[448,896]{1,0:T(8,128)(2,1)}, u32[]{:S(2)}, u32[]{:S(2)}) collective-permute-start(bf16[448,896]{1,0:T(8,128)(2,1)S(1)} %collective-permute-done.18.refs_20_), channel_id=1, source_target_pairs={{0,16},{1,17},{2,18},{3,19},{4,20},{5,21},{6,22},{7,23},{8,24},{9,... | collective-permute-start | bytes 2408456 | tf_op jit(solution)/shard_map/ppermute | solution.py:28
  40.4 33.8 %collective-permute-start.20 = (bf16[448,896]{1,0:T(8,128)(2,1)S(1)}, bf16[448,896]{1,0:T(8,128)(2,1)}, u32[]{:S(2)}, u32[]{:S(2)}) collective-permute-start(bf16[448,896]{1,0:T(8,128)(2,1)S(1)} %collective-permute-done.18.refs_20_), channel_id=1, source_target_pairs={{0,48},{1,49},{2,50},{3,51},{4,52},{5,53},{6,54},{7,55},{8,56},{9,... | collective-permute-start | bytes 2408456 | tf_op jit(solution)/shard_map/ppermute | solution.py:28
  43.1 58.5 %copy-start.33 = (f32[1000]{0:T(1024)S(1)}, f32[1000]{0:T(1024)}, u32[]{:S(2)}) copy-start(f32[1000]{0:T(1024)} %param.9) | copy-start | bytes 12004
  43.1 31.6 %collective-permute-start.6 = (bf16[448,896]{1,0:T(8,128)(2,1)S(1)}, bf16[448,896]{1,0:T(8,128)(2,1)S(1)}, u32[]{:S(2)}, u32[]{:S(2)}) collective-permute-start(bf16[448,896]{1,0:T(8,128)(2,1)S(1)} %collective-permute-done.4.refs_5_), channel_id=1, source_target_pairs={{0,2},{1,3},{2,4},{3,5},{4,6},{5,7},{6,0},{7,1},{8,10},{9,11},{10,... | collective-permute-start | bytes 2408456 | tf_op jit(solution)/shard_map/ppermute | solution.py:28
  43.2 32.4 %collective-permute-start.5 = (bf16[448,896]{1,0:T(8,128)(2,1)S(1)}, bf16[448,896]{1,0:T(8,128)(2,1)S(1)}, u32[]{:S(2)}, u32[]{:S(2)}) collective-permute-start(bf16[448,896]{1,0:T(8,128)(2,1)S(1)} %collective-permute-done.4.refs_5_), channel_id=1, source_target_pairs={{0,6},{1,7},{2,0},{3,1},{4,2},{5,3},{6,4},{7,5},{8,14},{9,15},{10,... | collective-permute-start | bytes 2408456 | tf_op jit(solution)/shard_map/ppermute | solution.py:28
  46.6 22.5 %collective-permute-start.3 = (bf16[224,896]{1,0:T(8,128)(2,1)S(1)}, bf16[224,896]{1,0:T(8,128)(2,1)S(1)}, u32[]{:S(2)}, u32[]{:S(2)}) collective-permute-start(bf16[224,896]{1,0:T(8,128)(2,1)S(1)} %slice.57), channel_id=1, source_target_pairs={{0,6},{1,7},{2,0},{3,1},{4,2},{5,3},{6,4},{7,5},{8,14},{9,15},{10,... | collective-permute-start | bytes 1204232 | tf_op jit(solution)/shard_map/ppermute | solution.py:28
  69.9 13.3 %collective-permute-start.19 = (bf16[448,896]{1,0:T(8,128)(2,1)S(1)}, bf16[448,896]{1,0:T(8,128)(2,1)S(1)}, u32[]{:S(2)}, u32[]{:S(2)}) collective-permute-start(bf16[448,896]{1,0:T(8,128)(2,1)S(1)} %collective-permute-done.18.refs_20_), channel_id=1, source_target_pairs={{0,8},{1,9},{2,10},{3,11},{4,12},{5,13},{6,14},{7,15},{8,0},{9,1},... | collective-permute-start | bytes 2408456 | tf_op jit(solution)/shard_map/ppermute | solution.py:28
  74.1 9.9 %collective-permute-start.11 = (bf16[448,896]{1,0:T(8,128)(2,1)S(1)}, bf16[448,896]{1,0:T(8,128)(2,1)S(1)}, u32[]{:S(2)}, u32[]{:S(2)}) collective-permute-start(bf16[448,896]{1,0:T(8,128)(2,1)S(1)} %collective-permute-done.10.refs_12_), channel_id=1, source_target_pairs={{0,8},{1,9},{2,10},{3,11},{4,12},{5,13},{6,14},{7,15},{8,0},{9,1},... | collective-permute-start | bytes 2408456 | tf_op jit(solution)/shard_map/ppermute | solution.py:28
  74.1 11.0 %collective-permute-start.17 = (bf16[448,896]{1,0:T(8,128)(2,1)S(1)}, bf16[448,896]{1,0:T(8,128)(2,1)S(1)}, u32[]{:S(2)}, u32[]{:S(2)}) collective-permute-start(bf16[448,896]{1,0:T(8,128)(2,1)S(1)} %collective-permute-done.12.refs_18_), channel_id=1, source_target_pairs={{0,8},{1,9},{2,10},{3,11},{4,12},{5,13},{6,14},{7,15},{8,0},{9,1},... | collective-permute-start | bytes 2408456 | tf_op jit(solution)/shard_map/ppermute | solution.py:28
  74.6 4.3 %collective-permute-start.15 = (bf16[224,896]{1,0:T(8,128)(2,1)S(1)}, bf16[224,896]{1,0:T(8,128)(2,1)S(1)}, u32[]{:S(2)}, u32[]{:S(2)}) collective-permute-start(bf16[224,896]{1,0:T(8,128)(2,1)S(1)} %collective-permute-done.13.refs_14_), channel_id=1, source_target_pairs={{0,8},{1,9},{2,10},{3,11},{4,12},{5,13},{6,14},{7,15},{8,0},{9,1},... | collective-permute-start | bytes 1204232 | tf_op jit(solution)/shard_map/ppermute | solution.py:28
  75.6 4.1 %collective-permute-start.16 = (bf16[224,896]{1,0:T(8,128)(2,1)S(1)}, bf16[224,896]{1,0:T(8,128)(2,1)S(1)}, u32[]{:S(2)}, u32[]{:S(2)}) collective-permute-start(bf16[224,896]{1,0:T(8,128)(2,1)S(1)} %collective-permute-done.14.refs_15_), channel_id=1, source_target_pairs={{0,8},{1,9},{2,10},{3,11},{4,12},{5,13},{6,14},{7,15},{8,0},{9,1},... | collective-permute-start | bytes 1204232 | tf_op jit(solution)/shard_map/ppermute | solution.py:28
  79.7 11.8 %collective-permute-start.23 = (bf16[224,896]{1,0:T(8,128)(2,1)S(1)}, bf16[224,896]{1,0:T(8,128)(2,1)}, u32[]{:S(2)}, u32[]{:S(2)}) collective-permute-start(bf16[224,896]{1,0:T(8,128)(2,1)S(1)} %slice.62), channel_id=1, source_target_pairs={{0,16},{1,17},{2,18},{3,19},{4,20},{5,21},{6,22},{7,23},{8,24},{9,... | collective-permute-start | bytes 1204232 | tf_op jit(solution)/shard_map/ppermute | solution.py:28
  80.4 11.2 %collective-permute-start.24 = (bf16[224,896]{1,0:T(8,128)(2,1)S(1)}, bf16[224,896]{1,0:T(8,128)(2,1)}, u32[]{:S(2)}, u32[]{:S(2)}) collective-permute-start(bf16[224,896]{1,0:T(8,128)(2,1)S(1)} %slice.63), channel_id=1, source_target_pairs={{0,48},{1,49},{2,50},{3,51},{4,52},{5,53},{6,54},{7,55},{8,56},{9,... | collective-permute-start | bytes 1204232 | tf_op jit(solution)/shard_map/ppermute | solution.py:28
  83.1 19.5 %collective-permute-start.21 = (bf16[448,896]{1,0:T(8,128)(2,1)}, bf16[448,896]{1,0:T(8,128)(2,1)}, u32[]{:S(2)}, u32[]{:S(2)}) collective-permute-start(bf16[448,896]{1,0:T(8,128)(2,1)} %collective-permute-done.20.refs_22_), channel_id=1, source_target_pairs={{0,8},{1,9},{2,10},{3,11},{4,12},{5,13},{6,14},{7,15},{8,0},{9,1},... | collective-permute-start | bytes 2408456 | tf_op jit(solution)/shard_map/ppermute | solution.py:28
  85.0 17.6 %collective-permute-start.27 = (bf16[448,896]{1,0:T(8,128)(2,1)}, bf16[448,896]{1,0:T(8,128)(2,1)}, u32[]{:S(2)}, u32[]{:S(2)}) collective-permute-start(bf16[448,896]{1,0:T(8,128)(2,1)} %collective-permute-done.22.refs_28_), channel_id=1, source_target_pairs={{0,8},{1,9},{2,10},{3,11},{4,12},{5,13},{6,14},{7,15},{8,0},{9,1},... | collective-permute-start | bytes 2408456 | tf_op jit(solution)/shard_map/ppermute | solution.py:28
  86.1 10.4 %collective-permute-start.7 = (bf16[224,896]{1,0:T(8,128)(2,1)S(1)}, bf16[224,896]{1,0:T(8,128)(2,1)S(1)}, u32[]{:S(2)}, u32[]{:S(2)}) collective-permute-start(bf16[224,896]{1,0:T(8,128)(2,1)S(1)} %slice.58), channel_id=1, source_target_pairs={{0,2},{1,3},{2,4},{3,5},{4,6},{5,7},{6,0},{7,1},{8,10},{9,11},{10,... | collective-permute-start | bytes 1204232 | tf_op jit(solution)/shard_map/ppermute | solution.py:28
  91.5 11.1 %collective-permute-start.8 = (bf16[224,896]{1,0:T(8,128)(2,1)}, bf16[224,896]{1,0:T(8,128)(2,1)}, u32[]{:S(2)}, u32[]{:S(2)}) collective-permute-start(bf16[224,896]{1,0:T(8,128)(2,1)} %slice.59), channel_id=1, source_target_pairs={{0,6},{1,7},{2,0},{3,1},{4,2},{5,3},{6,4},{7,5},{8,14},{9,15},{10,... | collective-permute-start | bytes 1204232 | tf_op jit(solution)/shard_map/ppermute | solution.py:28
  91.7 10.9 %collective-permute-start.25 = (bf16[224,896]{1,0:T(8,128)(2,1)}, bf16[224,896]{1,0:T(8,128)(2,1)}, u32[]{:S(2)}, u32[]{:S(2)}) collective-permute-start(bf16[224,896]{1,0:T(8,128)(2,1)} %collective-permute-done.23.refs_24_), channel_id=1, source_target_pairs={{0,8},{1,9},{2,10},{3,11},{4,12},{5,13},{6,14},{7,15},{8,0},{9,1},... | collective-permute-start | bytes 1204232 | tf_op jit(solution)/shard_map/ppermute | solution.py:28
  97.2 5.4 %collective-permute-start.26 = (bf16[224,896]{1,0:T(8,128)(2,1)}, bf16[224,896]{1,0:T(8,128)(2,1)}, u32[]{:S(2)}, u32[]{:S(2)}) collective-permute-start(bf16[224,896]{1,0:T(8,128)(2,1)} %collective-permute-done.24.refs_25_), channel_id=1, source_target_pairs={{0,8},{1,9},{2,10},{3,11},{4,12},{5,13},{6,14},{7,15},{8,0},{9,1},... | collective-permute-start | bytes 1204232 | tf_op jit(solution)/shard_map/ppermute | solution.py:28
  139.8 39.8 %collective-permute-start.29 = (s16[464,448]{0,1:T(8,128)(2,1)S(1)}, s16[464,448]{0,1:T(8,128)(2,1)S(1)}, u32[]{:S(2)}, u32[]{:S(2)}) collective-permute-start(s16[464,448]{0,1:T(8,128)(2,1)S(1)} %get-tuple-element.6), channel_id=1, source_target_pairs={{0,8},{1,24},{2,40},{3,56},{4,72},{5,88},{6,104},{7,120},{8,0},{9,... | collective-permute-start | bytes 1247240 | tf_op jit(solution)/shard_map/ppermute | solution.py:28
  142.0 47.6 %collective-permute-start.28 = (s16[464,448]{0,1:T(8,128)(2,1)S(1)}, s16[464,448]{0,1:T(8,128)(2,1)S(1)}, u32[]{:S(2)}, u32[]{:S(2)}) collective-permute-start(s16[464,448]{0,1:T(8,128)(2,1)S(1)} %get-tuple-element.5), channel_id=1, source_target_pairs={{0,0},{1,16},{2,32},{3,48},{4,64},{5,80},{6,96},{7,112},{8,8},{9,2... | collective-permute-start | bytes 1247240 | tf_op jit(solution)/shard_map/ppermute | solution.py:28
  (33 other events, 110.2 us)

commit v2 on v0

v2 whole, which is shorter than its diff:
```python
import jax
import jax.numpy as jnp
from jax import lax
from jax.experimental import pallas as pl
from jax.experimental.pallas import tpu as pltpu
from jax.sharding import PartitionSpec as P

Z_LO, X, CORE, Y, Z_HI = 2, 4, 2, 4, 2
AXES = ("row", "col")
LEVELS = 15


def device_index(z_lo, x, core, y, z_hi):
    return ((z_lo * X + x) * CORE + core) * (Y * Z_HI) + y * Z_HI + z_hi


def places():
    for z_lo in range(Z_LO):
        for x in range(X):
            for core in range(CORE):
                for y in range(Y):
                    for z_hi in range(Z_HI):
                        yield z_lo, x, core, y, z_hi


def send(block, target):
    pairs = [(device_index(*place), device_index(*target(*place))) for place in places()]
    return lax.ppermute(block, AXES, pairs)


def along_y(step):
    return lambda z_lo, x, core, y, z_hi: (z_lo, x, core, (y + step) % Y, z_hi)


def across_z_hi(z_lo, x, core, y, z_hi):
    return z_lo, x, core, y, 1 - z_hi


def mirrored(flip):
    def target(z_lo, x, core, y, z_hi):
        chip_row, chip_col = z_lo * X + x, y * Z_HI + z_hi
        return chip_col // X, chip_col % X, core ^ flip, chip_row // Z_HI, chip_row % Z_HI

    return target


def ring(block, along):
    half = block.shape[0] // 2
    before = send(block, along(1))
    after = send(block, along(-1))
    top = send(before[:half], along(1))
    bottom = send(after[half:], along(-1))
    return [(block,), (after,), (top, bottom), (before,)]


def gather(block, along, across):
    return ring(block, along) + ring(send(block, across), along)


def lookup(energies, orbital_index):
    labels = jnp.arange(energies.shape[0], dtype=jnp.int32)
    picked = jnp.where(orbital_index[:, None] == labels[None, :], energies[None, :], 0.0)
    return jnp.sum(picked, axis=1)


def product_kernel(counts, first, *refs):
    parts, refs = refs[:sum(counts)], refs[sum(counts):]
    panel_ref, out_ref, same_ref, cross_ref, left, right, acc, sem_a, sem_b = refs
    row, col = lax.axis_index("row"), lax.axis_index("col")
    core, y, z_hi = row % CORE, col // Z_HI, col % Z_HI
    rows, depth = left.shape[1], left.shape[2]
    copies = []
    at = 0
    for slot, count in enumerate(counts):
        part = 2 * rows // count
        mine = []
        for i in range(count):
            low, high = max(i * part, first), min((i + 1) * part, first + rows)
            if low < high:
                mine.append(pltpu.make_async_copy(
                    parts[at].at[pl.ds(low - i * part, high - low), :],
                    left.at[slot, pl.ds(low - first, high - low), :], sem_a.at[at]))
            at += 1
        block = lax.rem(y + slot % Y, Y) * Z_HI + (z_hi if slot < Y else 1 - z_hi)
        mine.append(pltpu.make_async_copy(
            panel_ref.at[pl.ds(pl.multiple_of(block * depth, depth), depth), :],
            right.at[slot], sem_b.at[slot]))
        copies.append(mine)
    for mine in copies:
        for copy in mine:
            copy.start()
    for slot, mine in enumerate(copies):
        for copy in mine:
            copy.wait()
        term = jnp.dot(left[slot], right[slot], preferred_element_type=jnp.float32)
        if slot == 0:
            acc[...] = term
        elif slot < len(copies) - 1:
            acc[...] += term
        else:
            out_ref[...] = acc[...] + term
    half = out_ref.shape[1] // 2
    low, high = out_ref[:, :half], out_ref[:, half:]
    encode(jnp.where(core == 0, low, high), same_ref)
    encode(jnp.where(core == 0, high, low), cross_ref)


def encode(block, payload_ref):
    part = block.shape[0] // 2
    packed = jnp.concatenate([block[:part], block[part:]], axis=1)
    top = jnp.maximum(jnp.max(jnp.abs(packed), axis=0, keepdims=True), 1e-30)
    power = jnp.ceil(jnp.log2(top) + 1e-3)
    payload_ref[:part, :] = jnp.round(packed * jnp.exp2(LEVELS - power)).astype(jnp.int32).astype(jnp.int16)
    payload_ref[part:, :] = jnp.broadcast_to(power, (16, packed.shape[1])).astype(jnp.int32).astype(jnp.int16)


def decode(payload_ref):
    part = payload_ref.shape[0] - 16
    power = payload_ref[part:, :].astype(jnp.int32).astype(jnp.float32)[:1]
    packed = payload_ref[:part, :].astype(jnp.int32).astype(jnp.float32) * jnp.exp2(power - LEVELS)
    width = packed.shape[1] // 2
    return jnp.concatenate([packed[:, :width], packed[:, width:]])


def combine_kernel(*refs):
    *inputs, row_gap_ref, col_gap_ref, out_ref = refs
    count = len(inputs) // 3
    products, same, cross = inputs[:count], inputs[count:2 * count], inputs[2 * count:]
    core = lax.axis_index("row") % CORE
    same = jnp.concatenate([decode(p) for p in same]).T
    cross = jnp.concatenate([decode(p) for p in cross]).T
    mirror = jnp.concatenate(
        [jnp.where(core == 0, same, cross), jnp.where(core == 0, cross, same)], axis=1)
    at = 0
    for product in products:
        part = product.shape[0]
        gap = row_gap_ref[at:at + part, :] + col_gap_ref[...]
        out_ref[at:at + part, :] = (product[...] + mirror[at:at + part]) / gap
        at += part


def combine(products, same, cross, row_gap, col_gap):
    rows, cols = row_gap.shape[0], col_gap.shape[0]
    inputs = [*products, *same, *cross, row_gap[:, None], col_gap[None, :]]
    return pl.pallas_call(
        combine_kernel,
        out_shape=jax.ShapeDtypeStruct((rows, cols), jnp.float32),
        in_specs=[pl.BlockSpec(memory_space=pltpu.VMEM)] * len(inputs),
        out_specs=pl.BlockSpec(memory_space=pltpu.VMEM),
        compiler_params=pltpu.CompilerParams(vmem_limit_bytes=32 * 2**20),
        cost_estimate=pl.CostEstimate(flops=4 * rows * cols, bytes_accessed=12 * rows * cols, transcendentals=0),
        name="combine",
    )(*inputs)


def local_product(groups, panel, first, rows):
    counts = [len(g) for g in groups]
    parts = [p for g in groups for p in g]
    slots, depth, cols = len(groups), groups[0][0].shape[1], panel.shape[1]
    payload = jax.ShapeDtypeStruct((rows // 2 + 16, cols), jnp.int16)
    hbm = pl.BlockSpec(memory_space=pltpu.HBM)
    vmem = pl.BlockSpec(memory_space=pltpu.VMEM)
    return pl.pallas_call(
        lambda *refs: product_kernel(counts, first, *refs),
        out_shape=[jax.ShapeDtypeStruct((rows, cols), jnp.float32), payload, payload],
        in_specs=[hbm] * (len(parts) + 1),
        out_specs=[vmem] * 3,
        scratch_shapes=[
            pltpu.VMEM((slots, rows, depth), jnp.bfloat16),
            pltpu.VMEM((slots, depth, cols), jnp.bfloat16),
            pltpu.VMEM((rows, cols), jnp.float32),
            pltpu.SemaphoreType.DMA((len(parts),)),
            pltpu.SemaphoreType.DMA((slots,)),
        ],
        compiler_params=pltpu.CompilerParams(vmem_limit_bytes=60 * 2**20),
        cost_estimate=pl.CostEstimate(
            flops=2 * rows * cols * depth * slots, bytes_accessed=16 * 2**20, transcendentals=0),
        name="local_product",
    )(*parts, panel)


def shards(amplitudes, integrals, occ_energy, vir_energy, pair_occ, pair_vir):
    tile_rows, tile_cols = amplitudes.shape
    panel = lax.all_gather(integrals, "row", axis=0, tiled=True)
    groups = gather(amplitudes, along_y, across_z_hi)
    part = tile_rows // 2
    products, same, cross = [], [], []
    for first in (0, part):
        product, to_same, to_cross = local_product(groups, panel, first, part)
        products.append(product)
        same.append(send(to_same, mirrored(0)))
        cross.append(send(to_cross, mirrored(1)))
    row_start = lax.axis_index("row") * tile_rows
    col_start = lax.axis_index("col") * tile_cols
    row_occ = lax.dynamic_slice_in_dim(pair_occ, row_start, tile_rows)
    row_vir = lax.dynamic_slice_in_dim(pair_vir, row_start, tile_rows)
    col_occ = lax.dynamic_slice_in_dim(pair_occ, col_start, tile_cols)
    col_vir = lax.dynamic_slice_in_dim(pair_vir, col_start, tile_cols)
    row_gap = lookup(occ_energy, row_occ) - lookup(vir_energy, row_vir)
    col_gap = lookup(occ_energy, col_occ) - lookup(vir_energy, col_vir)
    return combine(products, same, cross, row_gap, col_gap)


def solution(mesh):
    return jax.shard_map(
        shards,
        mesh=mesh,
        in_specs=(P("row", "col"), P("row", "col"), P(), P(), P(), P()),
        out_specs=P("row", "col"),
        check_vma=False,
    )
```

time: 324 us -> 161 us (0.50)
  waiting for transfers between devices: 279 us -> 92.6 us
  starting transfers between devices: 0.04 us -> 24.8 us
  matrix products: 21.5 us -> 0 us
  Pallas kernels: 0 us -> 18.1 us
  local copies, waits for them, and re-layouts: 3.1 us -> 8.63 us
  other arithmetic: 5.01 us -> 1.04 us
    all_gather x2 -> x1, waiting for transfers between devices: 278 us -> 19.3 us  [shards(): panel = lax.all_gather(integrals, 'row', axis=0, tiled=True)]
    ppermute x0 -> x13, waiting for transfers between devices: none -> 72.5 us  [send(): return lax.ppermute(block, AXES, pairs)]
    ppermute x0 -> x13, starting transfers between devices: none -> 24.8 us  [send(): return lax.ppermute(block, AXES, pairs)]
    dot_general x1 -> x0, matrix products: 21.5 us -> none  [shards(): jnp.einsum('lrk,lkc->rc', row_panels, lax.all_gather(right_local, 'row',...]
    pallas_call x0 -> x3, Pallas kernels: none -> 18.1 us  [the longest x2 15.5 us: local_product(): pl.pallas_call(lambda *refs: product_kernel(counts, first, *refs), out_sh...]
    another operation x1 -> x0, other arithmetic: 3.98 us -> none  [shards(): right_local = jnp.stack((integrals, amplitudes))]
    slice x0 -> x4, local copies, waits for them, and re-layouts: none -> 3.33 us  [the longest x2 1.68 us: ring(): top = send(before[:half], along(1))]
  transfers between devices with their start and end apart: 2 -> 14, of which waited for: 2 -> 11; matrix products, arithmetic and copies ran while one was open for 1% -> 5% of each run, Pallas kernels for 0% -> 5%
where the time goes in v2:
time: 161 us; the launch traced here: 159 us
  waiting for transfers between devices  92.6 us (58%)
  starting transfers between devices  24.8 us (15%)
  Pallas kernels  18.1 us (11%)
  between operations  13.5 us (8%)
  local copies, waits for them, and re-layouts  8.63 us (5%)
    ppermute x13, waiting for transfers between devices, send(): return lax.ppermute(block, AXES, pairs)  72.5 us
    ppermute x13, starting transfers between devices, send(): return lax.ppermute(block, AXES, pairs)  24.8 us
    all_gather x1, waiting for transfers between devices, shards(): panel = lax.all_gather(integrals, 'row', axis=0, tiled=True)  19.3 us
    pallas_call x2, Pallas kernels, local_product(): pl.pallas_call(lambda *refs: product_kernel(counts, first, *refs), out_sh...  15.5 us
  transfers between devices with their start and end apart: 14, of which 11 were waited for; matrix products, arithmetic and copies ran while one was open for 5% of the time, Pallas kernels for 5%

profile of v2, /device:TPU:16, one launch (start us, length us, event | category | flops | bytes accessed | tf_op | source)
XLA Modules:
  0.0 158.6 jit_solution(16034657516613049342)
XLA Ops:
  7.3 4.0 %collective-permute-start.4 = (bf16[448,896]{1,0:T(8,128)(2,1)}, bf16[448,896]{1,0:T(8,128)(2,1)S(1)}, u32[]{:S(2)}, u32[]{:S(2)}) collective-permute-start(bf16[448,896]{1,0:T(8,128)(2,1)} %refs_0_.3), channel_id=1, source_target_pairs={{0,1},{1,0},{2,3},{3,2},{4,5},{5,4},{6,7},{7,6},{8,9},{9,8},{10,11... | collective-permute-start | bytes 2408456 | tf_op jit(solution)/shard_map/ppermute | solution.py:28
  11.2 1.3 collective-permute-start.1
  13.2 24.6 %collective-permute-done.4.refs_5_ = bf16[448,896]{1,0:T(8,128)(2,1)S(1)} collective-permute-done((bf16[448,896]{1,0:T(8,128)(2,1)}, bf16[448,896]{1,0:T(8,128)(2,1)S(1)}, u32[]{:S(2)}, u32[]{:S(2)}) %collective-permute-start.4) | collective-permute-done | bytes 802848 | tf_op jit(solution)/shard_map/ppermute | solution.py:28
  37.9 1.4 collective-permute-start.6
  39.9 0.8 slice.16
  40.7 1.4 collective-permute-start.2
  42.1 0.9 slice.17
  43.6 15.1 %collective-permute-done.6.refs_9_ = bf16[448,896]{1,0:T(8,128)(2,1)S(1)} collective-permute-done((bf16[448,896]{1,0:T(8,128)(2,1)S(1)}, bf16[448,896]{1,0:T(8,128)(2,1)S(1)}, u32[]{:S(2)}, u32[]{:S(2)}) %collective-permute-start.6) | collective-permute-done | bytes 802848 | tf_op jit(solution)/shard_map/ppermute | solution.py:28
  58.7 0.8 slice.18
  59.5 1.4 collective-permute-start.7
  60.9 0.9 copy-done.5
  61.8 0.8 slice.19
  63.2 0.8 dynamic_slice.13
  64.0 0.8 dynamic_slice.12
  66.0 1.2 collective-permute-done.2.refs_2_
  67.2 1.1 collective-permute-done.3.refs_3_
  68.3 3.3 %collective-permute-done.7.refs_7_ = bf16[224,896]{1,0:T(8,128)(2,1)} collective-permute-done((bf16[224,896]{1,0:T(8,128)(2,1)}, bf16[224,896]{1,0:T(8,128)(2,1)}, u32[]{:S(2)}, u32[]{:S(2)}) %collective-permute-start.7) | collective-permute-done | bytes 401440 | tf_op jit(solution)/shard_map/ppermute | solution.py:28
  71.6 1.1 collective-permute-done.8.refs_8_
  72.7 19.3 %all-gather.2.cloned.1.call-done.refs_10_ = bf16[7168,896]{1,0:T(8,128)(2,1)} async-done(((bf16[448,896]{1,0:T(8,128)(2,1)}), bf16[7168,896]{1,0:T(8,128)(2,1)}) %all-gather.2.cloned.1.call-update) | async-done | bytes 12845072 | tf_op jit(solution)/shard_map/all_gather | solution.py:184
  92.1 7.8 %local_product.3 = (f32[224,896]{1,0:T(8,128)}, s16[128,896]{1,0:T(8,128)(2,1)}, s16[128,896]{1,0:T(8,128)(2,1)}) custom-call(bf16[448,896]{1,0:T(8,128)(2,1)} %refs_0_.3, bf16[448,896]{1,0:T(8,128)(2,1)} %copy-done.3, bf16[224,896]{1,0:T(8,128)(2,1)} %copy-done.7, bf16[224,896]{1,0:T(8,128)(2,1)} %copy-done.8, bf16[448,896]{1,0:T(8,128)(2,1)} %copy-done.2, ...), custom_call_target="tpu_custom_call" | custom-call | flops 2877292544 | bytes 16777216 | tf_op jit(solution)/shard_map/local_product/pallas_call | solution.py:163
  99.9 2.6 %collective-permute-start.10 = (s16[128,896]{1,0:T(8,128)(2,1)}, s16[128,896]{1,0:T(8,128)(2,1)S(1)}, u32[]{:S(2)}, u32[]{:S(2)}) collective-permute-start(s16[128,896]{1,0:T(8,128)(2,1)} %get-tuple-element.14), channel_id=1, source_target_pairs={{0,0},{1,16},{2,32},{3,48},{4,64},{5,80},{6,96},{7,112},{8,8},{9,2... | collective-permute-start | bytes 688136 | tf_op jit(solution)/shard_map/ppermute | solution.py:28
  102.5 3.6 %collective-permute-start.12 = (s16[128,896]{1,0:T(8,128)(2,1)}, s16[128,896]{1,0:T(8,128)(2,1)S(1)}, u32[]{:S(2)}, u32[]{:S(2)}) collective-permute-start(s16[128,896]{1,0:T(8,128)(2,1)} %get-tuple-element.16), channel_id=1, source_target_pairs={{0,8},{1,24},{2,40},{3,56},{4,72},{5,88},{6,104},{7,120},{8,0},{9,... | collective-permute-start | bytes 688136 | tf_op jit(solution)/shard_map/ppermute | solution.py:28
  106.1 7.7 %local_product.2 = (f32[224,896]{1,0:T(8,128)}, s16[128,896]{1,0:T(8,128)(2,1)}, s16[128,896]{1,0:T(8,128)(2,1)}) custom-call(bf16[448,896]{1,0:T(8,128)(2,1)} %refs_0_.3, bf16[448,896]{1,0:T(8,128)(2,1)} %copy-done.3, bf16[224,896]{1,0:T(8,128)(2,1)} %copy-done.7, bf16[224,896]{1,0:T(8,128)(2,1)} %copy-done.8, bf16[448,896]{1,0:T(8,128)(2,1)} %copy-done.2, ...), custom_call_target="tpu_custom_call" | custom-call | flops 2877292544 | bytes 16777216 | tf_op jit(solution)/shard_map/local_product/pallas_call | solution.py:163
  113.8 0.9 collective-permute-start.11
  114.7 5.7 %collective-permute-start.9 = (s16[128,896]{1,0:T(8,128)(2,1)}, s16[128,896]{1,0:T(8,128)(2,1)S(1)}, u32[]{:S(2)}, u32[]{:S(2)}) collective-permute-start(s16[128,896]{1,0:T(8,128)(2,1)} %get-tuple-element.13), channel_id=1, source_target_pairs={{0,0},{1,16},{2,32},{3,48},{4,64},{5,80},{6,96},{7,112},{8,8},{9,2... | collective-permute-start | bytes 688136 | tf_op jit(solution)/shard_map/ppermute | solution.py:28
  120.5 0.8 dynamic_slice.15
  121.9 11.5 %collective-permute-done.10.refs_3_ = s16[128,896]{1,0:T(8,128)(2,1)S(1)} collective-permute-done((s16[128,896]{1,0:T(8,128)(2,1)}, s16[128,896]{1,0:T(8,128)(2,1)S(1)}, u32[]{:S(2)}, u32[]{:S(2)}) %collective-permute-start.10) | collective-permute-done | bytes 229408 | tf_op jit(solution)/shard_map/ppermute | solution.py:28
  133.4 4.8 %collective-permute-done.12.refs_5_ = s16[128,896]{1,0:T(8,128)(2,1)S(1)} collective-permute-done((s16[128,896]{1,0:T(8,128)(2,1)}, s16[128,896]{1,0:T(8,128)(2,1)S(1)}, u32[]{:S(2)}, u32[]{:S(2)}) %collective-permute-start.12) | collective-permute-done | bytes 229408 | tf_op jit(solution)/shard_map/ppermute | solution.py:28
  138.2 4.9 %collective-permute-done.11.refs_4_ = s16[128,896]{1,0:T(8,128)(2,1)S(1)} collective-permute-done((s16[128,896]{1,0:T(8,128)(2,1)}, s16[128,896]{1,0:T(8,128)(2,1)S(1)}, u32[]{:S(2)}, u32[]{:S(2)}) %collective-permute-start.11) | collective-permute-done | bytes 229408 | tf_op jit(solution)/shard_map/ppermute | solution.py:28
  143.1 5.0 %collective-permute-done.9.refs_2_ = s16[128,896]{1,0:T(8,128)(2,1)S(1)} collective-permute-done((s16[128,896]{1,0:T(8,128)(2,1)}, s16[128,896]{1,0:T(8,128)(2,1)S(1)}, u32[]{:S(2)}, u32[]{:S(2)}) %collective-permute-start.9) | collective-permute-done | bytes 229408 | tf_op jit(solution)/shard_map/ppermute | solution.py:28
  148.1 1.1 copy-done.1
  149.2 2.5 %combine.1 = f32[448,896]{1,0:T(8,128)} custom-call(f32[224,896]{1,0:T(8,128)S(1)} %copy-done.1, f32[224,896]{1,0:T(8,128)S(1)} %copy-done, s16[128,896]{1,0:T(8,128)(2,1)S(1)} %collective-permute-done.9.refs_2_, s16[128,896]{1,0:T(8,128)(2,1)S(1)} %collective-permute-done.10.refs_3_, s16[128,896]{1,0:T(8,128)(2,1)S(1)} %collective-permute-done.11.refs_4_, ...), custom_call_target="tpu_custom_call" | custom-call | flops 1605632 | bytes 4816896 | tf_op jit(solution)/shard_map/combine/pallas_call | solution.py:145
  (38 shorter events, 5.4 us)
Async XLA Ops:
  6.5 59.0 %copy-start.10 = (f32[80]{0:T(128)S(1)}, f32[80]{0:T(128)}, u32[]{:S(2)}) copy-start(f32[80]{0:T(128)} %param.8) | copy-start | bytes 964
  6.5 59.1 %copy-start.9 = (f32[1000]{0:T(1024)S(1)}, f32[1000]{0:T(1024)}, u32[]{:S(2)}) copy-start(f32[1000]{0:T(1024)} %param.9) | copy-start | bytes 12004
  6.5 85.5 %all-gather.2.cloned.1.call-start = ((), (), s32[]{:S(2)}) async-start(), calls=%async_computation | async-start | bytes 13647872 | tf_op jit(solution)/shard_map/all_gather | solution.py:184
  7.3 30.6 %collective-permute-start.4 = (bf16[448,896]{1,0:T(8,128)(2,1)}, bf16[448,896]{1,0:T(8,128)(2,1)S(1)}, u32[]{:S(2)}, u32[]{:S(2)}) collective-permute-start(bf16[448,896]{1,0:T(8,128)(2,1)} %refs_0_.3), channel_id=1, source_target_pairs={{0,1},{1,0},{2,3},{3,2},{4,5},{5,4},{6,7},{7,6},{8,9},{9,8},{10,11... | collective-permute-start | bytes 2408456 | tf_op jit(solution)/shard_map/ppermute | solution.py:28
  11.2 28.7 %collective-permute-start.1 = (bf16[448,896]{1,0:T(8,128)(2,1)}, bf16[448,896]{1,0:T(8,128)(2,1)S(1)}, u32[]{:S(2)}, u32[]{:S(2)}) collective-permute-start(bf16[448,896]{1,0:T(8,128)(2,1)} %refs_0_.3), channel_id=1, source_target_pairs={{0,2},{1,3},{2,4},{3,5},{4,6},{5,7},{6,0},{7,1},{8,10},{9,11},{10,... | collective-permute-start | bytes 2408456 | tf_op jit(solution)/shard_map/ppermute | solution.py:28
  12.5 29.6 %collective-permute-start = (bf16[448,896]{1,0:T(8,128)(2,1)}, bf16[448,896]{1,0:T(8,128)(2,1)S(1)}, u32[]{:S(2)}, u32[]{:S(2)}) collective-permute-start(bf16[448,896]{1,0:T(8,128)(2,1)} %refs_0_.3), channel_id=1, source_target_pairs={{0,6},{1,7},{2,0},{3,1},{4,2},{5,3},{6,4},{7,5},{8,14},{9,15},{10,... | collective-permute-start | bytes 2408456 | tf_op jit(solution)/shard_map/ppermute | solution.py:28
  37.9 24.7 %copy-start.6 = (bf16[448,896]{1,0:T(8,128)(2,1)}, bf16[448,896]{1,0:T(8,128)(2,1)S(1)}, u32[]{:S(2)}) copy-start(bf16[448,896]{1,0:T(8,128)(2,1)S(1)} %collective-permute-done.4.refs_5_) | copy-start | bytes 2408452
  37.9 20.8 %collective-permute-start.6 = (bf16[448,896]{1,0:T(8,128)(2,1)S(1)}, bf16[448,896]{1,0:T(8,128)(2,1)S(1)}, u32[]{:S(2)}, u32[]{:S(2)}) collective-permute-start(bf16[448,896]{1,0:T(8,128)(2,1)S(1)} %collective-permute-done.4.refs_5_), channel_id=1, source_target_pairs={{0,2},{1,3},{2,4},{3,5},{4,6},{5,7},{6,0},{7,1},{8,10},{9,11},{10,... | collective-permute-start | bytes 2408456 | tf_op jit(solution)/shard_map/ppermute | solution.py:28
  39.2 21.7 %collective-permute-start.5 = (bf16[448,896]{1,0:T(8,128)(2,1)S(1)}, bf16[448,896]{1,0:T(8,128)(2,1)S(1)}, u32[]{:S(2)}, u32[]{:S(2)}) collective-permute-start(bf16[448,896]{1,0:T(8,128)(2,1)S(1)} %collective-permute-done.4.refs_5_), channel_id=1, source_target_pairs={{0,6},{1,7},{2,0},{3,1},{4,2},{5,3},{6,4},{7,5},{8,14},{9,15},{10,... | collective-permute-start | bytes 2408456 | tf_op jit(solution)/shard_map/ppermute | solution.py:28
  39.9 52.2 %copy-start.2 = (bf16[448,896]{1,0:T(8,128)(2,1)}, bf16[448,896]{1,0:T(8,128)(2,1)S(1)}, u32[]{:S(2)}) copy-start(bf16[448,896]{1,0:T(8,128)(2,1)S(1)} %collective-permute-done.1.refs_4_) | copy-start | bytes 2408452
  40.7 26.5 %collective-permute-start.2 = (bf16[224,896]{1,0:T(8,128)(2,1)}, bf16[224,896]{1,0:T(8,128)(2,1)S(1)}, u32[]{:S(2)}, u32[]{:S(2)}) collective-permute-start(bf16[224,896]{1,0:T(8,128)(2,1)} %slice.16), channel_id=1, source_target_pairs={{0,2},{1,3},{2,4},{3,5},{4,6},{5,7},{6,0},{7,1},{8,10},{9,11},{10,... | collective-permute-start | bytes 1204232 | tf_op jit(solution)/shard_map/ppermute | solution.py:28
  42.1 50.0 %copy-start.3 = (bf16[448,896]{1,0:T(8,128)(2,1)}, bf16[448,896]{1,0:T(8,128)(2,1)S(1)}, u32[]{:S(2)}) copy-start(bf16[448,896]{1,0:T(8,128)(2,1)S(1)} %collective-permute-done.refs_1_) | copy-start | bytes 2408452
  43.0 25.3 %collective-permute-start.3 = (bf16[224,896]{1,0:T(8,128)(2,1)}, bf16[224,896]{1,0:T(8,128)(2,1)S(1)}, u32[]{:S(2)}, u32[]{:S(2)}) collective-permute-start(bf16[224,896]{1,0:T(8,128)(2,1)} %slice.17), channel_id=1, source_target_pairs={{0,6},{1,7},{2,0},{3,1},{4,2},{5,3},{6,4},{7,5},{8,14},{9,15},{10,... | collective-permute-start | bytes 1204232 | tf_op jit(solution)/shard_map/ppermute | solution.py:28
  58.7 33.4 %copy-start.4 = (bf16[448,896]{1,0:T(8,128)(2,1)}, bf16[448,896]{1,0:T(8,128)(2,1)S(1)}, u32[]{:S(2)}) copy-start(bf16[448,896]{1,0:T(8,128)(2,1)S(1)} %collective-permute-done.6.refs_9_) | copy-start | bytes 2408452
  59.5 12.1 %collective-permute-start.7 = (bf16[224,896]{1,0:T(8,128)(2,1)}, bf16[224,896]{1,0:T(8,128)(2,1)}, u32[]{:S(2)}, u32[]{:S(2)}) collective-permute-start(bf16[224,896]{1,0:T(8,128)(2,1)} %slice.18), channel_id=1, source_target_pairs={{0,2},{1,3},{2,4},{3,5},{4,6},{5,7},{6,0},{7,1},{8,10},{9,11},{10,... | collective-permute-start | bytes 1204232 | tf_op jit(solution)/shard_map/ppermute | solution.py:28
  60.9 0.9 copy-start.5
  62.6 10.1 %collective-permute-start.8 = (bf16[224,896]{1,0:T(8,128)(2,1)}, bf16[224,896]{1,0:T(8,128)(2,1)}, u32[]{:S(2)}, u32[]{:S(2)}) collective-permute-start(bf16[224,896]{1,0:T(8,128)(2,1)} %slice.19), channel_id=1, source_target_pairs={{0,6},{1,7},{2,0},{3,1},{4,2},{5,3},{6,4},{7,5},{8,14},{9,15},{10,... | collective-permute-start | bytes 1204232 | tf_op jit(solution)/shard_map/ppermute | solution.py:28
  67.2 24.9 %copy-start.7 = (bf16[224,896]{1,0:T(8,128)(2,1)}, bf16[224,896]{1,0:T(8,128)(2,1)S(1)}, u32[]{:S(2)}) copy-start(bf16[224,896]{1,0:T(8,128)(2,1)S(1)} %collective-permute-done.2.refs_2_) | copy-start | bytes 1204228
  68.3 23.8 %copy-start.8 = (bf16[224,896]{1,0:T(8,128)(2,1)}, bf16[224,896]{1,0:T(8,128)(2,1)S(1)}, u32[]{:S(2)}) copy-start(bf16[224,896]{1,0:T(8,128)(2,1)S(1)} %collective-permute-done.3.refs_3_) | copy-start | bytes 1204228
  99.9 33.5 %collective-permute-start.10 = (s16[128,896]{1,0:T(8,128)(2,1)}, s16[128,896]{1,0:T(8,128)(2,1)S(1)}, u32[]{:S(2)}, u32[]{:S(2)}) collective-permute-start(s16[128,896]{1,0:T(8,128)(2,1)} %get-tuple-element.14), channel_id=1, source_target_pairs={{0,0},{1,16},{2,32},{3,48},{4,64},{5,80},{6,96},{7,112},{8,8},{9,2... | collective-permute-start | bytes 688136 | tf_op jit(solution)/shard_map/ppermute | solution.py:28
  102.5 45.6 %copy-start = (f32[224,896]{1,0:T(8,128)S(1)}, f32[224,896]{1,0:T(8,128)}, u32[]{:S(2)}) copy-start(f32[224,896]{1,0:T(8,128)} %get-tuple-element.12.refs_1_) | copy-start | bytes 2408452
  102.5 35.7 %collective-permute-start.12 = (s16[128,896]{1,0:T(8,128)(2,1)}, s16[128,896]{1,0:T(8,128)(2,1)S(1)}, u32[]{:S(2)}, u32[]{:S(2)}) collective-permute-start(s16[128,896]{1,0:T(8,128)(2,1)} %get-tuple-element.16), channel_id=1, source_target_pairs={{0,8},{1,24},{2,40},{3,56},{4,72},{5,88},{6,104},{7,120},{8,0},{9,... | collective-permute-start | bytes 688136 | tf_op jit(solution)/shard_map/ppermute | solution.py:28
  113.8 29.3 %collective-permute-start.11 = (s16[128,896]{1,0:T(8,128)(2,1)}, s16[128,896]{1,0:T(8,128)(2,1)S(1)}, u32[]{:S(2)}, u32[]{:S(2)}) collective-permute-start(s16[128,896]{1,0:T(8,128)(2,1)} %get-tuple-element.15), channel_id=1, source_target_pairs={{0,8},{1,24},{2,40},{3,56},{4,72},{5,88},{6,104},{7,120},{8,0},{9,... | collective-permute-start | bytes 688136 | tf_op jit(solution)/shard_map/ppermute | solution.py:28
  114.7 33.4 %collective-permute-start.9 = (s16[128,896]{1,0:T(8,128)(2,1)}, s16[128,896]{1,0:T(8,128)(2,1)S(1)}, u32[]{:S(2)}, u32[]{:S(2)}) collective-permute-start(s16[128,896]{1,0:T(8,128)(2,1)} %get-tuple-element.13), channel_id=1, source_target_pairs={{0,0},{1,16},{2,32},{3,48},{4,64},{5,80},{6,96},{7,112},{8,8},{9,2... | collective-permute-start | bytes 688136 | tf_op jit(solution)/shard_map/ppermute | solution.py:28
  148.1 1.1 copy-start.1
Sparse Core Ops, SparseCore 0:
  9.1 82.9 all-gather.1

commit v3 on v0

v3 whole, which is shorter than its diff:
```python
import jax
import jax.numpy as jnp
from jax import lax
from jax.experimental import pallas as pl
from jax.experimental.pallas import tpu as pltpu
from jax.sharding import PartitionSpec as P

Z_LO, X, CORE, Y, Z_HI = 2, 4, 2, 4, 2
AXES = ("row", "col")
LEVELS = 15
MIB = 2**20


def device_index(z_lo, x, core, y, z_hi):
    return ((z_lo * X + x) * CORE + core) * (Y * Z_HI) + y * Z_HI + z_hi


def places():
    for z_lo in range(Z_LO):
        for x in range(X):
            for core in range(CORE):
                for y in range(Y):
                    for z_hi in range(Z_HI):
                        yield z_lo, x, core, y, z_hi


def send(block, target):
    pairs = [(device_index(*place), device_index(*target(*place))) for place in places()]
    return lax.ppermute(block, AXES, pairs)


def along_x(step):
    return lambda z_lo, x, core, y, z_hi: (z_lo, (x + step) % X, core, y, z_hi)


def along_y(step):
    return lambda z_lo, x, core, y, z_hi: (z_lo, x, core, (y + step) % Y, z_hi)


def across_z_lo(z_lo, x, core, y, z_hi):
    return 1 - z_lo, x, core, y, z_hi


def across_z_hi(z_lo, x, core, y, z_hi):
    return z_lo, x, core, y, 1 - z_hi


def across_core(z_lo, x, core, y, z_hi):
    return z_lo, x, 1 - core, y, z_hi


def mirrored(flip):
    def target(z_lo, x, core, y, z_hi):
        chip_row, chip_col = z_lo * X + x, y * Z_HI + z_hi
        return chip_col // X, chip_col % X, core ^ flip, chip_row // Z_HI, chip_row % Z_HI

    return target


def after(block, *earlier):
    return lax.optimization_barrier((block, *earlier))[0]


def gather(left, right):
    half = left.shape[0] // 2
    right_z = send(right, across_z_lo)
    right_up, right_down = send(right, along_x(1)), send(right, along_x(-1))
    left_up, left_down = send(left, along_y(1)), send(left, along_y(-1))
    left_z = send(after(left, right_z), across_z_hi)
    right_z = after(right_z, right_up, right_down)
    right_z_up, right_z_down = send(right_z, along_x(1)), send(right_z, along_x(-1))
    left_top, left_bottom = send(left_up[:half], along_y(1)), send(left_down[half:], along_y(-1))
    left_z_up, left_z_down = send(left_z, along_y(1)), send(left_z, along_y(-1))
    right_top = send(jnp.concatenate([right_up[:half], right_z_up[:half]]), along_x(1))
    right_bottom = send(jnp.concatenate([right_down[half:], right_z_down[half:]]), along_x(-1))
    left_z_top, left_z_bottom = send(left_z_up[:half], along_y(1)), send(left_z_down[half:], along_y(-1))
    near = [(left, 0, 0), (left_down, 1, 0), (left_top, 2, 0), (left_bottom, 2, half), (left_up, 3, 0)]
    far = [(left_z, 0, 0), (left_z_down, 1, 0), (left_z_top, 2, 0), (left_z_bottom, 2, half), (left_z_up, 3, 0)]
    return near, far, [
        (right, 0), (right_down, 1), (right_up, 3), (right_z, 4), (right_z_down, 5), (right_z_up, 7),
        (right_top, 2, 6), (right_bottom, 2, 6)]


def lookup(energies, orbital_index):
    labels = jnp.arange(energies.shape[0], dtype=jnp.int32)
    picked = jnp.where(orbital_index[:, None] == labels[None, :], energies[None, :], 0.0)
    return jnp.sum(picked, axis=1)


def partial_kernel(far, left_places, right_places, *refs):
    left_parts, refs = refs[:len(left_places)], refs[len(left_places):]
    right_parts, refs = refs[:len(right_places)], refs[len(right_places):]
    if far:
        sum_ref, give_ref, keep_ref, left, right, acc, sem_left, sem_right = refs
    else:
        out_ref, left, right, acc, sem_left, sem_right = refs
    row, col = lax.axis_index("row"), lax.axis_index("col")
    z_lo, x, core = row // (X * CORE), (row // CORE) % X, row % CORE
    y, z_hi = col // Z_HI, col % Z_HI
    rows, depth = left.shape[1], left.shape[2] // 2
    half = rows // 2
    copies = []
    for i, (slot, at) in enumerate(left_places):
        part = left_parts[i]
        copies.append(pltpu.make_async_copy(part, left.at[slot, pl.ds(at, part.shape[0]), :], sem_left.at[i]))
    at = 0
    for i, (first, *second) in enumerate(right_places):
        part = right_parts[i]
        if second:
            base = half if i == len(right_places) - 1 else 0
            for which, slot in enumerate((first, *second)):
                copies.append(pltpu.make_async_copy(
                    part.at[pl.ds(which * half, half), :], right.at[slot, pl.ds(base, half), :], sem_right.at[at]))
                at += 1
        else:
            copies.append(pltpu.make_async_copy(part, right.at[first], sem_right.at[at]))
            at += 1
    for copy in copies:
        copy.start()
    for copy in copies:
        copy.wait()
    for slot in range(Y):
        block = lax.rem(y + slot, Y) * Z_HI + (1 - z_hi if far else z_hi)
        plane = (block // X + z_lo) % Z_LO
        place = plane * X + lax.rem(block % X - x + X, X)
        both = jnp.concatenate([left[slot][:, :depth], left[slot][:, depth:]])
        term = jnp.dot(both, right[place], preferred_element_type=jnp.float32)
        if slot == 0:
            acc[...] = term + sum_ref[...] if far else term
        elif far or slot < Y - 1:
            acc[...] += term
        else:
            out_ref[...] = acc[...] + term
    if far:
        give_ref[...] = acc[pl.ds(pl.multiple_of((1 - core) * rows, rows), rows), :]
        keep_ref[...] = acc[pl.ds(pl.multiple_of(core * rows, rows), rows), :]


def partial_product(left, right, earlier=None):
    far = earlier is not None
    rows, cols = left[0][0].shape
    parts = [part for part, *_ in left] + [part for part, *_ in right] + ([earlier] if far else [])
    left_places = [tuple(place) for _, *place in left]
    right_places = [tuple(place) for _, *place in right]
    whole = jax.ShapeDtypeStruct((2 * rows, cols), jnp.float32)
    one = jax.ShapeDtypeStruct((rows, cols), jnp.float32)
    vmem = pl.BlockSpec(memory_space=pltpu.VMEM)
    return pl.pallas_call(
        lambda *refs: partial_kernel(far, left_places, right_places, *refs),
        out_shape=[one, one] if far else whole,
        in_specs=[pl.BlockSpec(memory_space=pl.ANY)] * (len(left) + len(right)) + ([vmem] if far else []),
        out_specs=[vmem, vmem] if far else vmem,
        scratch_shapes=[
            pltpu.VMEM((Y, rows, cols), jnp.bfloat16),
            pltpu.VMEM((Z_LO * X, rows, cols), jnp.bfloat16),
            pltpu.VMEM((2 * rows, cols), jnp.float32),
            pltpu.SemaphoreType.DMA((len(left),)),
            pltpu.SemaphoreType.DMA((len(right) + 2,)),
        ],
        compiler_params=pltpu.CompilerParams(vmem_limit_bytes=26 * MIB),
        cost_estimate=pl.CostEstimate(
            flops=2 * Y * 2 * rows * cols * cols // 2, bytes_accessed=18 * MIB, transcendentals=0),
        name="partial_product",
    )(*parts)


def encode(block, payload_ref):
    part = block.shape[0] // 2
    packed = jnp.concatenate([block[:part], block[part:]], axis=1)
    top = jnp.maximum(jnp.max(jnp.abs(packed), axis=0, keepdims=True), 1e-30)
    power = jnp.ceil(jnp.log2(top) + 1e-3)
    payload_ref[:part, :] = jnp.round(packed * jnp.exp2(LEVELS - power)).astype(jnp.int32).astype(jnp.int16)
    payload_ref[part:, :] = jnp.broadcast_to(power, (16, packed.shape[1])).astype(jnp.int32).astype(jnp.int16)


def decode(payload_ref):
    part = payload_ref.shape[0] - 16
    power = payload_ref[part:, :].astype(jnp.int32).astype(jnp.float32)[:1]
    packed = payload_ref[:part, :].astype(jnp.int32).astype(jnp.float32) * jnp.exp2(power - LEVELS)
    width = packed.shape[1] // 2
    return jnp.concatenate([packed[:, :width], packed[:, width:]])


def join_kernel(keep_ref, got_ref, out_ref, same_ref, cross_ref):
    core = lax.axis_index("row") % CORE
    out_ref[...] = keep_ref[...] + got_ref[...]
    half = out_ref.shape[1] // 2
    low, high = out_ref[:, :half], out_ref[:, half:]
    encode(jnp.where(core == 0, low, high), same_ref)
    encode(jnp.where(core == 0, high, low), cross_ref)


def join(keep, got):
    rows, cols = keep.shape
    payload = jax.ShapeDtypeStruct((rows // 2 + 16, cols), jnp.int16)
    vmem = pl.BlockSpec(memory_space=pltpu.VMEM)
    return pl.pallas_call(
        join_kernel,
        out_shape=[jax.ShapeDtypeStruct((rows, cols), jnp.float32), payload, payload],
        in_specs=[vmem] * 2,
        out_specs=[vmem] * 3,
        compiler_params=pltpu.CompilerParams(vmem_limit_bytes=26 * MIB),
        cost_estimate=pl.CostEstimate(flops=4 * rows * cols, bytes_accessed=12 * rows * cols, transcendentals=0),
        name="join",
    )(keep, got)


def combine_kernel(product_ref, same_ref, cross_ref, row_gap_ref, col_gap_ref, out_ref):
    core = lax.axis_index("row") % CORE
    same, cross = decode(same_ref).T, decode(cross_ref).T
    mirror = jnp.concatenate(
        [jnp.where(core == 0, same, cross), jnp.where(core == 0, cross, same)], axis=1)
    out_ref[...] = (product_ref[...] + mirror) / (row_gap_ref[...] + col_gap_ref[...])


def combine(product, same, cross, row_gap, col_gap):
    rows, cols = product.shape
    return pl.pallas_call(
        combine_kernel,
        out_shape=jax.ShapeDtypeStruct((rows, cols), jnp.float32),
        in_specs=[pl.BlockSpec(memory_space=pltpu.VMEM)] * 5,
        out_specs=pl.BlockSpec(memory_space=pltpu.VMEM),
        compiler_params=pltpu.CompilerParams(vmem_limit_bytes=26 * MIB),
        cost_estimate=pl.CostEstimate(flops=4 * rows * cols, bytes_accessed=12 * rows * cols, transcendentals=0),
        name="combine",
    )(product, same, cross, row_gap[:, None], col_gap[None, :])


def shards(amplitudes, integrals, occ_energy, vir_energy, pair_occ, pair_vir):
    tile_rows, tile_cols = amplitudes.shape
    core = lax.axis_index("row") % CORE
    other = send(jnp.roll(amplitudes, tile_cols // 2, axis=1), across_core)
    lane = lax.broadcasted_iota(jnp.int32, amplitudes.shape, 1)
    left = jnp.where((lane < tile_cols // 2) == (core == 0), amplitudes, other)
    near, far, right = gather(left, integrals)
    give, keep = partial_product(far, right, partial_product(near, right))
    product, to_same, to_cross = join(keep, send(give, across_core))
    same, cross = send(to_same, mirrored(0)), send(to_cross, mirrored(1))

    row_start = lax.axis_index("row") * tile_rows
    col_start = lax.axis_index("col") * tile_cols
    row_occ = lax.dynamic_slice_in_dim(pair_occ, row_start, tile_rows)
    row_vir = lax.dynamic_slice_in_dim(pair_vir, row_start, tile_rows)
    col_occ = lax.dynamic_slice_in_dim(pair_occ, col_start, tile_cols)
    col_vir = lax.dynamic_slice_in_dim(pair_vir, col_start, tile_cols)
    row_gap = lookup(occ_energy, row_occ) - lookup(vir_energy, row_vir)
    col_gap = lookup(occ_energy, col_occ) - lookup(vir_energy, col_vir)
    return combine(product, same, cross, row_gap, col_gap)


def solution(mesh):
    return jax.shard_map(
        shards,
        mesh=mesh,
        in_specs=(P("row", "col"), P("row", "col"), P(), P(), P(), P()),
        out_specs=P("row", "col"),
        check_vma=False,
    )
```

time: 324 us -> 151 us (0.47)
  waiting for transfers between devices: 279 us -> 93.7 us
  starting transfers between devices: 0.04 us -> 25.8 us
  matrix products: 21.5 us -> 0 us
  Pallas kernels: 0 us -> 17.8 us
  between operations: 13.4 us -> 0.21 us
  local copies, waits for them, and re-layouts: 3.1 us -> 7.54 us
    all_gather x2 -> x0, waiting for transfers between devices: 278 us -> none  [the longest x1 144 us: shards(): row_panels = lax.all_gather(left_local, 'col', axis=2, tiled=True)]
    ppermute x0 -> x20, waiting for transfers between devices: none -> 93.7 us  [send(): return lax.ppermute(block, AXES, pairs)]
    ppermute x0 -> x20, starting transfers between devices: none -> 25.8 us  [send(): return lax.ppermute(block, AXES, pairs)]
    dot_general x1 -> x0, matrix products: 21.5 us -> none  [shards(): jnp.einsum('lrk,lkc->rc', row_panels, lax.all_gather(right_local, 'row',...]
    pallas_call x0 -> x4, Pallas kernels: none -> 17.8 us  [the longest x2 13.6 us: partial_product(): pl.pallas_call(lambda *refs: partial_kernel(far, left_places, right_place...]
    another operation x1 -> x0, other arithmetic: 3.98 us -> none  [shards(): right_local = jnp.stack((integrals, amplitudes))]
  transfers between devices with their start and end apart: 2 -> 20, of which waited for: 2 -> 12; matrix products, arithmetic and copies ran while one was open for 1% -> 4% of each run, Pallas kernels for 0% -> 4%
where the time goes in v3:
time: 151 us; the launch traced here: 149 us
  waiting for transfers between devices  93.7 us (62%)
  starting transfers between devices  25.8 us (17%)
  Pallas kernels  17.8 us (12%)
  local copies, waits for them, and re-layouts  7.54 us (5%)
  other arithmetic  3.8 us (3%)
    ppermute x20, waiting for transfers between devices, send(): return lax.ppermute(block, AXES, pairs)  93.7 us
    ppermute x20, starting transfers between devices, send(): return lax.ppermute(block, AXES, pairs)  25.8 us
    pallas_call x2, Pallas kernels, partial_product(): pl.pallas_call(lambda *refs: partial_kernel(far, left_places, right_place...  13.6 us
  transfers between devices with their start and end apart: 20, of which 12 were waited for; matrix products, arithmetic and copies ran while one was open for 4% of the time, Pallas kernels for 4%

profile of v3, /device:TPU:16, one launch (start us, length us, event | category | flops | bytes accessed | tf_op | source)
XLA Modules:
  0.0 148.9 jit_solution(14700439475906043463)
XLA Ops:
  0.0 1.5 fusion.1
  1.5 1.1 pad_maximum_fusion
  2.6 1.9 %collective-permute-start.1 = (bf16[448,896]{1,0:T(8,128)(2,1)S(1)}, bf16[448,896]{1,0:T(8,128)(2,1)S(1)}, u32[]{:S(2)}, u32[]{:S(2)}) collective-permute-start(bf16[448,896]{1,0:T(8,128)(2,1)S(1)} %copy-done), channel_id=1, source_target_pairs={{0,64},{1,65},{2,66},{3,67},{4,68},{5,69},{6,70},{7,71},{8,72},{9,... | collective-permute-start | bytes 2408456 | tf_op jit(solution)/shard_map/ppermute | solution.py:29
  4.5 2.8 %collective-permute-start.7 = (bf16[448,896]{1,0:T(8,128)(2,1)S(1)}, bf16[448,896]{1,0:T(8,128)(2,1)S(1)}, u32[]{:S(2)}, u32[]{:S(2)}) collective-permute-start(bf16[448,896]{1,0:T(8,128)(2,1)S(1)} %copy-done), channel_id=1, source_target_pairs={{0,48},{1,49},{2,50},{3,51},{4,52},{5,53},{6,54},{7,55},{8,56},{9,... | collective-permute-start | bytes 2408456 | tf_op jit(solution)/shard_map/ppermute | solution.py:29
  7.3 1.5 broadcast_select_fusion.refs_0_
  8.8 14.3 %collective-permute-done.1.refs_8_ = bf16[448,896]{1,0:T(8,128)(2,1)S(1)} collective-permute-done((bf16[448,896]{1,0:T(8,128)(2,1)S(1)}, bf16[448,896]{1,0:T(8,128)(2,1)S(1)}, u32[]{:S(2)}, u32[]{:S(2)}) %collective-permute-start.1) | collective-permute-done | bytes 802848 | tf_op jit(solution)/shard_map/ppermute | solution.py:29
  23.1 3.7 %collective-permute-start.2 = (bf16[448,896]{1,0:T(8,128)(2,1)S(1)}, bf16[448,896]{1,0:T(8,128)(2,1)S(1)}, u32[]{:S(2)}, u32[]{:S(2)}) collective-permute-start(bf16[448,896]{1,0:T(8,128)(2,1)S(1)} %broadcast_select_fusion.refs_0_), channel_id=1, source_target_pairs={{0,1},{1,0},{2,3},{3,2},{4,5},{5,4},{6,7},{7,6},{8,9},{9,8},{10,11... | collective-permute-start | bytes 2408456 | tf_op jit(solution)/shard_map/ppermute | solution.py:29
  26.8 1.4 collective-permute-done.8.refs_7_
  28.3 3.2 %collective-permute-start.9 = (bf16[448,896]{1,0:T(8,128)(2,1)S(1)}, bf16[448,896]{1,0:T(8,128)(2,1)S(1)}, u32[]{:S(2)}, u32[]{:S(2)}) collective-permute-start(bf16[448,896]{1,0:T(8,128)(2,1)S(1)} %collective-permute-done.1.refs_8_), channel_id=1, source_target_pairs={{0,48},{1,49},{2,50},{3,51},{4,52},{5,53},{6,54},{7,55},{8,56},{9,... | collective-permute-start | bytes 2408456 | tf_op jit(solution)/shard_map/ppermute | solution.py:29
  31.5 1.3 collective-permute-start.14
  33.5 11.1 %collective-permute-done.2.refs_0_ = bf16[448,896]{1,0:T(8,128)(2,1)S(1)} collective-permute-done((bf16[448,896]{1,0:T(8,128)(2,1)S(1)}, bf16[448,896]{1,0:T(8,128)(2,1)S(1)}, u32[]{:S(2)}, u32[]{:S(2)}) %collective-permute-start.2) | collective-permute-done | bytes 802848 | tf_op jit(solution)/shard_map/ppermute | solution.py:29
  44.6 1.3 collective-permute-start.4
  45.9 2.4 %collective-permute-done.10.refs_10_ = bf16[448,896]{1,0:T(8,128)(2,1)S(1)} collective-permute-done((bf16[448,896]{1,0:T(8,128)(2,1)S(1)}, bf16[448,896]{1,0:T(8,128)(2,1)S(1)}, u32[]{:S(2)}, u32[]{:S(2)}) %collective-permute-start.10) | collective-permute-done | bytes 802848 | tf_op jit(solution)/shard_map/ppermute | solution.py:29
  49.2 3.1 %collective-permute-done.14.refs_4_ = bf16[448,896]{1,0:T(8,128)(2,1)S(1)} collective-permute-done((bf16[448,896]{1,0:T(8,128)(2,1)S(1)}, bf16[448,896]{1,0:T(8,128)(2,1)S(1)}, u32[]{:S(2)}, u32[]{:S(2)}) %collective-permute-start.14) | collective-permute-done | bytes 802848 | tf_op jit(solution)/shard_map/ppermute | solution.py:29
  52.5 1.6 %collective-permute-start.15 = (bf16[224,896]{1,0:T(8,128)(2,1)S(1)}, bf16[224,896]{1,0:T(8,128)(2,1)S(1)}, u32[]{:S(2)}, u32[]{:S(2)}) collective-permute-start(bf16[224,896]{1,0:T(8,128)(2,1)S(1)} %slice.48), channel_id=1, source_target_pairs={{0,2},{1,3},{2,4},{3,5},{4,6},{5,7},{6,0},{7,1},{8,10},{9,11},{10,... | collective-permute-start | bytes 1204232 | tf_op jit(solution)/shard_map/ppermute | solution.py:29
  54.1 15.4 %collective-permute-done.4.refs_4_ = bf16[448,896]{1,0:T(8,128)(2,1)S(1)} collective-permute-done((bf16[448,896]{1,0:T(8,128)(2,1)S(1)}, bf16[448,896]{1,0:T(8,128)(2,1)S(1)}, u32[]{:S(2)}, u32[]{:S(2)}) %collective-permute-start.4) | collective-permute-done | bytes 802848 | tf_op jit(solution)/shard_map/ppermute | solution.py:29
  70.0 1.6 %collective-permute-start.5 = (bf16[224,896]{1,0:T(8,128)(2,1)S(1)}, bf16[224,896]{1,0:T(8,128)(2,1)S(1)}, u32[]{:S(2)}, u32[]{:S(2)}) collective-permute-start(bf16[224,896]{1,0:T(8,128)(2,1)S(1)} %slice.42), channel_id=1, source_target_pairs={{0,2},{1,3},{2,4},{3,5},{4,6},{5,7},{6,0},{7,1},{8,10},{9,11},{10,... | collective-permute-start | bytes 1204232 | tf_op jit(solution)/shard_map/ppermute | solution.py:29
  71.7 6.4 %collective-permute-done.15.refs_2_ = bf16[224,896]{1,0:T(8,128)(2,1)S(1)} collective-permute-done((bf16[224,896]{1,0:T(8,128)(2,1)S(1)}, bf16[224,896]{1,0:T(8,128)(2,1)S(1)}, u32[]{:S(2)}, u32[]{:S(2)}) %collective-permute-start.15) | collective-permute-done | bytes 401440 | tf_op jit(solution)/shard_map/ppermute | solution.py:29
  78.9 6.0 %partial_product.2.refs_13_ = f32[896,896]{1,0:T(8,128)S(1)} custom-call(bf16[448,896]{1,0:T(8,128)(2,1)S(1)} %broadcast_select_fusion.refs_0_, bf16[448,896]{1,0:T(8,128)(2,1)S(1)} %collective-permute-done.13.refs_1_, bf16[224,896]{1,0:T(8,128)(2,1)S(1)} %collective-permute-done.15.refs_2_, bf16[224,896]{1,0:T(8,128)(2,1)S(1)} %collective-permute-done.16.refs_3_, ...), custom_call_target="tpu_custom_call" | custom-call | flops 2877292544 | bytes 18874368 | tf_op jit(solution)/shard_map/partial_product/pallas_call | solution.py:148
  84.9 1.1 collective-permute-done.6.refs_3_
  86.0 7.6 %partial_product.3 = (f32[448,896]{1,0:T(8,128)}, f32[448,896]{1,0:T(8,128)S(1)}) custom-call(bf16[448,896]{1,0:T(8,128)(2,1)S(1)} %collective-permute-done.2.refs_0_, bf16[448,896]{1,0:T(8,128)(2,1)S(1)} %collective-permute-done.3.refs_1_, bf16[224,896]{1,0:T(8,128)(2,1)S(1)} %collective-permute-done.5.refs_2_, ...), custom_call_target="tpu_custom_call" | custom-call | flops 2877292544 | bytes 18874368 | tf_op jit(solution)/shard_map/partial_product/pallas_call | solution.py:148
  93.6 1.2 copy-done.1
  94.7 0.8 dynamic_slice.13
  95.5 0.8 dynamic_slice.12
  96.3 0.8 dynamic_slice.15
  98.4 1.4 copy-done.2
  99.8 1.7 %join.1 = (f32[448,896]{1,0:T(8,128)S(1)}, s16[240,896]{1,0:T(8,128)(2,1)}, s16[240,896]{1,0:T(8,128)(2,1)}) custom-call(f32[448,896]{1,0:T(8,128)S(1)} %copy-done.2, f32[448,896]{1,0:T(8,128)S(1)} %collective-permute-done.17.got_ref), custom_call_target="tpu_custom_call" | custom-call | flops 1605632 | bytes 4816896 | tf_op jit(solution)/shard_map/join/pallas_call | solution.py:197
  101.6 3.3 %collective-permute-start.18 = (s16[240,896]{1,0:T(8,128)(2,1)}, s16[240,896]{1,0:T(8,128)(2,1)S(1)}, u32[]{:S(2)}, u32[]{:S(2)}) collective-permute-start(s16[240,896]{1,0:T(8,128)(2,1)} %get-tuple-element.17), channel_id=1, source_target_pairs={{0,0},{1,16},{2,32},{3,48},{4,64},{5,80},{6,96},{7,112},{8,8},{9,2... | collective-permute-start | bytes 1290248 | tf_op jit(solution)/shard_map/ppermute | solution.py:29
  104.8 2.8 %collective-permute-start.19 = (s16[240,896]{1,0:T(8,128)(2,1)}, s16[240,896]{1,0:T(8,128)(2,1)S(1)}, u32[]{:S(2)}, u32[]{:S(2)}) collective-permute-start(s16[240,896]{1,0:T(8,128)(2,1)} %get-tuple-element.18), channel_id=1, source_target_pairs={{0,8},{1,24},{2,40},{3,56},{4,72},{5,88},{6,104},{7,120},{8,0},{9,... | collective-permute-start | bytes 1290248 | tf_op jit(solution)/shard_map/ppermute | solution.py:29
  108.5 30.0 %collective-permute-done.18.same_ref = s16[240,896]{1,0:T(8,128)(2,1)S(1)} collective-permute-done((s16[240,896]{1,0:T(8,128)(2,1)}, s16[240,896]{1,0:T(8,128)(2,1)S(1)}, u32[]{:S(2)}, u32[]{:S(2)}) %collective-permute-start.18) | collective-permute-done | bytes 430112 | tf_op jit(solution)/shard_map/ppermute | solution.py:29
  138.4 7.9 %collective-permute-done.19.cross_ref = s16[240,896]{1,0:T(8,128)(2,1)S(1)} collective-permute-done((s16[240,896]{1,0:T(8,128)(2,1)}, s16[240,896]{1,0:T(8,128)(2,1)S(1)}, u32[]{:S(2)}, u32[]{:S(2)}) %collective-permute-start.19) | collective-permute-done | bytes 430112 | tf_op jit(solution)/shard_map/ppermute | solution.py:29
  146.3 2.5 %combine.1 = f32[448,896]{1,0:T(8,128)} custom-call(f32[448,896]{1,0:T(8,128)S(1)} %get-tuple-element.16.product_ref, s16[240,896]{1,0:T(8,128)(2,1)S(1)} %collective-permute-done.18.same_ref, s16[240,896]{1,0:T(8,128)(2,1)S(1)} %collective-permute-done.19.cross_ref, f32[448,1]{1,0:T(8,128)S(1)} %copy.8.row_gap_ref, f32[1,896]{1,0:T(1,128)S(1)} %sub.29.col_gap_ref), custom_call_target="tpu_custom_call" | custom-call | flops 1605632 | bytes 4816896 | tf_op jit(solution)/shard_map/combine/pallas_call | solution.py:218
  (48 shorter events, 5.3 us)
Async XLA Ops:
  0.0 2.6 %copy-start = (bf16[448,896]{1,0:T(8,128)(2,1)S(1)}, bf16[448,896]{1,0:T(8,128)(2,1)}, u32[]{:S(2)}) copy-start(bf16[448,896]{1,0:T(8,128)(2,1)} %refs_5_.3) | copy-start | bytes 2408452
  2.6 4.7 %collective-permute-start = (bf16[448,896]{1,0:T(8,128)(2,1)}, bf16[448,896]{1,0:T(8,128)(2,1)}, u32[]{:S(2)}, u32[]{:S(2)}) collective-permute-start(bf16[448,896]{1,0:T(8,128)(2,1)} %pad_maximum_fusion), channel_id=1, source_target_pairs={{0,8},{1,9},{2,10},{3,11},{4,12},{5,13},{6,14},{7,15},{8,0},{9,1},... | collective-permute-start | bytes 2408456 | tf_op jit(solution)/shard_map/ppermute | solution.py:29
  2.6 20.5 %collective-permute-start.1 = (bf16[448,896]{1,0:T(8,128)(2,1)S(1)}, bf16[448,896]{1,0:T(8,128)(2,1)S(1)}, u32[]{:S(2)}, u32[]{:S(2)}) collective-permute-start(bf16[448,896]{1,0:T(8,128)(2,1)S(1)} %copy-done), channel_id=1, source_target_pairs={{0,64},{1,65},{2,66},{3,67},{4,68},{5,69},{6,70},{7,71},{8,72},{9,... | collective-permute-start | bytes 2408456 | tf_op jit(solution)/shard_map/ppermute | solution.py:29
  4.5 22.3 %collective-permute-start.7 = (bf16[448,896]{1,0:T(8,128)(2,1)S(1)}, bf16[448,896]{1,0:T(8,128)(2,1)S(1)}, u32[]{:S(2)}, u32[]{:S(2)}) collective-permute-start(bf16[448,896]{1,0:T(8,128)(2,1)S(1)} %copy-done), channel_id=1, source_target_pairs={{0,48},{1,49},{2,50},{3,51},{4,52},{5,53},{6,54},{7,55},{8,56},{9,... | collective-permute-start | bytes 2408456 | tf_op jit(solution)/shard_map/ppermute | solution.py:29
  7.3 21.0 %collective-permute-start.8 = (bf16[448,896]{1,0:T(8,128)(2,1)S(1)}, bf16[448,896]{1,0:T(8,128)(2,1)S(1)}, u32[]{:S(2)}, u32[]{:S(2)}) collective-permute-start(bf16[448,896]{1,0:T(8,128)(2,1)S(1)} %copy-done), channel_id=1, source_target_pairs={{0,16},{1,17},{2,18},{3,19},{4,20},{5,21},{6,22},{7,23},{8,24},{9,... | collective-permute-start | bytes 2408456 | tf_op jit(solution)/shard_map/ppermute | solution.py:29
  23.1 21.5 %collective-permute-start.2 = (bf16[448,896]{1,0:T(8,128)(2,1)S(1)}, bf16[448,896]{1,0:T(8,128)(2,1)S(1)}, u32[]{:S(2)}, u32[]{:S(2)}) collective-permute-start(bf16[448,896]{1,0:T(8,128)(2,1)S(1)} %broadcast_select_fusion.refs_0_), channel_id=1, source_target_pairs={{0,1},{1,0},{2,3},{3,2},{4,5},{5,4},{6,7},{7,6},{8,9},{9,8},{10,11... | collective-permute-start | bytes 2408456 | tf_op jit(solution)/shard_map/ppermute | solution.py:29
  28.3 20.1 %collective-permute-start.10 = (bf16[448,896]{1,0:T(8,128)(2,1)S(1)}, bf16[448,896]{1,0:T(8,128)(2,1)S(1)}, u32[]{:S(2)}, u32[]{:S(2)}) collective-permute-start(bf16[448,896]{1,0:T(8,128)(2,1)S(1)} %collective-permute-done.1.refs_8_), channel_id=1, source_target_pairs={{0,16},{1,17},{2,18},{3,19},{4,20},{5,21},{6,22},{7,23},{8,24},{9,... | collective-permute-start | bytes 2408456 | tf_op jit(solution)/shard_map/ppermute | solution.py:29
  28.3 20.2 %collective-permute-start.9 = (bf16[448,896]{1,0:T(8,128)(2,1)S(1)}, bf16[448,896]{1,0:T(8,128)(2,1)S(1)}, u32[]{:S(2)}, u32[]{:S(2)}) collective-permute-start(bf16[448,896]{1,0:T(8,128)(2,1)S(1)} %collective-permute-done.1.refs_8_), channel_id=1, source_target_pairs={{0,48},{1,49},{2,50},{3,51},{4,52},{5,53},{6,54},{7,55},{8,56},{9,... | collective-permute-start | bytes 2408456 | tf_op jit(solution)/shard_map/ppermute | solution.py:29
  31.5 20.8 %collective-permute-start.14 = (bf16[448,896]{1,0:T(8,128)(2,1)S(1)}, bf16[448,896]{1,0:T(8,128)(2,1)S(1)}, u32[]{:S(2)}, u32[]{:S(2)}) collective-permute-start(bf16[448,896]{1,0:T(8,128)(2,1)S(1)} %broadcast_select_fusion.refs_0_), channel_id=1, source_target_pairs={{0,2},{1,3},{2,4},{3,5},{4,6},{5,7},{6,0},{7,1},{8,10},{9,11},{10,... | collective-permute-start | bytes 2408456 | tf_op jit(solution)/shard_map/ppermute | solution.py:29
  32.8 19.7 %collective-permute-start.13 = (bf16[448,896]{1,0:T(8,128)(2,1)S(1)}, bf16[448,896]{1,0:T(8,128)(2,1)S(1)}, u32[]{:S(2)}, u32[]{:S(2)}) collective-permute-start(bf16[448,896]{1,0:T(8,128)(2,1)S(1)} %broadcast_select_fusion.refs_0_), channel_id=1, source_target_pairs={{0,6},{1,7},{2,0},{3,1},{4,2},{5,3},{6,4},{7,5},{8,14},{9,15},{10,... | collective-permute-start | bytes 2408456 | tf_op jit(solution)/shard_map/ppermute | solution.py:29
  44.6 24.9 %collective-permute-start.4 = (bf16[448,896]{1,0:T(8,128)(2,1)S(1)}, bf16[448,896]{1,0:T(8,128)(2,1)S(1)}, u32[]{:S(2)}, u32[]{:S(2)}) collective-permute-start(bf16[448,896]{1,0:T(8,128)(2,1)S(1)} %collective-permute-done.2.refs_0_), channel_id=1, source_target_pairs={{0,2},{1,3},{2,4},{3,5},{4,6},{5,7},{6,0},{7,1},{8,10},{9,11},{10,... | collective-permute-start | bytes 2408456 | tf_op jit(solution)/shard_map/ppermute | solution.py:29
  48.5 30.4 %collective-permute-start.11 = (bf16[448,896]{1,0:T(8,128)(2,1)S(1)}, bf16[448,896]{1,0:T(8,128)(2,1)S(1)}, u32[]{:S(2)}, u32[]{:S(2)}) collective-permute-start(bf16[448,896]{1,0:T(8,128)(2,1)S(1)} %pad_maximum_fusion.1), channel_id=1, source_target_pairs={{0,16},{1,17},{2,18},{3,19},{4,20},{5,21},{6,22},{7,23},{8,24},{9,... | collective-permute-start | bytes 2408456 | tf_op jit(solution)/shard_map/ppermute | solution.py:29
  48.6 21.5 %collective-permute-start.3 = (bf16[448,896]{1,0:T(8,128)(2,1)S(1)}, bf16[448,896]{1,0:T(8,128)(2,1)S(1)}, u32[]{:S(2)}, u32[]{:S(2)}) collective-permute-start(bf16[448,896]{1,0:T(8,128)(2,1)S(1)} %collective-permute-done.2.refs_0_), channel_id=1, source_target_pairs={{0,6},{1,7},{2,0},{3,1},{4,2},{5,3},{6,4},{7,5},{8,14},{9,15},{10,... | collective-permute-start | bytes 2408456 | tf_op jit(solution)/shard_map/ppermute | solution.py:29
  52.3 26.6 %collective-permute-start.12 = (bf16[448,896]{1,0:T(8,128)(2,1)S(1)}, bf16[448,896]{1,0:T(8,128)(2,1)S(1)}, u32[]{:S(2)}, u32[]{:S(2)}) collective-permute-start(bf16[448,896]{1,0:T(8,128)(2,1)S(1)} %pad_maximum_fusion.2), channel_id=1, source_target_pairs={{0,48},{1,49},{2,50},{3,51},{4,52},{5,53},{6,54},{7,55},{8,56},{9,... | collective-permute-start | bytes 2408456 | tf_op jit(solution)/shard_map/ppermute | solution.py:29
  52.5 25.7 %collective-permute-start.15 = (bf16[224,896]{1,0:T(8,128)(2,1)S(1)}, bf16[224,896]{1,0:T(8,128)(2,1)S(1)}, u32[]{:S(2)}, u32[]{:S(2)}) collective-permute-start(bf16[224,896]{1,0:T(8,128)(2,1)S(1)} %slice.48), channel_id=1, source_target_pairs={{0,2},{1,3},{2,4},{3,5},{4,6},{5,7},{6,0},{7,1},{8,10},{9,11},{10,... | collective-permute-start | bytes 1204232 | tf_op jit(solution)/shard_map/ppermute | solution.py:29
  69.5 9.4 %collective-permute-start.16 = (bf16[224,896]{1,0:T(8,128)(2,1)S(1)}, bf16[224,896]{1,0:T(8,128)(2,1)S(1)}, u32[]{:S(2)}, u32[]{:S(2)}) collective-permute-start(bf16[224,896]{1,0:T(8,128)(2,1)S(1)} %slice.49), channel_id=1, source_target_pairs={{0,6},{1,7},{2,0},{3,1},{4,2},{5,3},{6,4},{7,5},{8,14},{9,15},{10,... | collective-permute-start | bytes 1204232 | tf_op jit(solution)/shard_map/ppermute | solution.py:29
  70.0 14.9 %collective-permute-start.5 = (bf16[224,896]{1,0:T(8,128)(2,1)S(1)}, bf16[224,896]{1,0:T(8,128)(2,1)S(1)}, u32[]{:S(2)}, u32[]{:S(2)}) collective-permute-start(bf16[224,896]{1,0:T(8,128)(2,1)S(1)} %slice.42), channel_id=1, source_target_pairs={{0,2},{1,3},{2,4},{3,5},{4,6},{5,7},{6,0},{7,1},{8,10},{9,11},{10,... | collective-permute-start | bytes 1204232 | tf_op jit(solution)/shard_map/ppermute | solution.py:29
  78.1 7.9 %collective-permute-start.6 = (bf16[224,896]{1,0:T(8,128)(2,1)S(1)}, bf16[224,896]{1,0:T(8,128)(2,1)S(1)}, u32[]{:S(2)}, u32[]{:S(2)}) collective-permute-start(bf16[224,896]{1,0:T(8,128)(2,1)S(1)} %slice.43), channel_id=1, source_target_pairs={{0,6},{1,7},{2,0},{3,1},{4,2},{5,3},{6,4},{7,5},{8,14},{9,15},{10,... | collective-permute-start | bytes 1204232 | tf_op jit(solution)/shard_map/ppermute | solution.py:29
  84.9 12.9 %copy-start.3 = (f32[1000]{0:T(1024)S(1)}, f32[1000]{0:T(1024)}, u32[]{:S(2)}) copy-start(f32[1000]{0:T(1024)} %param.9) | copy-start | bytes 12004
  93.6 1.2 copy-start.1
  94.7 3.7 %collective-permute-start.17 = (f32[448,896]{1,0:T(8,128)}, f32[448,896]{1,0:T(8,128)S(1)}, u32[]{:S(2)}, u32[]{:S(2)}) collective-permute-start(f32[448,896]{1,0:T(8,128)} %get-tuple-element.15), channel_id=1, source_target_pairs={{0,8},{1,9},{2,10},{3,11},{4,12},{5,13},{6,14},{7,15},{8,0},{9,1},... | collective-permute-start | bytes 4816904 | tf_op jit(solution)/shard_map/ppermute | solution.py:29
  98.4 1.4 copy-start.2
  99.8 7.8 %copy-start.4 = (f32[80]{0:T(128)S(1)}, f32[80]{0:T(128)}, u32[]{:S(2)}) copy-start(f32[80]{0:T(128)} %param.8) | copy-start | bytes 964
  101.6 36.9 %collective-permute-start.18 = (s16[240,896]{1,0:T(8,128)(2,1)}, s16[240,896]{1,0:T(8,128)(2,1)S(1)}, u32[]{:S(2)}, u32[]{:S(2)}) collective-permute-start(s16[240,896]{1,0:T(8,128)(2,1)} %get-tuple-element.17), channel_id=1, source_target_pairs={{0,0},{1,16},{2,32},{3,48},{4,64},{5,80},{6,96},{7,112},{8,8},{9,2... | collective-permute-start | bytes 1290248 | tf_op jit(solution)/shard_map/ppermute | solution.py:29
  104.8 41.5 %collective-permute-start.19 = (s16[240,896]{1,0:T(8,128)(2,1)}, s16[240,896]{1,0:T(8,128)(2,1)S(1)}, u32[]{:S(2)}, u32[]{:S(2)}) collective-permute-start(s16[240,896]{1,0:T(8,128)(2,1)} %get-tuple-element.18), channel_id=1, source_target_pairs={{0,8},{1,24},{2,40},{3,56},{4,72},{5,88},{6,104},{7,120},{8,0},{9,... | collective-permute-start | bytes 1290248 | tf_op jit(solution)/shard_map/ppermute | solution.py:29

commit v4 on v3

--- a/solution.py
+++ b/solution.py
@@ -55,6 +55,16 @@
         return chip_col // X, chip_col % X, core ^ flip, chip_row // Z_HI, chip_row % Z_HI
 
     return target
+
+
+def detour(z_lo, x, core, y, z_hi):
+    x_bit = x // 2 ^ y % 2 ^ z_hi
+    return x % 2 ^ z_hi ^ z_lo, x // 2 * 2 + x_bit, core, y, x % 2
+
+
+def after_detour(z_lo, x, core, y, z_hi):
+    start = next(place for place in places() if detour(*place) == (z_lo, x, core, y, z_hi))
+    return mirrored(1)(*start)
 
 
 def after(block, *earlier):
@@ -70,12 +80,13 @@
     right_z = after(right_z, right_up, right_down)
     right_z_up, right_z_down = send(right_z, along_x(1)), send(right_z, along_x(-1))
     left_top, left_bottom = send(left_up[:half], along_y(1)), send(left_down[half:], along_y(-1))
+    left_z = after(left_z, left_top, left_bottom)
     left_z_up, left_z_down = send(left_z, along_y(1)), send(left_z, along_y(-1))
     right_top = send(jnp.concatenate([right_up[:half], right_z_up[:half]]), along_x(1))
     right_bottom = send(jnp.concatenate([right_down[half:], right_z_down[half:]]), along_x(-1))
     left_z_top, left_z_bottom = send(left_z_up[:half], along_y(1)), send(left_z_down[half:], along_y(-1))
-    near = [(left, 0, 0), (left_down, 1, 0), (left_top, 2, 0), (left_bottom, 2, half), (left_up, 3, 0)]
-    far = [(left_z, 0, 0), (left_z_down, 1, 0), (left_z_top, 2, 0), (left_z_bottom, 2, half), (left_z_up, 3, 0)]
+    near = [(left,), (left_down,), (left_top, left_bottom), (left_up,)]
+    far = [(left_z,), (left_z_down,), (left_z_top, left_z_bottom), (left_z_up,)]
     return near, far, [
         (right, 0), (right_down, 1), (right_up, 3), (right_z, 4), (right_z_down, 5), (right_z_up, 7),
         (right_top, 2, 6), (right_bottom, 2, 6)]
@@ -87,81 +98,112 @@
     return jnp.sum(picked, axis=1)
 
 
-def partial_kernel(far, left_places, right_places, *refs):
-    left_parts, refs = refs[:len(left_places)], refs[len(left_places):]
-    right_parts, refs = refs[:len(right_places)], refs[len(right_places):]
-    if far:
-        sum_ref, give_ref, keep_ref, left, right, acc, sem_left, sem_right = refs
-    else:
-        out_ref, left, right, acc, sem_left, sem_right = refs
+def whole(parts, lanes):
+    return jnp.concatenate([part[:, lanes] for part in parts]) if len(parts) > 1 else parts[0][:, lanes]
+
+
+def grouped(refs, counts):
+    groups, at = [], 0
+    for count in counts:
+        groups.append(refs[at:at + count])
+        at += count
+    return groups, refs[at:]
+
+
+def place_of(slot, far):
     row, col = lax.axis_index("row"), lax.axis_index("col")
-    z_lo, x, core = row // (X * CORE), (row // CORE) % X, row % CORE
+    z_lo, x = row // (X * CORE), (row // CORE) % X
     y, z_hi = col // Z_HI, col % Z_HI
-    rows, depth = left.shape[1], left.shape[2] // 2
+    block = lax.rem(y + slot, Y) * Z_HI + (1 - z_hi if far else z_hi)
+    return (block // X + z_lo) % Z_LO * X + lax.rem(block % X - x + X, X)
+
+
+def near_kernel(counts, right_places, *refs):
+    left, refs = grouped(refs, counts)
+    right_parts, (sum_ref, stack_ref, acc, sem) = refs[:len(right_places)], refs[len(right_places):]
+    rows, depth = stack_ref.shape[1], stack_ref.shape[2] // 2
     half = rows // 2
     copies = []
-    for i, (slot, at) in enumerate(left_places):
-        part = left_parts[i]
-        copies.append(pltpu.make_async_copy(part, left.at[slot, pl.ds(at, part.shape[0]), :], sem_left.at[i]))
-    at = 0
     for i, (first, *second) in enumerate(right_places):
         part = right_parts[i]
         if second:
             base = half if i == len(right_places) - 1 else 0
             for which, slot in enumerate((first, *second)):
                 copies.append(pltpu.make_async_copy(
-                    part.at[pl.ds(which * half, half), :], right.at[slot, pl.ds(base, half), :], sem_right.at[at]))
-                at += 1
+                    part.at[pl.ds(which * half, half), :], stack_ref.at[slot, pl.ds(base, half), :],
+                    sem.at[len(copies)]))
         else:
-            copies.append(pltpu.make_async_copy(part, right.at[first], sem_right.at[at]))
-            at += 1
+            copies.append(pltpu.make_async_copy(part, stack_ref.at[first], sem.at[len(copies)]))
     for copy in copies:
         copy.start()
     for copy in copies:
         copy.wait()
     for slot in range(Y):
-        block = lax.rem(y + slot, Y) * Z_HI + (1 - z_hi if far else z_hi)
-        plane = (block // X + z_lo) % Z_LO
-        place = plane * X + lax.rem(block % X - x + X, X)
-        both = jnp.concatenate([left[slot][:, :depth], left[slot][:, depth:]])
-        term = jnp.dot(both, right[place], preferred_element_type=jnp.float32)
+        both = jnp.concatenate([whole(left[slot], slice(0, depth)), whole(left[slot], slice(depth, 2 * depth))])
+        term = jnp.dot(both, stack_ref[place_of(slot, False)], preferred_element_type=jnp.float32)
         if slot == 0:
-            acc[...] = term + sum_ref[...] if far else term
-        elif far or slot < Y - 1:
+            acc[...] = term
+        elif slot < Y - 1:
+            acc[...] += term
+        else:
+            sum_ref[...] = acc[...] + term
+
+
+def near_product(left, right):
+    rows, cols = left[0][0].shape
+    counts = [len(group) for group in left]
+    right_places = [tuple(place) for _, *place in right]
+    vmem = pl.BlockSpec(memory_space=pltpu.VMEM)
+    return pl.pallas_call(
+        lambda *refs: near_kernel(counts, right_places, *refs),
+        out_shape=[
+            jax.ShapeDtypeStruct((2 * rows, cols), jnp.float32),
+            jax.ShapeDtypeStruct((Z_LO * X, rows, cols), jnp.bfloat16)],
+        in_specs=[vmem] * sum(counts) + [pl.BlockSpec(memory_space=pl.ANY)] * len(right),
+        out_specs=[vmem] * 2,
+        scratch_shapes=[
+            pltpu.VMEM((2 * rows, cols), jnp.float32),
+            pltpu.SemaphoreType.DMA((len(right) + 2,)),
+        ],
+        compiler_params=pltpu.CompilerParams(vmem_limit_bytes=24 * MIB),
+        cost_estimate=pl.CostEstimate(
+            flops=4 * Y * rows * cols * cols // 2, bytes_accessed=18 * MIB, transcendentals=0),
+        name="near_product",
+    )(*[part for group in left for part in group], *[part for part, *_ in right])
+
+
+def far_kernel(counts, own, *refs):
+    left, (sum_ref, stack_ref, out_ref, acc) = grouped(refs, counts)
+    depth = stack_ref.shape[2] // 2
+    rows = out_ref.shape[0]
+    first = 0 if own else 1
+    lanes = slice(first * depth, (first + 1) * depth)
+    for slot in range(Y):
+        term = jnp.dot(
+            whole(left[slot], lanes), stack_ref[place_of(slot, True)], preferred_element_type=jnp.float32)
+        if slot == 0:
+            acc[...] = term + sum_ref[first * rows:(first + 1) * rows, :]
+        elif slot < Y - 1:
             acc[...] += term
         else:
             out_ref[...] = acc[...] + term
-    if far:
-        give_ref[...] = acc[pl.ds(pl.multiple_of((1 - core) * rows, rows), rows), :]
-        keep_ref[...] = acc[pl.ds(pl.multiple_of(core * rows, rows), rows), :]
-
-
-def partial_product(left, right, earlier=None):
-    far = earlier is not None
+
+
+def far_product(left, total, stack, own):
     rows, cols = left[0][0].shape
-    parts = [part for part, *_ in left] + [part for part, *_ in right] + ([earlier] if far else [])
-    left_places = [tuple(place) for _, *place in left]
-    right_places = [tuple(place) for _, *place in right]
-    whole = jax.ShapeDtypeStruct((2 * rows, cols), jnp.float32)
-    one = jax.ShapeDtypeStruct((rows, cols), jnp.float32)
+    counts = [len(group) for group in left]
     vmem = pl.BlockSpec(memory_space=pltpu.VMEM)
     return pl.pallas_call(
-        lambda *refs: partial_kernel(far, left_places, right_places, *refs),
-        out_shape=[one, one] if far else whole,
-        in_specs=[pl.BlockSpec(memory_space=pl.ANY)] * (len(left) + len(right)) + ([vmem] if far else []),
-        out_specs=[vmem, vmem] if far else vmem,
-        scratch_shapes=[
-            pltpu.VMEM((Y, rows, cols), jnp.bfloat16),
-            pltpu.VMEM((Z_LO * X, rows, cols), jnp.bfloat16),
-            pltpu.VMEM((2 * rows, cols), jnp.float32),
-            pltpu.SemaphoreType.DMA((len(left),)),
-            pltpu.SemaphoreType.DMA((len(right) + 2,)),
-        ],
-        compiler_params=pltpu.CompilerParams(vmem_limit_bytes=26 * MIB),
+        lambda *refs: far_kernel(counts, own, *refs),
+        out_shape=jax.ShapeDtypeStruct((rows, cols), jnp.float32),
+        in_specs=[vmem] * (sum(counts) + 2),
+        out_specs=vmem,
+        scratch_shapes=[pltpu.VMEM((rows, cols), jnp.float32)],
+        compiler_params=pltpu.CompilerParams(vmem_limit_bytes=24 * MIB),
         cost_estimate=pl.CostEstimate(
-            flops=2 * Y * 2 * rows * cols * cols // 2, bytes_accessed=18 * MIB, transcendentals=0),
-        name="partial_product",
-    )(*parts)
+            flops=2 * Y * rows * cols * cols // 2, bytes_accessed=12 * MIB, transcendentals=0),
+        name="far_product",
+    )(*[part for group in left for part in group], total, stack)
 
 
 def encode(block, payload_ref):
@@ -199,7 +241,7 @@
         out_shape=[jax.ShapeDtypeStruct((rows, cols), jnp.float32), payload, payload],
         in_specs=[vmem] * 2,
         out_specs=[vmem] * 3,
-        compiler_params=pltpu.CompilerParams(vmem_limit_bytes=26 * MIB),
+        compiler_params=pltpu.CompilerParams(vmem_limit_bytes=16 * MIB),
         cost_estimate=pl.CostEstimate(flops=4 * rows * cols, bytes_accessed=12 * rows * cols, transcendentals=0),
         name="join",
     )(keep, got)
@@ -229,13 +271,21 @@
 def shards(amplitudes, integrals, occ_energy, vir_energy, pair_occ, pair_vir):
     tile_rows, tile_cols = amplitudes.shape
     core = lax.axis_index("row") % CORE
-    other = send(jnp.roll(amplitudes, tile_cols // 2, axis=1), across_core)
+    other = send(amplitudes, across_core)
     lane = lax.broadcasted_iota(jnp.int32, amplitudes.shape, 1)
-    left = jnp.where((lane < tile_cols // 2) == (core == 0), amplitudes, other)
+    half = tile_cols // 2
+    left = jnp.where(
+        lane < half,
+        jnp.where(core == 0, amplitudes, jnp.roll(amplitudes, half, axis=1)),
+        jnp.where(core == 0, jnp.roll(other, half, axis=1), other))
     near, far, right = gather(left, integrals)
-    give, keep = partial_product(far, right, partial_product(near, right))
-    product, to_same, to_cross = join(keep, send(give, across_core))
-    same, cross = send(to_same, mirrored(0)), send(to_cross, mirrored(1))
+    total, stack = near_product(near, right)
+    give = far_product(far, total, stack, False)
+    got = send(give, across_core)
+    keep = far_product(far, total, stack, True)
+    product, to_same, to_cross = join(keep, got)
+    same = send(to_same, mirrored(0))
+    cross = send(send(to_cross, detour), after_detour)
 
     row_start = lax.axis_index("row") * tile_rows
     col_start = lax.axis_index("col") * tile_cols

time: 151 us -> 132 us (0.87)
  the two profiles are of different devices: /device:TPU:16 before, /device:TPU:25 now
where the time goes in v4:
time: 132 us; the launch traced here: 131 us
  waiting for transfers between devices  77.9 us (59%)
  starting transfers between devices  33 us (25%)
  Pallas kernels  13 us (10%)
  local copies, waits for them, and re-layouts  5.16 us (4%)
  other arithmetic  1.94 us (1%)
    ppermute x21, waiting for transfers between devices, send(): return lax.ppermute(block, AXES, pairs)  77.9 us
    ppermute x21, starting transfers between devices, send(): return lax.ppermute(block, AXES, pairs)  33 us
    pallas_call x1, Pallas kernels, near_product(): pl.pallas_call(lambda *refs: near_kernel(counts, right_places, *refs), ou...  5.37 us
    pallas_call x2, Pallas kernels, far_product(): pl.pallas_call(lambda *refs: far_kernel(counts, own, *refs), out_shape=ja...  4.16 us
  transfers between devices with their start and end apart: 21, of which 10 were waited for; matrix products, arithmetic and copies ran while one was open for 5% of the time, Pallas kernels for 6%

profile of v4, /device:TPU:25, one launch (start us, length us, event | category | flops | bytes accessed | tf_op | source)
XLA Modules:
  0.0 131.3 jit_solution(7702332433986003715)
XLA Ops:
  0.0 0.7 collective-permute-start
  0.7 2.5 %collective-permute-start.11 = (bf16[448,896]{1,0:T(8,128)(2,1)}, bf16[448,896]{1,0:T(8,128)(2,1)S(1)}, u32[]{:S(2)}, u32[]{:S(2)}) collective-permute-start(bf16[448,896]{1,0:T(8,128)(2,1)} %refs_5_.1), channel_id=1, source_target_pairs={{0,48},{1,49},{2,50},{3,51},{4,52},{5,53},{6,54},{7,55},{8,56},{9,... | collective-permute-start | bytes 2408456 | tf_op jit(solution)/shard_map/ppermute | solution.py:29
  3.2 1.6 %collective-permute-start.1 = (bf16[448,896]{1,0:T(8,128)(2,1)}, bf16[448,896]{1,0:T(8,128)(2,1)S(1)}, u32[]{:S(2)}, u32[]{:S(2)}) collective-permute-start(bf16[448,896]{1,0:T(8,128)(2,1)} %refs_5_.1), channel_id=1, source_target_pairs={{0,64},{1,65},{2,66},{3,67},{4,68},{5,69},{6,70},{7,71},{8,72},{9,... | collective-permute-start | bytes 2408456 | tf_op jit(solution)/shard_map/ppermute | solution.py:29
  4.8 1.5 %fusion.2 = (bf16[448,448]{1,0:T(8,128)(2,1)S(1)}, bf16[448,448]{1,0:T(8,128)(2,1)S(1)}) fusion(bf16[448,896]{1,0:T(8,128)(2,1)} %param.6), kind=kLoop, calls=%fused_computation.15 | loop fusion | bytes 1605632 | tf_op jit(solution)/shard_map/jit(_roll_static)/slice | solution.py:279
  6.5 0.8 fusion.refs_0_
  7.3 1.5 %collective-permute-start.5 = (bf16[448,896]{1,0:T(8,128)(2,1)S(1)}, bf16[448,896]{1,0:T(8,128)(2,1)S(1)}, u32[]{:S(2)}, u32[]{:S(2)}) collective-permute-start(bf16[448,896]{1,0:T(8,128)(2,1)S(1)} %fusion.refs_0_), channel_id=1, source_target_pairs={{0,6},{1,7},{2,0},{3,1},{4,2},{5,3},{6,4},{7,5},{8,14},{9,15},{10,... | collective-permute-start | bytes 2408456 | tf_op jit(solution)/shard_map/ppermute | solution.py:29
  8.8 12.0 %collective-permute-done.11.refs_6_ = bf16[448,896]{1,0:T(8,128)(2,1)S(1)} collective-permute-done((bf16[448,896]{1,0:T(8,128)(2,1)}, bf16[448,896]{1,0:T(8,128)(2,1)S(1)}, u32[]{:S(2)}, u32[]{:S(2)}) %collective-permute-start.11) | collective-permute-done | bytes 802848 | tf_op jit(solution)/shard_map/ppermute | solution.py:29
  20.8 3.0 %collective-permute-done.12.refs_7_ = bf16[448,896]{1,0:T(8,128)(2,1)S(1)} collective-permute-done((bf16[448,896]{1,0:T(8,128)(2,1)}, bf16[448,896]{1,0:T(8,128)(2,1)S(1)}, u32[]{:S(2)}, u32[]{:S(2)}) %collective-permute-start.12) | collective-permute-done | bytes 802848 | tf_op jit(solution)/shard_map/ppermute | solution.py:29
  23.8 2.7 %collective-permute-start.13 = (bf16[448,896]{1,0:T(8,128)(2,1)S(1)}, bf16[448,896]{1,0:T(8,128)(2,1)S(1)}, u32[]{:S(2)}, u32[]{:S(2)}) collective-permute-start(bf16[448,896]{1,0:T(8,128)(2,1)S(1)} %collective-permute-done.1.refs_8_), channel_id=1, source_target_pairs={{0,48},{1,49},{2,50},{3,51},{4,52},{5,53},{6,54},{7,55},{8,56},{9,... | collective-permute-start | bytes 2408456 | tf_op jit(solution)/shard_map/ppermute | solution.py:29
  26.5 3.6 %collective-permute-start.2 = (bf16[448,896]{1,0:T(8,128)(2,1)S(1)}, bf16[448,896]{1,0:T(8,128)(2,1)S(1)}, u32[]{:S(2)}, u32[]{:S(2)}) collective-permute-start(bf16[448,896]{1,0:T(8,128)(2,1)S(1)} %fusion.refs_0_), channel_id=1, source_target_pairs={{0,1},{1,0},{2,3},{3,2},{4,5},{5,4},{6,7},{7,6},{8,9},{9,8},{10,11... | collective-permute-start | bytes 2408456 | tf_op jit(solution)/shard_map/ppermute | solution.py:29
  30.2 1.5 %collective-permute-start.6 = (bf16[224,896]{1,0:T(8,128)(2,1)S(1)}, bf16[224,896]{1,0:T(8,128)(2,1)S(1)}, u32[]{:S(2)}, u32[]{:S(2)}) collective-permute-start(bf16[224,896]{1,0:T(8,128)(2,1)S(1)} %slice.53), channel_id=1, source_target_pairs={{0,6},{1,7},{2,0},{3,1},{4,2},{5,3},{6,4},{7,5},{8,14},{9,15},{10,... | collective-permute-start | bytes 1204232 | tf_op jit(solution)/shard_map/ppermute | solution.py:29
  31.8 11.5 %collective-permute-done.14.refs_10_ = bf16[448,896]{1,0:T(8,128)(2,1)S(1)} collective-permute-done((bf16[448,896]{1,0:T(8,128)(2,1)S(1)}, bf16[448,896]{1,0:T(8,128)(2,1)S(1)}, u32[]{:S(2)}, u32[]{:S(2)}) %collective-permute-start.14) | collective-permute-done | bytes 802848 | tf_op jit(solution)/shard_map/ppermute | solution.py:29
  43.6 3.0 %collective-permute-done.2.refs_0_ = bf16[448,896]{1,0:T(8,128)(2,1)S(1)} collective-permute-done((bf16[448,896]{1,0:T(8,128)(2,1)S(1)}, bf16[448,896]{1,0:T(8,128)(2,1)S(1)}, u32[]{:S(2)}, u32[]{:S(2)}) %collective-permute-start.2) | collective-permute-done | bytes 802848 | tf_op jit(solution)/shard_map/ppermute | solution.py:29
  47.1 2.2 %collective-permute-start.8 = (bf16[448,896]{1,0:T(8,128)(2,1)S(1)}, bf16[448,896]{1,0:T(8,128)(2,1)S(1)}, u32[]{:S(2)}, u32[]{:S(2)}) collective-permute-start(bf16[448,896]{1,0:T(8,128)(2,1)S(1)} %collective-permute-done.2.refs_0_), channel_id=1, source_target_pairs={{0,2},{1,3},{2,4},{3,5},{4,6},{5,7},{6,0},{7,1},{8,10},{9,11},{10,... | collective-permute-start | bytes 2408456 | tf_op jit(solution)/shard_map/ppermute | solution.py:29
  49.4 15.5 %collective-permute-done.7.refs_1_ = bf16[448,896]{1,0:T(8,128)(2,1)S(1)} collective-permute-done((bf16[448,896]{1,0:T(8,128)(2,1)S(1)}, bf16[448,896]{1,0:T(8,128)(2,1)S(1)}, u32[]{:S(2)}, u32[]{:S(2)}) %collective-permute-start.7) | collective-permute-done | bytes 802848 | tf_op jit(solution)/shard_map/ppermute | solution.py:29
  65.1 2.9 %collective-permute-start.9 = (bf16[224,896]{1,0:T(8,128)(2,1)S(1)}, bf16[224,896]{1,0:T(8,128)(2,1)S(1)}, u32[]{:S(2)}, u32[]{:S(2)}) collective-permute-start(bf16[224,896]{1,0:T(8,128)(2,1)S(1)} %slice.54), channel_id=1, source_target_pairs={{0,2},{1,3},{2,4},{3,5},{4,6},{5,7},{6,0},{7,1},{8,10},{9,11},{10,... | collective-permute-start | bytes 1204232 | tf_op jit(solution)/shard_map/ppermute | solution.py:29
  68.0 5.4 %near_product.1 = (f32[896,896]{1,0:T(8,128)S(1)}, bf16[8,448,896]{2,1,0:T(8,128)(2,1)S(1)}) custom-call(bf16[448,896]{1,0:T(8,128)(2,1)S(1)} %fusion.refs_0_, bf16[448,896]{1,0:T(8,128)(2,1)S(1)} %collective-permute-done.5.refs_1_, bf16[224,896]{1,0:T(8,128)(2,1)S(1)} %collective-permute-done.4.refs_2_, ...), custom_call_target="tpu_custom_call" | custom-call | flops 2877292544 | bytes 18874368 | tf_op jit(solution)/shard_map/near_product/pallas_call | solution.py:157
  73.8 2.1 %far_product.3 = f32[448,896]{1,0:T(8,128)S(1)} custom-call(bf16[448,896]{1,0:T(8,128)(2,1)S(1)} %collective-permute-done.2.refs_0_, bf16[448,896]{1,0:T(8,128)(2,1)S(1)} %collective-permute-done.7.refs_1_, bf16[224,896]{1,0:T(8,128)(2,1)S(1)} %collective-permute-done.9.refs_2_, bf16[224,896]{1,0:T(8,128)(2,1)S(1)} %collective-permute-done.10.refs_3_, ...), custom_call_target="tpu_custom_call" | custom-call | flops 1438646272 | bytes 12582912 | tf_op jit(solution)/shard_map/far_product/pallas_call | solution.py:196
  75.9 4.2 %collective-permute-start.17 = (f32[448,896]{1,0:T(8,128)S(1)}, f32[448,896]{1,0:T(8,128)S(1)}, u32[]{:S(2)}, u32[]{:S(2)}) collective-permute-start(f32[448,896]{1,0:T(8,128)S(1)} %far_product.3), channel_id=1, source_target_pairs={{0,8},{1,9},{2,10},{3,11},{4,12},{5,13},{6,14},{7,15},{8,0},{9,1},... | collective-permute-start | bytes 4816904 | tf_op jit(solution)/shard_map/ppermute | solution.py:29
  80.1 2.1 %far_product.2.keep_ref = f32[448,896]{1,0:T(8,128)S(1)} custom-call(bf16[448,896]{1,0:T(8,128)(2,1)S(1)} %collective-permute-done.2.refs_0_, bf16[448,896]{1,0:T(8,128)(2,1)S(1)} %collective-permute-done.7.refs_1_, bf16[224,896]{1,0:T(8,128)(2,1)S(1)} %collective-permute-done.9.refs_2_, bf16[224,896]{1,0:T(8,128)(2,1)S(1)} %collective-permute-done.10.refs_3_, ...), custom_call_target="tpu_custom_call" | custom-call | flops 1438646272 | bytes 12582912 | tf_op jit(solution)/shard_map/far_product/pallas_call | solution.py:196
  82.2 1.0 collective-permute-done.17.got_ref
  83.2 0.9 join.1
  84.1 1.9 %collective-permute-start.19 = (s16[240,896]{1,0:T(8,128)(2,1)S(1)}, s16[240,896]{1,0:T(8,128)(2,1)}, u32[]{:S(2)}, u32[]{:S(2)}) collective-permute-start(s16[240,896]{1,0:T(8,128)(2,1)S(1)} %get-tuple-element.20), channel_id=1, source_target_pairs={{0,0},{1,80},{2,18},{3,66},{4,4},{5,84},{6,22},{7,70},{8,8},{9,88}... | collective-permute-start | bytes 1290248 | tf_op jit(solution)/shard_map/ppermute | solution.py:29
  86.1 0.8 dynamic_slice.13
  86.9 0.8 dynamic_slice.12
  87.6 0.8 dynamic_slice.15
  88.4 0.8 dynamic_slice.14
  89.5 6.8 %collective-permute-start.18 = (s16[240,896]{1,0:T(8,128)(2,1)S(1)}, s16[240,896]{1,0:T(8,128)(2,1)S(1)}, u32[]{:S(2)}, u32[]{:S(2)}) collective-permute-start(s16[240,896]{1,0:T(8,128)(2,1)S(1)} %get-tuple-element.19), channel_id=1, source_target_pairs={{0,0},{1,16},{2,32},{3,48},{4,64},{5,80},{6,96},{7,112},{8,8},{9,2... | collective-permute-start | bytes 1290248 | tf_op jit(solution)/shard_map/ppermute | solution.py:29
  96.3 2.2 %collective-permute-done.19 = s16[240,896]{1,0:T(8,128)(2,1)} collective-permute-done((s16[240,896]{1,0:T(8,128)(2,1)S(1)}, s16[240,896]{1,0:T(8,128)(2,1)}, u32[]{:S(2)}, u32[]{:S(2)}) %collective-permute-start.19) | collective-permute-done | bytes 430112 | tf_op jit(solution)/shard_map/ppermute | solution.py:29
  99.4 12.9 %collective-permute-done.18.same_ref = s16[240,896]{1,0:T(8,128)(2,1)S(1)} collective-permute-done((s16[240,896]{1,0:T(8,128)(2,1)S(1)}, s16[240,896]{1,0:T(8,128)(2,1)S(1)}, u32[]{:S(2)}, u32[]{:S(2)}) %collective-permute-start.18) | collective-permute-done | bytes 430112 | tf_op jit(solution)/shard_map/ppermute | solution.py:29
  112.4 16.4 %collective-permute-done.20.cross_ref = s16[240,896]{1,0:T(8,128)(2,1)S(1)} collective-permute-done((s16[240,896]{1,0:T(8,128)(2,1)}, s16[240,896]{1,0:T(8,128)(2,1)S(1)}, u32[]{:S(2)}, u32[]{:S(2)}) %collective-permute-start.20) | collective-permute-done | bytes 430112 | tf_op jit(solution)/shard_map/ppermute | solution.py:29
  128.8 2.5 %combine.1 = f32[448,896]{1,0:T(8,128)} custom-call(f32[448,896]{1,0:T(8,128)S(1)} %get-tuple-element.18.product_ref, s16[240,896]{1,0:T(8,128)(2,1)S(1)} %collective-permute-done.18.same_ref, s16[240,896]{1,0:T(8,128)(2,1)S(1)} %collective-permute-done.20.cross_ref, f32[448,1]{1,0:T(8,128)S(1)} %copy.8.row_gap_ref, f32[1,896]{1,0:T(1,128)S(1)} %sub.29.col_gap_ref), custom_call_target="tpu_custom_call" | custom-call | flops 1605632 | bytes 4816896 | tf_op jit(solution)/shard_map/combine/pallas_call | solution.py:260
  (54 shorter events, 3.1 us)
Async XLA Ops:
  0.0 6.3 %collective-permute-start = (bf16[448,896]{1,0:T(8,128)(2,1)}, bf16[448,896]{1,0:T(8,128)(2,1)S(1)}, u32[]{:S(2)}, u32[]{:S(2)}) collective-permute-start(bf16[448,896]{1,0:T(8,128)(2,1)} %param.6), channel_id=1, source_target_pairs={{0,8},{1,9},{2,10},{3,11},{4,12},{5,13},{6,14},{7,15},{8,0},{9,1},... | collective-permute-start | bytes 2408456 | tf_op jit(solution)/shard_map/ppermute | solution.py:29
  0.7 20.1 %collective-permute-start.11 = (bf16[448,896]{1,0:T(8,128)(2,1)}, bf16[448,896]{1,0:T(8,128)(2,1)S(1)}, u32[]{:S(2)}, u32[]{:S(2)}) collective-permute-start(bf16[448,896]{1,0:T(8,128)(2,1)} %refs_5_.1), channel_id=1, source_target_pairs={{0,48},{1,49},{2,50},{3,51},{4,52},{5,53},{6,54},{7,55},{8,56},{9,... | collective-permute-start | bytes 2408456 | tf_op jit(solution)/shard_map/ppermute | solution.py:29
  3.2 20.6 %collective-permute-start.12 = (bf16[448,896]{1,0:T(8,128)(2,1)}, bf16[448,896]{1,0:T(8,128)(2,1)S(1)}, u32[]{:S(2)}, u32[]{:S(2)}) collective-permute-start(bf16[448,896]{1,0:T(8,128)(2,1)} %refs_5_.1), channel_id=1, source_target_pairs={{0,16},{1,17},{2,18},{3,19},{4,20},{5,21},{6,22},{7,23},{8,24},{9,... | collective-permute-start | bytes 2408456 | tf_op jit(solution)/shard_map/ppermute | solution.py:29
  3.2 20.6 %collective-permute-start.1 = (bf16[448,896]{1,0:T(8,128)(2,1)}, bf16[448,896]{1,0:T(8,128)(2,1)S(1)}, u32[]{:S(2)}, u32[]{:S(2)}) collective-permute-start(bf16[448,896]{1,0:T(8,128)(2,1)} %refs_5_.1), channel_id=1, source_target_pairs={{0,64},{1,65},{2,66},{3,67},{4,68},{5,69},{6,70},{7,71},{8,72},{9,... | collective-permute-start | bytes 2408456 | tf_op jit(solution)/shard_map/ppermute | solution.py:29
  4.8 1.7 %copy-start.3 = (bf16[448,896]{1,0:T(8,128)(2,1)S(1)}, bf16[448,896]{1,0:T(8,128)(2,1)}, u32[]{:S(2)}) copy-start(bf16[448,896]{1,0:T(8,128)(2,1)} %param.6) | copy-start | bytes 2408452
  7.3 22.8 %collective-permute-start.3 = (bf16[448,896]{1,0:T(8,128)(2,1)S(1)}, bf16[448,896]{1,0:T(8,128)(2,1)S(1)}, u32[]{:S(2)}, u32[]{:S(2)}) collective-permute-start(bf16[448,896]{1,0:T(8,128)(2,1)S(1)} %fusion.refs_0_), channel_id=1, source_target_pairs={{0,2},{1,3},{2,4},{3,5},{4,6},{5,7},{6,0},{7,1},{8,10},{9,11},{10,... | collective-permute-start | bytes 2408456 | tf_op jit(solution)/shard_map/ppermute | solution.py:29
  7.3 22.8 %collective-permute-start.5 = (bf16[448,896]{1,0:T(8,128)(2,1)S(1)}, bf16[448,896]{1,0:T(8,128)(2,1)S(1)}, u32[]{:S(2)}, u32[]{:S(2)}) collective-permute-start(bf16[448,896]{1,0:T(8,128)(2,1)S(1)} %fusion.refs_0_), channel_id=1, source_target_pairs={{0,6},{1,7},{2,0},{3,1},{4,2},{5,3},{6,4},{7,5},{8,14},{9,15},{10,... | collective-permute-start | bytes 2408456 | tf_op jit(solution)/shard_map/ppermute | solution.py:29
  20.8 11.0 %copy-start = (bf16[448,896]{1,0:T(8,128)(2,1)}, bf16[448,896]{1,0:T(8,128)(2,1)S(1)}, u32[]{:S(2)}) copy-start(bf16[448,896]{1,0:T(8,128)(2,1)S(1)} %collective-permute-done.11.refs_6_) | copy-start | bytes 2408452
  23.8 19.5 %collective-permute-start.14 = (bf16[448,896]{1,0:T(8,128)(2,1)S(1)}, bf16[448,896]{1,0:T(8,128)(2,1)S(1)}, u32[]{:S(2)}, u32[]{:S(2)}) collective-permute-start(bf16[448,896]{1,0:T(8,128)(2,1)S(1)} %collective-permute-done.1.refs_8_), channel_id=1, source_target_pairs={{0,16},{1,17},{2,18},{3,19},{4,20},{5,21},{6,22},{7,23},{8,24},{9,... | collective-permute-start | bytes 2408456 | tf_op jit(solution)/shard_map/ppermute | solution.py:29
  23.8 19.7 %collective-permute-start.13 = (bf16[448,896]{1,0:T(8,128)(2,1)S(1)}, bf16[448,896]{1,0:T(8,128)(2,1)S(1)}, u32[]{:S(2)}, u32[]{:S(2)}) collective-permute-start(bf16[448,896]{1,0:T(8,128)(2,1)S(1)} %collective-permute-done.1.refs_8_), channel_id=1, source_target_pairs={{0,48},{1,49},{2,50},{3,51},{4,52},{5,53},{6,54},{7,55},{8,56},{9,... | collective-permute-start | bytes 2408456 | tf_op jit(solution)/shard_map/ppermute | solution.py:29
  26.5 20.1 %collective-permute-start.2 = (bf16[448,896]{1,0:T(8,128)(2,1)S(1)}, bf16[448,896]{1,0:T(8,128)(2,1)S(1)}, u32[]{:S(2)}, u32[]{:S(2)}) collective-permute-start(bf16[448,896]{1,0:T(8,128)(2,1)S(1)} %fusion.refs_0_), channel_id=1, source_target_pairs={{0,1},{1,0},{2,3},{3,2},{4,5},{5,4},{6,7},{7,6},{8,9},{9,8},{10,11... | collective-permute-start | bytes 2408456 | tf_op jit(solution)/shard_map/ppermute | solution.py:29
  30.1 16.5 %collective-permute-start.4 = (bf16[224,896]{1,0:T(8,128)(2,1)S(1)}, bf16[224,896]{1,0:T(8,128)(2,1)S(1)}, u32[]{:S(2)}, u32[]{:S(2)}) collective-permute-start(bf16[224,896]{1,0:T(8,128)(2,1)S(1)} %slice.52), channel_id=1, source_target_pairs={{0,2},{1,3},{2,4},{3,5},{4,6},{5,7},{6,0},{7,1},{8,10},{9,11},{10,... | collective-permute-start | bytes 1204232 | tf_op jit(solution)/shard_map/ppermute | solution.py:29
  30.2 16.4 %collective-permute-start.6 = (bf16[224,896]{1,0:T(8,128)(2,1)S(1)}, bf16[224,896]{1,0:T(8,128)(2,1)S(1)}, u32[]{:S(2)}, u32[]{:S(2)}) collective-permute-start(bf16[224,896]{1,0:T(8,128)(2,1)S(1)} %slice.53), channel_id=1, source_target_pairs={{0,6},{1,7},{2,0},{3,1},{4,2},{5,3},{6,4},{7,5},{8,14},{9,15},{10,... | collective-permute-start | bytes 1204232 | tf_op jit(solution)/shard_map/ppermute | solution.py:29
  43.3 6.0 %slice-start = ((bf16[448,896]{1,0:T(8,128)(2,1)}), bf16[224,896]{1,0:T(8,128)(2,1)S(1)}, s32[]{:S(2)}) async-start(bf16[448,896]{1,0:T(8,128)(2,1)} %copy-done), calls=%async_computation | async-start | bytes 802816 | tf_op jit(solution)/shard_map/slice | solution.py:86
  43.4 24.6 %collective-permute-start.15 = (bf16[448,896]{1,0:T(8,128)(2,1)S(1)}, bf16[448,896]{1,0:T(8,128)(2,1)S(1)}, u32[]{:S(2)}, u32[]{:S(2)}) collective-permute-start(bf16[448,896]{1,0:T(8,128)(2,1)S(1)} %pad_maximum_fusion), channel_id=1, source_target_pairs={{0,16},{1,17},{2,18},{3,19},{4,20},{5,21},{6,22},{7,23},{8,24},{9,... | collective-permute-start | bytes 2408456 | tf_op jit(solution)/shard_map/ppermute | solution.py:29
  43.5 24.5 %copy-start.1 = (bf16[448,896]{1,0:T(8,128)(2,1)S(1)}, bf16[448,896]{1,0:T(8,128)(2,1)}, u32[]{:S(2)}) copy-start(bf16[448,896]{1,0:T(8,128)(2,1)} %copy-done) | copy-start | bytes 2408452
  43.5 24.4 %copy-start.2 = (bf16[448,896]{1,0:T(8,128)(2,1)S(1)}, bf16[448,896]{1,0:T(8,128)(2,1)}, u32[]{:S(2)}) copy-start(bf16[448,896]{1,0:T(8,128)(2,1)} %refs_5_.1) | copy-start | bytes 2408452
  46.6 18.3 %collective-permute-start.7 = (bf16[448,896]{1,0:T(8,128)(2,1)S(1)}, bf16[448,896]{1,0:T(8,128)(2,1)S(1)}, u32[]{:S(2)}, u32[]{:S(2)}) collective-permute-start(bf16[448,896]{1,0:T(8,128)(2,1)S(1)} %collective-permute-done.2.refs_0_), channel_id=1, source_target_pairs={{0,6},{1,7},{2,0},{3,1},{4,2},{5,3},{6,4},{7,5},{8,14},{9,15},{10,... | collective-permute-start | bytes 2408456 | tf_op jit(solution)/shard_map/ppermute | solution.py:29
  47.1 18.0 %collective-permute-start.8 = (bf16[448,896]{1,0:T(8,128)(2,1)S(1)}, bf16[448,896]{1,0:T(8,128)(2,1)S(1)}, u32[]{:S(2)}, u32[]{:S(2)}) collective-permute-start(bf16[448,896]{1,0:T(8,128)(2,1)S(1)} %collective-permute-done.2.refs_0_), channel_id=1, source_target_pairs={{0,2},{1,3},{2,4},{3,5},{4,6},{5,7},{6,0},{7,1},{8,10},{9,11},{10,... | collective-permute-start | bytes 2408456 | tf_op jit(solution)/shard_map/ppermute | solution.py:29
  49.4 18.6 %collective-permute-start.16 = (bf16[448,896]{1,0:T(8,128)(2,1)S(1)}, bf16[448,896]{1,0:T(8,128)(2,1)S(1)}, u32[]{:S(2)}, u32[]{:S(2)}) collective-permute-start(bf16[448,896]{1,0:T(8,128)(2,1)S(1)} %pad_maximum_fusion.1), channel_id=1, source_target_pairs={{0,48},{1,49},{2,50},{3,51},{4,52},{5,53},{6,54},{7,55},{8,56},{9,... | collective-permute-start | bytes 2408456 | tf_op jit(solution)/shard_map/ppermute | solution.py:29
  64.9 8.8 %collective-permute-start.10 = (bf16[224,896]{1,0:T(8,128)(2,1)S(1)}, bf16[224,896]{1,0:T(8,128)(2,1)S(1)}, u32[]{:S(2)}, u32[]{:S(2)}) collective-permute-start(bf16[224,896]{1,0:T(8,128)(2,1)S(1)} %slice.55), channel_id=1, source_target_pairs={{0,6},{1,7},{2,0},{3,1},{4,2},{5,3},{6,4},{7,5},{8,14},{9,15},{10,... | collective-permute-start | bytes 1204232 | tf_op jit(solution)/shard_map/ppermute | solution.py:29
  65.1 8.7 %collective-permute-start.9 = (bf16[224,896]{1,0:T(8,128)(2,1)S(1)}, bf16[224,896]{1,0:T(8,128)(2,1)S(1)}, u32[]{:S(2)}, u32[]{:S(2)}) collective-permute-start(bf16[224,896]{1,0:T(8,128)(2,1)S(1)} %slice.54), channel_id=1, source_target_pairs={{0,2},{1,3},{2,4},{3,5},{4,6},{5,7},{6,0},{7,1},{8,10},{9,11},{10,... | collective-permute-start | bytes 1204232 | tf_op jit(solution)/shard_map/ppermute | solution.py:29
  75.9 7.3 %collective-permute-start.17 = (f32[448,896]{1,0:T(8,128)S(1)}, f32[448,896]{1,0:T(8,128)S(1)}, u32[]{:S(2)}, u32[]{:S(2)}) collective-permute-start(f32[448,896]{1,0:T(8,128)S(1)} %far_product.3), channel_id=1, source_target_pairs={{0,8},{1,9},{2,10},{3,11},{4,12},{5,13},{6,14},{7,15},{8,0},{9,1},... | collective-permute-start | bytes 4816904 | tf_op jit(solution)/shard_map/ppermute | solution.py:29
  82.2 7.0 %copy-start.4 = (f32[1000]{0:T(1024)S(1)}, f32[1000]{0:T(1024)}, u32[]{:S(2)}) copy-start(f32[1000]{0:T(1024)} %param.9) | copy-start | bytes 12004
  82.2 16.4 %copy-start.5 = (f32[80]{0:T(128)S(1)}, f32[80]{0:T(128)}, u32[]{:S(2)}) copy-start(f32[80]{0:T(128)} %param.8) | copy-start | bytes 964
  84.1 14.3 %collective-permute-start.19 = (s16[240,896]{1,0:T(8,128)(2,1)S(1)}, s16[240,896]{1,0:T(8,128)(2,1)}, u32[]{:S(2)}, u32[]{:S(2)}) collective-permute-start(s16[240,896]{1,0:T(8,128)(2,1)S(1)} %get-tuple-element.20), channel_id=1, source_target_pairs={{0,0},{1,80},{2,18},{3,66},{4,4},{5,84},{6,22},{7,70},{8,8},{9,88}... | collective-permute-start | bytes 1290248 | tf_op jit(solution)/shard_map/ppermute | solution.py:29
  89.5 22.9 %collective-permute-start.18 = (s16[240,896]{1,0:T(8,128)(2,1)S(1)}, s16[240,896]{1,0:T(8,128)(2,1)S(1)}, u32[]{:S(2)}, u32[]{:S(2)}) collective-permute-start(s16[240,896]{1,0:T(8,128)(2,1)S(1)} %get-tuple-element.19), channel_id=1, source_target_pairs={{0,0},{1,16},{2,32},{3,48},{4,64},{5,80},{6,96},{7,112},{8,8},{9,2... | collective-permute-start | bytes 1290248 | tf_op jit(solution)/shard_map/ppermute | solution.py:29
  98.5 30.3 %collective-permute-start.20 = (s16[240,896]{1,0:T(8,128)(2,1)}, s16[240,896]{1,0:T(8,128)(2,1)S(1)}, u32[]{:S(2)}, u32[]{:S(2)}) collective-permute-start(s16[240,896]{1,0:T(8,128)(2,1)} %collective-permute-done.19), channel_id=1, source_target_pairs={{0,8},{1,13},{2,60},{3,57},{4,72},{5,77},{6,124},{7,121},{8,0},{9,... | collective-permute-start | bytes 1290248 | tf_op jit(solution)/shard_map/ppermute | solution.py:29

commit v5 on v4

--- a/solution.py
+++ b/solution.py
@@ -71,25 +71,31 @@
     return lax.optimization_barrier((block, *earlier))[0]
 
 
-def gather(left, right):
+def gather(left, right, other):
     half = left.shape[0] // 2
     right_z = send(right, across_z_lo)
-    right_up, right_down = send(right, along_x(1)), send(right, along_x(-1))
+    late = after(right, other)
+    right_up, right_down = send(late, along_x(1)), send(late, along_x(-1))
     left_up, left_down = send(left, along_y(1)), send(left, along_y(-1))
     left_z = send(after(left, right_z), across_z_hi)
-    right_z = after(right_z, right_up, right_down)
-    right_z_up, right_z_down = send(right_z, along_x(1)), send(right_z, along_x(-1))
-    left_top, left_bottom = send(left_up[:half], along_y(1)), send(left_down[half:], along_y(-1))
-    left_z = after(left_z, left_top, left_bottom)
+    right_up, right_down, right_z = lax.optimization_barrier((right_up, right_down, right_z))
+    right_two = send(right_up, along_x(1))
+    right_z_down = send(right_z, along_x(-1))
+    right_z_up = send(after(right_z, right_two), along_x(1))
+    right_z_two = send(right_z_down, along_x(-1))
+    left_two = jnp.concatenate([send(left_up[:half], along_y(1)), send(left_down[half:], along_y(-1))])
+    left_z, left_two = lax.optimization_barrier((left_z, left_two))
     left_z_up, left_z_down = send(left_z, along_y(1)), send(left_z, along_y(-1))
-    right_top = send(jnp.concatenate([right_up[:half], right_z_up[:half]]), along_x(1))
-    right_bottom = send(jnp.concatenate([right_down[half:], right_z_down[half:]]), along_x(-1))
-    left_z_top, left_z_bottom = send(left_z_up[:half], along_y(1)), send(left_z_down[half:], along_y(-1))
-    near = [(left,), (left_down,), (left_top, left_bottom), (left_up,)]
-    far = [(left_z,), (left_z_down,), (left_z_top, left_z_bottom), (left_z_up,)]
-    return near, far, [
-        (right, 0), (right_down, 1), (right_up, 3), (right_z, 4), (right_z_down, 5), (right_z_up, 7),
-        (right_top, 2, 6), (right_bottom, 2, 6)]
+    left_z_two = send(left_two, across_z_hi)
+    near = [left, left_down, left_two, left_up]
+    far = [left_z, left_z_down, left_z_two, left_z_up]
+    return near, far, [right, right_down, right_two, right_up, right_z, right_z_down], [right_z_two, right_z_up]
+
+
+def block_of(values, index, count):
+    table = values.reshape(count, -1)
+    rows = lax.broadcasted_iota(jnp.int32, table.shape, 0)
+    return jnp.sum(jnp.where(rows == index, table, 0), axis=0)
 
 
 def lookup(energies, orbital_index):
@@ -98,16 +104,30 @@
     return jnp.sum(picked, axis=1)
 
 
-def whole(parts, lanes):
-    return jnp.concatenate([part[:, lanes] for part in parts]) if len(parts) > 1 else parts[0][:, lanes]
-
-
-def grouped(refs, counts):
-    groups, at = [], 0
-    for count in counts:
-        groups.append(refs[at:at + count])
-        at += count
-    return groups, refs[at:]
+LATE = 2
+
+
+def stack_kernel(*refs):
+    *parts, stack_ref, sem = refs
+    copies = [pltpu.make_async_copy(part, stack_ref.at[i], sem.at[i]) for i, part in enumerate(parts)]
+    for copy in copies:
+        copy.start()
+    for copy in copies:
+        copy.wait()
+
+
+def stacked(parts):
+    rows, cols = parts[0].shape
+    return pl.pallas_call(
+        stack_kernel,
+        out_shape=jax.ShapeDtypeStruct((len(parts) + LATE, rows, cols), jnp.bfloat16),
+        in_specs=[pl.BlockSpec(memory_space=pl.ANY)] * len(parts),
+        out_specs=pl.BlockSpec(memory_space=pltpu.VMEM),
+        scratch_shapes=[pltpu.SemaphoreType.DMA((len(parts),))],
+        compiler_params=pltpu.CompilerParams(vmem_limit_bytes=4 * MIB),
+        cost_estimate=pl.CostEstimate(flops=0, bytes_accessed=4 * MIB, transcendentals=0),
+        name="stacked",
+    )(*parts)
 
 
 def place_of(slot, far):
@@ -118,28 +138,17 @@
     return (block // X + z_lo) % Z_LO * X + lax.rem(block % X - x + X, X)
 
 
-def near_kernel(counts, right_places, *refs):
-    left, refs = grouped(refs, counts)
-    right_parts, (sum_ref, stack_ref, acc, sem) = refs[:len(right_places)], refs[len(right_places):]
-    rows, depth = stack_ref.shape[1], stack_ref.shape[2] // 2
-    half = rows // 2
-    copies = []
-    for i, (first, *second) in enumerate(right_places):
-        part = right_parts[i]
-        if second:
-            base = half if i == len(right_places) - 1 else 0
-            for which, slot in enumerate((first, *second)):
-                copies.append(pltpu.make_async_copy(
-                    part.at[pl.ds(which * half, half), :], stack_ref.at[slot, pl.ds(base, half), :],
-                    sem.at[len(copies)]))
-        else:
-            copies.append(pltpu.make_async_copy(part, stack_ref.at[first], sem.at[len(copies)]))
+def near_kernel(*refs):
+    left, late, (_, sum_ref, stack_ref, acc, sem) = refs[:Y], refs[Y:Y + LATE], refs[Y + LATE:]
+    depth = stack_ref.shape[2] // 2
+    first = stack_ref.shape[0] - LATE
+    copies = [pltpu.make_async_copy(part, stack_ref.at[first + i], sem.at[i]) for i, part in enumerate(late)]
     for copy in copies:
         copy.start()
     for copy in copies:
         copy.wait()
     for slot in range(Y):
-        both = jnp.concatenate([whole(left[slot], slice(0, depth)), whole(left[slot], slice(depth, 2 * depth))])
+        both = jnp.concatenate([left[slot][:, :depth], left[slot][:, depth:]])
         term = jnp.dot(both, stack_ref[place_of(slot, False)], preferred_element_type=jnp.float32)
         if slot == 0:
             acc[...] = term
@@ -149,38 +158,37 @@
             sum_ref[...] = acc[...] + term
 
 
-def near_product(left, right):
-    rows, cols = left[0][0].shape
-    counts = [len(group) for group in left]
-    right_places = [tuple(place) for _, *place in right]
+def near_product(left, right, stack):
+    rows, cols = left[0].shape
     vmem = pl.BlockSpec(memory_space=pltpu.VMEM)
     return pl.pallas_call(
-        lambda *refs: near_kernel(counts, right_places, *refs),
+        near_kernel,
         out_shape=[
             jax.ShapeDtypeStruct((2 * rows, cols), jnp.float32),
-            jax.ShapeDtypeStruct((Z_LO * X, rows, cols), jnp.bfloat16)],
-        in_specs=[vmem] * sum(counts) + [pl.BlockSpec(memory_space=pl.ANY)] * len(right),
+            jax.ShapeDtypeStruct(stack.shape, stack.dtype)],
+        in_specs=[vmem] * Y + [pl.BlockSpec(memory_space=pl.ANY)] * LATE + [vmem],
         out_specs=[vmem] * 2,
         scratch_shapes=[
             pltpu.VMEM((2 * rows, cols), jnp.float32),
-            pltpu.SemaphoreType.DMA((len(right) + 2,)),
+            pltpu.SemaphoreType.DMA((LATE,)),
         ],
-        compiler_params=pltpu.CompilerParams(vmem_limit_bytes=24 * MIB),
+        input_output_aliases={Y + LATE: 1},
+        compiler_params=pltpu.CompilerParams(vmem_limit_bytes=10 * MIB),
         cost_estimate=pl.CostEstimate(
-            flops=4 * Y * rows * cols * cols // 2, bytes_accessed=18 * MIB, transcendentals=0),
+            flops=4 * Y * rows * cols * cols // 2, bytes_accessed=12 * MIB, transcendentals=0),
         name="near_product",
-    )(*[part for group in left for part in group], *[part for part, *_ in right])
-
-
-def far_kernel(counts, own, *refs):
-    left, (sum_ref, stack_ref, out_ref, acc) = grouped(refs, counts)
+    )(*left, *right, stack)
+
+
+def far_kernel(own, *refs):
+    left, (sum_ref, stack_ref, out_ref, acc) = refs[:Y], refs[Y:]
     depth = stack_ref.shape[2] // 2
     rows = out_ref.shape[0]
     first = 0 if own else 1
-    lanes = slice(first * depth, (first + 1) * depth)
     for slot in range(Y):
         term = jnp.dot(
-            whole(left[slot], lanes), stack_ref[place_of(slot, True)], preferred_element_type=jnp.float32)
+            left[slot][:, first * depth:(first + 1) * depth], stack_ref[place_of(slot, True)],
+            preferred_element_type=jnp.float32)
         if slot == 0:
             acc[...] = term + sum_ref[first * rows:(first + 1) * rows, :]
         elif slot < Y - 1:
@@ -190,20 +198,19 @@
 
 
 def far_product(left, total, stack, own):
-    rows, cols = left[0][0].shape
-    counts = [len(group) for group in left]
+    rows, cols = left[0].shape
     vmem = pl.BlockSpec(memory_space=pltpu.VMEM)
     return pl.pallas_call(
-        lambda *refs: far_kernel(counts, own, *refs),
+        lambda *refs: far_kernel(own, *refs),
         out_shape=jax.ShapeDtypeStruct((rows, cols), jnp.float32),
-        in_specs=[vmem] * (sum(counts) + 2),
+        in_specs=[vmem] * (Y + 2),
         out_specs=vmem,
         scratch_shapes=[pltpu.VMEM((rows, cols), jnp.float32)],
-        compiler_params=pltpu.CompilerParams(vmem_limit_bytes=24 * MIB),
+        compiler_params=pltpu.CompilerParams(vmem_limit_bytes=6 * MIB),
         cost_estimate=pl.CostEstimate(
             flops=2 * Y * rows * cols * cols // 2, bytes_accessed=12 * MIB, transcendentals=0),
         name="far_product",
-    )(*[part for group in left for part in group], total, stack)
+    )(*left, total, stack)
 
 
 def encode(block, payload_ref):
@@ -241,7 +248,7 @@
         out_shape=[jax.ShapeDtypeStruct((rows, cols), jnp.float32), payload, payload],
         in_specs=[vmem] * 2,
         out_specs=[vmem] * 3,
-        compiler_params=pltpu.CompilerParams(vmem_limit_bytes=16 * MIB),
+        compiler_params=pltpu.CompilerParams(vmem_limit_bytes=6 * MIB),
         cost_estimate=pl.CostEstimate(flops=4 * rows * cols, bytes_accessed=12 * rows * cols, transcendentals=0),
         name="join",
     )(keep, got)
@@ -262,7 +269,7 @@
         out_shape=jax.ShapeDtypeStruct((rows, cols), jnp.float32),
         in_specs=[pl.BlockSpec(memory_space=pltpu.VMEM)] * 5,
         out_specs=pl.BlockSpec(memory_space=pltpu.VMEM),
-        compiler_params=pltpu.CompilerParams(vmem_limit_bytes=26 * MIB),
+        compiler_params=pltpu.CompilerParams(vmem_limit_bytes=8 * MIB),
         cost_estimate=pl.CostEstimate(flops=4 * rows * cols, bytes_accessed=12 * rows * cols, transcendentals=0),
         name="combine",
     )(product, same, cross, row_gap[:, None], col_gap[None, :])
@@ -278,8 +285,17 @@
         lane < half,
         jnp.where(core == 0, amplitudes, jnp.roll(amplitudes, half, axis=1)),
         jnp.where(core == 0, jnp.roll(other, half, axis=1), other))
-    near, far, right = gather(left, integrals)
-    total, stack = near_product(near, right)
+    near, far, early, late = gather(left, integrals, other)
+
+    row_count, col_count = lax.axis_size("row"), lax.axis_size("col")
+    row, col = lax.axis_index("row"), lax.axis_index("col")
+    row_occ, row_vir = block_of(pair_occ, row, row_count), block_of(pair_vir, row, row_count)
+    col_occ, col_vir = block_of(pair_occ, col, col_count), block_of(pair_vir, col, col_count)
+    row_gap = lookup(occ_energy, row_occ) - lookup(vir_energy, row_vir)
+    col_gap = lookup(occ_energy, col_occ) - lookup(vir_energy, col_vir)
+
+    stack, row_gap, col_gap = lax.optimization_barrier((stacked(early), row_gap, col_gap))
+    total, stack = near_product(near, late, stack)
     give = far_product(far, total, stack, False)
     got = send(give, across_core)
     keep = far_product(far, total, stack, True)
@@ -287,14 +303,6 @@
     same = send(to_same, mirrored(0))
     cross = send(send(to_cross, detour), after_detour)
 
-    row_start = lax.axis_index("row") * tile_rows
-    col_start = lax.axis_index("col") * tile_cols
-    row_occ = lax.dynamic_slice_in_dim(pair_occ, row_start, tile_rows)
-    row_vir = lax.dynamic_slice_in_dim(pair_vir, row_start, tile_rows)
-    col_occ = lax.dynamic_slice_in_dim(pair_occ, col_start, tile_cols)
-    col_vir = lax.dynamic_slice_in_dim(pair_vir, col_start, tile_cols)
-    row_gap = lookup(occ_energy, row_occ) - lookup(vir_energy, row_vir)
-    col_gap = lookup(occ_energy, col_occ) - lookup(vir_energy, col_vir)
     return combine(product, same, cross, row_gap, col_gap)
 
 

time: 132 us -> 123 us (0.932)
  waiting for transfers between devices: 77.9 us -> 65.3 us
  Pallas kernels: 13 us -> 15.2 us
    ppermute x21 -> x20, waiting for transfers between devices: 77.9 us -> 65.3 us  [send(): return lax.ppermute(block, AXES, pairs)]
    dynamic_slice x4 -> x0, local copies, waits for them, and re-layouts: 3.09 us -> none  [the longest x1 0.78 us: shards(): row_vir = lax.dynamic_slice_in_dim(pair_vir, row_start, tile_rows)]
    pallas_call x3 -> x4, Pallas kernels: 9.53 us -> 11.8 us  [the longest x1 5.41 us: near_product(): pl.pallas_call(near_kernel, out_shape=[jax.ShapeDtypeStruct((2 * rows, co...]
    ppermute x21 -> x20, starting transfers between devices: 33 us -> 33.2 us  [send(): return lax.ppermute(block, AXES, pairs)]
  transfers between devices with their start and end apart: 21 -> 20, of which waited for: 10 -> 9; matrix products, arithmetic and copies ran while one was open for 5% -> 6% of each run, Pallas kernels for 6% -> 8%
where the time goes in v5:
time: 123 us
  waiting for transfers between devices  65.3 us (53%)
  starting transfers between devices  33.2 us (27%)
  Pallas kernels  15.2 us (12%)
  local copies, waits for them, and re-layouts  5.32 us (4%)
  other arithmetic  3.26 us (3%)
    ppermute x20, waiting for transfers between devices, send(): return lax.ppermute(block, AXES, pairs)  65.3 us
    ppermute x20, starting transfers between devices, send(): return lax.ppermute(block, AXES, pairs)  33.2 us
    pallas_call x1, Pallas kernels, near_product(): pl.pallas_call(near_kernel, out_shape=[jax.ShapeDtypeStruct((2 * rows, co...  5.41 us
    pallas_call x2, Pallas kernels, far_product(): pl.pallas_call(lambda *refs: far_kernel(own, *refs), out_shape=jax.ShapeD...  4.14 us
    pallas_call x1, Pallas kernels, combine(): pl.pallas_call(combine_kernel, out_shape=jax.ShapeDtypeStruct((rows, cols...  2.53 us
  transfers between devices with their start and end apart: 20, of which 9 were waited for; matrix products, arithmetic and copies ran while one was open for 6% of the time, Pallas kernels for 8%

profile of v5, /device:TPU:25, one launch (start us, length us, event | category | flops | bytes accessed | tf_op | source)
XLA Modules:
  0.0 122.6 jit_solution(3795859431191242750)
XLA Ops:
  0.7 1.7 %collective-permute-start.1 = (bf16[448,896]{1,0:T(8,128)(2,1)}, bf16[448,896]{1,0:T(8,128)(2,1)}, u32[]{:S(2)}, u32[]{:S(2)}) collective-permute-start(bf16[448,896]{1,0:T(8,128)(2,1)} %refs_0_.1), channel_id=1, source_target_pairs={{0,64},{1,65},{2,66},{3,67},{4,68},{5,69},{6,70},{7,71},{8,72},{9,... | collective-permute-start | bytes 2408456 | tf_op jit(solution)/shard_map/ppermute | solution.py:29
  2.3 2.3 %fusion.2 = (bf16[448,448]{1,0:T(8,128)(2,1)}, bf16[448,448]{1,0:T(8,128)(2,1)}) fusion(bf16[448,896]{1,0:T(8,128)(2,1)} %param.6), kind=kLoop, calls=%fused_computation.20 | loop fusion | bytes 1605632 | tf_op jit(solution)/shard_map/jit(_roll_static)/slice | solution.py:286
  4.6 1.3 %collective-permute-start.10 = (bf16[448,896]{1,0:T(8,128)(2,1)S(1)}, bf16[448,896]{1,0:T(8,128)(2,1)}, u32[]{:S(2)}, u32[]{:S(2)}) collective-permute-start(bf16[448,896]{1,0:T(8,128)(2,1)S(1)} %copy-done), channel_id=1, source_target_pairs={{0,16},{1,17},{2,18},{3,19},{4,20},{5,21},{6,22},{7,23},{8,24},{9,... | collective-permute-start | bytes 2408456 | tf_op jit(solution)/shard_map/ppermute | solution.py:29
  5.9 1.5 %collective-permute-start.11 = (bf16[448,896]{1,0:T(8,128)(2,1)S(1)}, bf16[448,896]{1,0:T(8,128)(2,1)}, u32[]{:S(2)}, u32[]{:S(2)}) collective-permute-start(bf16[448,896]{1,0:T(8,128)(2,1)S(1)} %copy-done), channel_id=1, source_target_pairs={{0,48},{1,49},{2,50},{3,51},{4,52},{5,53},{6,54},{7,55},{8,56},{9,... | collective-permute-start | bytes 2408456 | tf_op jit(solution)/shard_map/ppermute | solution.py:29
  9.4 1.5 %collective-permute-start.5 = (bf16[448,896]{1,0:T(8,128)(2,1)S(1)}, bf16[448,896]{1,0:T(8,128)(2,1)S(1)}, u32[]{:S(2)}, u32[]{:S(2)}) collective-permute-start(bf16[448,896]{1,0:T(8,128)(2,1)S(1)} %fusion.refs_0_), channel_id=1, source_target_pairs={{0,6},{1,7},{2,0},{3,1},{4,2},{5,3},{6,4},{7,5},{8,14},{9,15},{10,... | collective-permute-start | bytes 2408456 | tf_op jit(solution)/shard_map/ppermute | solution.py:29
  10.9 9.9 %collective-permute-done.1.refs_4_ = bf16[448,896]{1,0:T(8,128)(2,1)} collective-permute-done((bf16[448,896]{1,0:T(8,128)(2,1)}, bf16[448,896]{1,0:T(8,128)(2,1)}, u32[]{:S(2)}, u32[]{:S(2)}) %collective-permute-start.1) | collective-permute-done | bytes 802848 | tf_op jit(solution)/shard_map/ppermute | solution.py:29
  20.8 4.3 %collective-permute-done.10.refs_3_ = bf16[448,896]{1,0:T(8,128)(2,1)} collective-permute-done((bf16[448,896]{1,0:T(8,128)(2,1)S(1)}, bf16[448,896]{1,0:T(8,128)(2,1)}, u32[]{:S(2)}, u32[]{:S(2)}) %collective-permute-start.10) | collective-permute-done | bytes 802848 | tf_op jit(solution)/shard_map/ppermute | solution.py:29
  25.1 0.9 collective-permute-start.14
  26.0 1.8 %collective-permute-start.12 = (bf16[448,896]{1,0:T(8,128)(2,1)}, bf16[448,896]{1,0:T(8,128)(2,1)}, u32[]{:S(2)}, u32[]{:S(2)}) collective-permute-start(bf16[448,896]{1,0:T(8,128)(2,1)} %collective-permute-done.1.refs_4_), channel_id=1, source_target_pairs={{0,48},{1,49},{2,50},{3,51},{4,52},{5,53},{6,54},{7,55},{8,56},{9,... | collective-permute-start | bytes 2408456 | tf_op jit(solution)/shard_map/ppermute | solution.py:29
  27.8 3.3 %collective-permute-start.2 = (bf16[448,896]{1,0:T(8,128)(2,1)S(1)}, bf16[448,896]{1,0:T(8,128)(2,1)S(1)}, u32[]{:S(2)}, u32[]{:S(2)}) collective-permute-start(bf16[448,896]{1,0:T(8,128)(2,1)S(1)} %fusion.refs_0_), channel_id=1, source_target_pairs={{0,1},{1,0},{2,3},{3,2},{4,5},{5,4},{6,7},{7,6},{8,9},{9,8},{10,11... | collective-permute-start | bytes 2408456 | tf_op jit(solution)/shard_map/ppermute | solution.py:29
  32.7 1.5 %collective-permute-start.6 = (bf16[224,896]{1,0:T(8,128)(2,1)}, bf16[224,896]{1,0:T(8,128)(2,1)}, u32[]{:S(2)}, u32[]{:S(2)}) collective-permute-start(bf16[224,896]{1,0:T(8,128)(2,1)} %slice.29), channel_id=1, source_target_pairs={{0,6},{1,7},{2,0},{3,1},{4,2},{5,3},{6,4},{7,5},{8,14},{9,15},{10,... | collective-permute-start | bytes 1204232 | tf_op jit(solution)/shard_map/ppermute | solution.py:29
  34.4 10.4 %collective-permute-done.14.refs_2_ = bf16[448,896]{1,0:T(8,128)(2,1)} collective-permute-done((bf16[448,896]{1,0:T(8,128)(2,1)}, bf16[448,896]{1,0:T(8,128)(2,1)}, u32[]{:S(2)}, u32[]{:S(2)}) %collective-permute-start.14) | collective-permute-done | bytes 802848 | tf_op jit(solution)/shard_map/ppermute | solution.py:29
  44.9 2.7 %collective-permute-start.13 = (bf16[448,896]{1,0:T(8,128)(2,1)}, bf16[448,896]{1,0:T(8,128)(2,1)}, u32[]{:S(2)}, u32[]{:S(2)}) collective-permute-start(bf16[448,896]{1,0:T(8,128)(2,1)} %collective-permute-done.12.refs_5_), channel_id=1, source_target_pairs={{0,48},{1,49},{2,50},{3,51},{4,52},{5,53},{6,54},{7,55},{8,56},{9,... | collective-permute-start | bytes 2408456 | tf_op jit(solution)/shard_map/ppermute | solution.py:29
  48.1 1.3 %pad_maximum_fusion.refs_2_ = bf16[448,896]{1,0:T(8,128)(2,1)S(1)} fusion(bf16[224,896]{1,0:T(8,128)(2,1)} %collective-permute-done.6, bf16[224,896]{1,0:T(8,128)(2,1)} %collective-permute-done.4), kind=kLoop, calls=%fused_computation.7 | loop fusion | flops 1605632 | bytes 1605632 | tf_op jit(solution)/shard_map/concatenate | solution.py:86
  49.9 2.2 %collective-permute-start.9 = (bf16[448,896]{1,0:T(8,128)(2,1)S(1)}, bf16[448,896]{1,0:T(8,128)(2,1)S(1)}, u32[]{:S(2)}, u32[]{:S(2)}) collective-permute-start(bf16[448,896]{1,0:T(8,128)(2,1)S(1)} %collective-permute-done.2.refs_0_), channel_id=1, source_target_pairs={{0,2},{1,3},{2,4},{3,5},{4,6},{5,7},{6,0},{7,1},{8,10},{9,11},{10,... | collective-permute-start | bytes 2408456 | tf_op jit(solution)/shard_map/ppermute | solution.py:29
  52.1 3.3 %collective-permute-start.8 = (bf16[448,896]{1,0:T(8,128)(2,1)S(1)}, bf16[448,896]{1,0:T(8,128)(2,1)S(1)}, u32[]{:S(2)}, u32[]{:S(2)}) collective-permute-start(bf16[448,896]{1,0:T(8,128)(2,1)S(1)} %pad_maximum_fusion.refs_2_), channel_id=1, source_target_pairs={{0,1},{1,0},{2,3},{3,2},{4,5},{5,4},{6,7},{7,6},{8,9},{9,8},{10,11... | collective-permute-start | bytes 2408456 | tf_op jit(solution)/shard_map/ppermute | solution.py:29
  56.1 2.2 %stacked.1.refs_6_ = bf16[8,448,896]{2,1,0:T(8,128)(2,1)S(1)} custom-call(bf16[448,896]{1,0:T(8,128)(2,1)S(1)} %copy-done.1, bf16[448,896]{1,0:T(8,128)(2,1)} %collective-permute-done.11.refs_1_, bf16[448,896]{1,0:T(8,128)(2,1)} %collective-permute-done.14.refs_2_, bf16[448,896]{1,0:T(8,128)(2,1)} %collective-permute-done.10.refs_3_, ...), custom_call_target="tpu_custom_call" | custom-call | bytes 4194304 | tf_op jit(solution)/shard_map/stacked/pallas_call | solution.py:121
  58.3 5.3 %collective-permute-done.15.refs_5_ = bf16[448,896]{1,0:T(8,128)(2,1)} collective-permute-done((bf16[448,896]{1,0:T(8,128)(2,1)}, bf16[448,896]{1,0:T(8,128)(2,1)}, u32[]{:S(2)}, u32[]{:S(2)}) %collective-permute-start.15) | collective-permute-done | bytes 802848 | tf_op jit(solution)/shard_map/ppermute | solution.py:29
  63.7 5.4 %near_product.1 = (f32[896,896]{1,0:T(8,128)S(1)}, bf16[8,448,896]{2,1,0:T(8,128)(2,1)S(1)}) custom-call(bf16[448,896]{1,0:T(8,128)(2,1)S(1)} %fusion.refs_0_, bf16[448,896]{1,0:T(8,128)(2,1)S(1)} %collective-permute-done.5.refs_1_, bf16[448,896]{1,0:T(8,128)(2,1)S(1)} %pad_maximum_fusion.refs_2_, ...), custom_call_target="tpu_custom_call", output_to_operand_aliasing={{1}: (6, {})} | custom-call | flops 2877292544 | bytes 12582912 | tf_op jit(solution)/shard_map/near_product/pallas_call | solution.py:164
  69.1 1.3 %collective-permute-done.8.refs_2_ = bf16[448,896]{1,0:T(8,128)(2,1)S(1)} collective-permute-done((bf16[448,896]{1,0:T(8,128)(2,1)S(1)}, bf16[448,896]{1,0:T(8,128)(2,1)S(1)}, u32[]{:S(2)}, u32[]{:S(2)}) %collective-permute-start.8) | collective-permute-done | bytes 802848 | tf_op jit(solution)/shard_map/ppermute | solution.py:29
  70.4 2.1 %far_product.3 = f32[448,896]{1,0:T(8,128)S(1)} custom-call(bf16[448,896]{1,0:T(8,128)(2,1)S(1)} %collective-permute-done.2.refs_0_, bf16[448,896]{1,0:T(8,128)(2,1)S(1)} %collective-permute-done.7.refs_1_, bf16[448,896]{1,0:T(8,128)(2,1)S(1)} %collective-permute-done.8.refs_2_, bf16[448,896]{1,0:T(8,128)(2,1)S(1)} %collective-permute-done.9.refs_3_, ...), custom_call_target="tpu_custom_call" | custom-call | flops 1438646272 | bytes 12582912 | tf_op jit(solution)/shard_map/far_product/pallas_call | solution.py:203
  72.5 4.0 %collective-permute-start.16 = (f32[448,896]{1,0:T(8,128)S(1)}, f32[448,896]{1,0:T(8,128)S(1)}, u32[]{:S(2)}, u32[]{:S(2)}) collective-permute-start(f32[448,896]{1,0:T(8,128)S(1)} %far_product.3), channel_id=1, source_target_pairs={{0,8},{1,9},{2,10},{3,11},{4,12},{5,13},{6,14},{7,15},{8,0},{9,1},... | collective-permute-start | bytes 4816904 | tf_op jit(solution)/shard_map/ppermute | solution.py:29
  76.4 2.0 %far_product.2.keep_ref = f32[448,896]{1,0:T(8,128)S(1)} custom-call(bf16[448,896]{1,0:T(8,128)(2,1)S(1)} %collective-permute-done.2.refs_0_, bf16[448,896]{1,0:T(8,128)(2,1)S(1)} %collective-permute-done.7.refs_1_, bf16[448,896]{1,0:T(8,128)(2,1)S(1)} %collective-permute-done.8.refs_2_, bf16[448,896]{1,0:T(8,128)(2,1)S(1)} %collective-permute-done.9.refs_3_, ...), custom_call_target="tpu_custom_call" | custom-call | flops 1438646272 | bytes 12582912 | tf_op jit(solution)/shard_map/far_product/pallas_call | solution.py:203
  78.5 1.0 collective-permute-done.16.got_ref
  79.5 0.9 join.1
  80.4 1.9 %collective-permute-start.18 = (s16[240,896]{1,0:T(8,128)(2,1)S(1)}, s16[240,896]{1,0:T(8,128)(2,1)}, u32[]{:S(2)}, u32[]{:S(2)}) collective-permute-start(s16[240,896]{1,0:T(8,128)(2,1)S(1)} %get-tuple-element.34), channel_id=1, source_target_pairs={{0,0},{1,80},{2,18},{3,66},{4,4},{5,84},{6,22},{7,70},{8,8},{9,88}... | collective-permute-start | bytes 1290248 | tf_op jit(solution)/shard_map/ppermute | solution.py:29
  82.4 3.3 %collective-permute-start.17 = (s16[240,896]{1,0:T(8,128)(2,1)S(1)}, s16[240,896]{1,0:T(8,128)(2,1)S(1)}, u32[]{:S(2)}, u32[]{:S(2)}) collective-permute-start(s16[240,896]{1,0:T(8,128)(2,1)S(1)} %get-tuple-element.33), channel_id=1, source_target_pairs={{0,0},{1,16},{2,32},{3,48},{4,64},{5,80},{6,96},{7,112},{8,8},{9,2... | collective-permute-start | bytes 1290248 | tf_op jit(solution)/shard_map/ppermute | solution.py:29
  85.7 9.1 %collective-permute-done.18 = s16[240,896]{1,0:T(8,128)(2,1)} collective-permute-done((s16[240,896]{1,0:T(8,128)(2,1)S(1)}, s16[240,896]{1,0:T(8,128)(2,1)}, u32[]{:S(2)}, u32[]{:S(2)}) %collective-permute-start.18) | collective-permute-done | bytes 430112 | tf_op jit(solution)/shard_map/ppermute | solution.py:29
  94.8 1.2 %collective-permute-start.19 = (s16[240,896]{1,0:T(8,128)(2,1)}, s16[240,896]{1,0:T(8,128)(2,1)S(1)}, u32[]{:S(2)}, u32[]{:S(2)}) collective-permute-start(s16[240,896]{1,0:T(8,128)(2,1)} %collective-permute-done.18), channel_id=1, source_target_pairs={{0,8},{1,13},{2,60},{3,57},{4,72},{5,77},{6,124},{7,121},{8,0},{9,... | collective-permute-start | bytes 1290248 | tf_op jit(solution)/shard_map/ppermute | solution.py:29
  96.2 6.7 %collective-permute-done.17.same_ref = s16[240,896]{1,0:T(8,128)(2,1)S(1)} collective-permute-done((s16[240,896]{1,0:T(8,128)(2,1)S(1)}, s16[240,896]{1,0:T(8,128)(2,1)S(1)}, u32[]{:S(2)}, u32[]{:S(2)}) %collective-permute-start.17) | collective-permute-done | bytes 430112 | tf_op jit(solution)/shard_map/ppermute | solution.py:29
  102.9 17.1 %collective-permute-done.19.cross_ref = s16[240,896]{1,0:T(8,128)(2,1)S(1)} collective-permute-done((s16[240,896]{1,0:T(8,128)(2,1)}, s16[240,896]{1,0:T(8,128)(2,1)S(1)}, u32[]{:S(2)}, u32[]{:S(2)}) %collective-permute-start.19) | collective-permute-done | bytes 430112 | tf_op jit(solution)/shard_map/ppermute | solution.py:29
  120.0 2.5 %combine.1 = f32[448,896]{1,0:T(8,128)} custom-call(f32[448,896]{1,0:T(8,128)S(1)} %get-tuple-element.32.product_ref, s16[240,896]{1,0:T(8,128)(2,1)S(1)} %collective-permute-done.17.same_ref, s16[240,896]{1,0:T(8,128)(2,1)S(1)} %collective-permute-done.19.cross_ref, f32[448,1]{1,0:T(8,128)S(1)} %copy.9.row_gap_ref, f32[1,896]{1,0:T(1,128)S(1)} %broadcast_in_dim.87.col_gap_ref), custom_call_target="tpu_custom_call" | custom-call | flops 1605632 | bytes 4816896 | tf_op jit(solution)/shard_map/combine/pallas_call | solution.py:267
  (55 shorter events, 6.4 us)
Async XLA Ops:
  0.0 7.6 %copy-start.2 = (bf16[448,896]{1,0:T(8,128)(2,1)S(1)}, bf16[448,896]{1,0:T(8,128)(2,1)}, u32[]{:S(2)}) copy-start(bf16[448,896]{1,0:T(8,128)(2,1)} %param.6) | copy-start | bytes 2408452
  0.0 4.6 %copy-start = (bf16[448,896]{1,0:T(8,128)(2,1)S(1)}, bf16[448,896]{1,0:T(8,128)(2,1)}, u32[]{:S(2)}) copy-start(bf16[448,896]{1,0:T(8,128)(2,1)} %refs_0_.1) | copy-start | bytes 2408452
  0.0 4.6 %collective-permute-start = (bf16[448,896]{1,0:T(8,128)(2,1)}, bf16[448,896]{1,0:T(8,128)(2,1)S(1)}, u32[]{:S(2)}, u32[]{:S(2)}) collective-permute-start(bf16[448,896]{1,0:T(8,128)(2,1)} %param.6), channel_id=1, source_target_pairs={{0,8},{1,9},{2,10},{3,11},{4,12},{5,13},{6,14},{7,15},{8,0},{9,1},... | collective-permute-start | bytes 2408456 | tf_op jit(solution)/shard_map/ppermute | solution.py:29
  0.7 20.1 %collective-permute-start.1 = (bf16[448,896]{1,0:T(8,128)(2,1)}, bf16[448,896]{1,0:T(8,128)(2,1)}, u32[]{:S(2)}, u32[]{:S(2)}) collective-permute-start(bf16[448,896]{1,0:T(8,128)(2,1)} %refs_0_.1), channel_id=1, source_target_pairs={{0,64},{1,65},{2,66},{3,67},{4,68},{5,69},{6,70},{7,71},{8,72},{9,... | collective-permute-start | bytes 2408456 | tf_op jit(solution)/shard_map/ppermute | solution.py:29
  4.6 20.5 %collective-permute-start.10 = (bf16[448,896]{1,0:T(8,128)(2,1)S(1)}, bf16[448,896]{1,0:T(8,128)(2,1)}, u32[]{:S(2)}, u32[]{:S(2)}) collective-permute-start(bf16[448,896]{1,0:T(8,128)(2,1)S(1)} %copy-done), channel_id=1, source_target_pairs={{0,16},{1,17},{2,18},{3,19},{4,20},{5,21},{6,22},{7,23},{8,24},{9,... | collective-permute-start | bytes 2408456 | tf_op jit(solution)/shard_map/ppermute | solution.py:29
  5.9 19.2 %collective-permute-start.11 = (bf16[448,896]{1,0:T(8,128)(2,1)S(1)}, bf16[448,896]{1,0:T(8,128)(2,1)}, u32[]{:S(2)}, u32[]{:S(2)}) collective-permute-start(bf16[448,896]{1,0:T(8,128)(2,1)S(1)} %copy-done), channel_id=1, source_target_pairs={{0,48},{1,49},{2,50},{3,51},{4,52},{5,53},{6,54},{7,55},{8,56},{9,... | collective-permute-start | bytes 2408456 | tf_op jit(solution)/shard_map/ppermute | solution.py:29
  7.4 1.0 copy-start.3
  7.4 1.2 copy-start.4
  9.3 24.9 %copy-start.5 = (s32[7168]{0:T(1024)S(1)}, s32[7168]{0:T(1024)}, u32[]{:S(2)}) copy-start(s32[7168]{0:T(1024)} %param.10) | copy-start | bytes 86020
  9.3 24.9 %copy-start.6 = (s32[7168]{0:T(1024)S(1)}, s32[7168]{0:T(1024)}, u32[]{:S(2)}) copy-start(s32[7168]{0:T(1024)} %param.11) | copy-start | bytes 86020
  9.3 38.2 %copy-start.7 = (f32[1000]{0:T(1024)S(1)}, f32[1000]{0:T(1024)}, u32[]{:S(2)}) copy-start(f32[1000]{0:T(1024)} %param.9) | copy-start | bytes 12004
  9.3 38.6 %copy-start.8 = (f32[80]{0:T(128)S(1)}, f32[80]{0:T(128)}, u32[]{:S(2)}) copy-start(f32[80]{0:T(128)} %param.8) | copy-start | bytes 964
  9.3 21.8 %collective-permute-start.3 = (bf16[448,896]{1,0:T(8,128)(2,1)S(1)}, bf16[448,896]{1,0:T(8,128)(2,1)S(1)}, u32[]{:S(2)}, u32[]{:S(2)}) collective-permute-start(bf16[448,896]{1,0:T(8,128)(2,1)S(1)} %fusion.refs_0_), channel_id=1, source_target_pairs={{0,2},{1,3},{2,4},{3,5},{4,6},{5,7},{6,0},{7,1},{8,10},{9,11},{10,... | collective-permute-start | bytes 2408456 | tf_op jit(solution)/shard_map/ppermute | solution.py:29
  9.4 22.5 %collective-permute-start.5 = (bf16[448,896]{1,0:T(8,128)(2,1)S(1)}, bf16[448,896]{1,0:T(8,128)(2,1)S(1)}, u32[]{:S(2)}, u32[]{:S(2)}) collective-permute-start(bf16[448,896]{1,0:T(8,128)(2,1)S(1)} %fusion.refs_0_), channel_id=1, source_target_pairs={{0,6},{1,7},{2,0},{3,1},{4,2},{5,3},{6,4},{7,5},{8,14},{9,15},{10,... | collective-permute-start | bytes 2408456 | tf_op jit(solution)/shard_map/ppermute | solution.py:29
  25.1 19.7 %collective-permute-start.14 = (bf16[448,896]{1,0:T(8,128)(2,1)}, bf16[448,896]{1,0:T(8,128)(2,1)}, u32[]{:S(2)}, u32[]{:S(2)}) collective-permute-start(bf16[448,896]{1,0:T(8,128)(2,1)} %collective-permute-done.10.refs_3_), channel_id=1, source_target_pairs={{0,16},{1,17},{2,18},{3,19},{4,20},{5,21},{6,22},{7,23},{8,24},{9,... | collective-permute-start | bytes 2408456 | tf_op jit(solution)/shard_map/ppermute | solution.py:29
  26.0 18.8 %collective-permute-start.12 = (bf16[448,896]{1,0:T(8,128)(2,1)}, bf16[448,896]{1,0:T(8,128)(2,1)}, u32[]{:S(2)}, u32[]{:S(2)}) collective-permute-start(bf16[448,896]{1,0:T(8,128)(2,1)} %collective-permute-done.1.refs_4_), channel_id=1, source_target_pairs={{0,48},{1,49},{2,50},{3,51},{4,52},{5,53},{6,54},{7,55},{8,56},{9,... | collective-permute-start | bytes 2408456 | tf_op jit(solution)/shard_map/ppermute | solution.py:29
  27.8 21.5 %collective-permute-start.2 = (bf16[448,896]{1,0:T(8,128)(2,1)S(1)}, bf16[448,896]{1,0:T(8,128)(2,1)S(1)}, u32[]{:S(2)}, u32[]{:S(2)}) collective-permute-start(bf16[448,896]{1,0:T(8,128)(2,1)S(1)} %fusion.refs_0_), channel_id=1, source_target_pairs={{0,1},{1,0},{2,3},{3,2},{4,5},{5,4},{6,7},{7,6},{8,9},{9,8},{10,11... | collective-permute-start | bytes 2408456 | tf_op jit(solution)/shard_map/ppermute | solution.py:29
  31.9 16.1 %collective-permute-start.4 = (bf16[224,896]{1,0:T(8,128)(2,1)}, bf16[224,896]{1,0:T(8,128)(2,1)}, u32[]{:S(2)}, u32[]{:S(2)}) collective-permute-start(bf16[224,896]{1,0:T(8,128)(2,1)} %slice.28), channel_id=1, source_target_pairs={{0,2},{1,3},{2,4},{3,5},{4,6},{5,7},{6,0},{7,1},{8,10},{9,11},{10,... | collective-permute-start | bytes 1204232 | tf_op jit(solution)/shard_map/ppermute | solution.py:29
  32.7 15.4 %collective-permute-start.6 = (bf16[224,896]{1,0:T(8,128)(2,1)}, bf16[224,896]{1,0:T(8,128)(2,1)}, u32[]{:S(2)}, u32[]{:S(2)}) collective-permute-start(bf16[224,896]{1,0:T(8,128)(2,1)} %slice.29), channel_id=1, source_target_pairs={{0,6},{1,7},{2,0},{3,1},{4,2},{5,3},{6,4},{7,5},{8,14},{9,15},{10,... | collective-permute-start | bytes 1204232 | tf_op jit(solution)/shard_map/ppermute | solution.py:29
  44.8 18.8 %collective-permute-start.15 = (bf16[448,896]{1,0:T(8,128)(2,1)}, bf16[448,896]{1,0:T(8,128)(2,1)}, u32[]{:S(2)}, u32[]{:S(2)}) collective-permute-start(bf16[448,896]{1,0:T(8,128)(2,1)} %collective-permute-done.1.refs_4_), channel_id=1, source_target_pairs={{0,16},{1,17},{2,18},{3,19},{4,20},{5,21},{6,22},{7,23},{8,24},{9,... | collective-permute-start | bytes 2408456 | tf_op jit(solution)/shard_map/ppermute | solution.py:29
  44.9 18.8 %collective-permute-start.13 = (bf16[448,896]{1,0:T(8,128)(2,1)}, bf16[448,896]{1,0:T(8,128)(2,1)}, u32[]{:S(2)}, u32[]{:S(2)}) collective-permute-start(bf16[448,896]{1,0:T(8,128)(2,1)} %collective-permute-done.12.refs_5_), channel_id=1, source_target_pairs={{0,48},{1,49},{2,50},{3,51},{4,52},{5,53},{6,54},{7,55},{8,56},{9,... | collective-permute-start | bytes 2408456 | tf_op jit(solution)/shard_map/ppermute | solution.py:29
  47.9 8.2 %copy-start.1 = (bf16[448,896]{1,0:T(8,128)(2,1)S(1)}, bf16[448,896]{1,0:T(8,128)(2,1)}, u32[]{:S(2)}) copy-start(bf16[448,896]{1,0:T(8,128)(2,1)} %refs_0_.1) | copy-start | bytes 2408452
  49.3 19.7 %collective-permute-start.7 = (bf16[448,896]{1,0:T(8,128)(2,1)S(1)}, bf16[448,896]{1,0:T(8,128)(2,1)S(1)}, u32[]{:S(2)}, u32[]{:S(2)}) collective-permute-start(bf16[448,896]{1,0:T(8,128)(2,1)S(1)} %collective-permute-done.2.refs_0_), channel_id=1, source_target_pairs={{0,6},{1,7},{2,0},{3,1},{4,2},{5,3},{6,4},{7,5},{8,14},{9,15},{10,... | collective-permute-start | bytes 2408456 | tf_op jit(solution)/shard_map/ppermute | solution.py:29
  49.9 20.5 %collective-permute-start.9 = (bf16[448,896]{1,0:T(8,128)(2,1)S(1)}, bf16[448,896]{1,0:T(8,128)(2,1)S(1)}, u32[]{:S(2)}, u32[]{:S(2)}) collective-permute-start(bf16[448,896]{1,0:T(8,128)(2,1)S(1)} %collective-permute-done.2.refs_0_), channel_id=1, source_target_pairs={{0,2},{1,3},{2,4},{3,5},{4,6},{5,7},{6,0},{7,1},{8,10},{9,11},{10,... | collective-permute-start | bytes 2408456 | tf_op jit(solution)/shard_map/ppermute | solution.py:29
  52.1 18.3 %collective-permute-start.8 = (bf16[448,896]{1,0:T(8,128)(2,1)S(1)}, bf16[448,896]{1,0:T(8,128)(2,1)S(1)}, u32[]{:S(2)}, u32[]{:S(2)}) collective-permute-start(bf16[448,896]{1,0:T(8,128)(2,1)S(1)} %pad_maximum_fusion.refs_2_), channel_id=1, source_target_pairs={{0,1},{1,0},{2,3},{3,2},{4,5},{5,4},{6,7},{7,6},{8,9},{9,8},{10,11... | collective-permute-start | bytes 2408456 | tf_op jit(solution)/shard_map/ppermute | solution.py:29
  72.5 7.0 %collective-permute-start.16 = (f32[448,896]{1,0:T(8,128)S(1)}, f32[448,896]{1,0:T(8,128)S(1)}, u32[]{:S(2)}, u32[]{:S(2)}) collective-permute-start(f32[448,896]{1,0:T(8,128)S(1)} %far_product.3), channel_id=1, source_target_pairs={{0,8},{1,9},{2,10},{3,11},{4,12},{5,13},{6,14},{7,15},{8,0},{9,1},... | collective-permute-start | bytes 4816904 | tf_op jit(solution)/shard_map/ppermute | solution.py:29
  80.4 14.3 %collective-permute-start.18 = (s16[240,896]{1,0:T(8,128)(2,1)S(1)}, s16[240,896]{1,0:T(8,128)(2,1)}, u32[]{:S(2)}, u32[]{:S(2)}) collective-permute-start(s16[240,896]{1,0:T(8,128)(2,1)S(1)} %get-tuple-element.34), channel_id=1, source_target_pairs={{0,0},{1,80},{2,18},{3,66},{4,4},{5,84},{6,22},{7,70},{8,8},{9,88}... | collective-permute-start | bytes 1290248 | tf_op jit(solution)/shard_map/ppermute | solution.py:29
  82.4 20.5 %collective-permute-start.17 = (s16[240,896]{1,0:T(8,128)(2,1)S(1)}, s16[240,896]{1,0:T(8,128)(2,1)S(1)}, u32[]{:S(2)}, u32[]{:S(2)}) collective-permute-start(s16[240,896]{1,0:T(8,128)(2,1)S(1)} %get-tuple-element.33), channel_id=1, source_target_pairs={{0,0},{1,16},{2,32},{3,48},{4,64},{5,80},{6,96},{7,112},{8,8},{9,2... | collective-permute-start | bytes 1290248 | tf_op jit(solution)/shard_map/ppermute | solution.py:29
  94.8 25.3 %collective-permute-start.19 = (s16[240,896]{1,0:T(8,128)(2,1)}, s16[240,896]{1,0:T(8,128)(2,1)S(1)}, u32[]{:S(2)}, u32[]{:S(2)}) collective-permute-start(s16[240,896]{1,0:T(8,128)(2,1)} %collective-permute-done.18), channel_id=1, source_target_pairs={{0,8},{1,13},{2,60},{3,57},{4,72},{5,77},{6,124},{7,121},{8,0},{9,... | collective-permute-start | bytes 1290248 | tf_op jit(solution)/shard_map/ppermute | solution.py:29

commit v6 on v5

--- a/solution.py
+++ b/solution.py
@@ -84,12 +84,11 @@
     right_z_up = send(after(right_z, right_two), along_x(1))
     right_z_two = send(right_z_down, along_x(-1))
     left_two = jnp.concatenate([send(left_up[:half], along_y(1)), send(left_down[half:], along_y(-1))])
-    left_z, left_two = lax.optimization_barrier((left_z, left_two))
     left_z_up, left_z_down = send(left_z, along_y(1)), send(left_z, along_y(-1))
     left_z_two = send(left_two, across_z_hi)
     near = [left, left_down, left_two, left_up]
     far = [left_z, left_z_down, left_z_two, left_z_up]
-    return near, far, [right, right_down, right_two, right_up, right_z, right_z_down], [right_z_two, right_z_up]
+    return near, far, [right, right_down, right_two, right_up], [right_z, right_z_down, right_z_two, right_z_up]
 
 
 def block_of(values, index, count):
@@ -104,113 +103,111 @@
     return jnp.sum(picked, axis=1)
 
 
-LATE = 2
-
-
-def stack_kernel(*refs):
-    *parts, stack_ref, sem = refs
-    copies = [pltpu.make_async_copy(part, stack_ref.at[i], sem.at[i]) for i, part in enumerate(parts)]
+def copies_into(stack_ref, first, parts, sem):
+    return [pltpu.make_async_copy(part, stack_ref.at[first + i], sem.at[i]) for i, part in enumerate(parts)]
+
+
+def product_terms(kind):
+    row, col = lax.axis_index("row"), lax.axis_index("col")
+    z_lo, x = row // (X * CORE), (row // CORE) % X
+    y, z_hi = col // Z_HI, col % Z_HI
+    left_far, right_far = kind
+    low = 1 - z_hi if left_far else z_hi
+    high = 1 - z_lo if right_far else z_lo
+    terms = []
+    for middle in range(2):
+        left_y, right_x = high * 2 + middle, middle * 2 + low
+        terms.append((
+            left_far * Y + lax.rem(left_y - y + Y, Y), right_far * X + lax.rem(right_x - x + X, X)))
+    return terms
+
+
+def near_kernel(*refs):
+    left, right, (sum_ref, stack_ref, left_stack, acc, sem_left, sem_right) = refs[:Y], refs[Y:Y + X], refs[Y + X:]
+    depth = stack_ref.shape[2] // 2
+    copies = copies_into(left_stack, 0, left, sem_left) + copies_into(stack_ref, 0, right, sem_right)
     for copy in copies:
         copy.start()
     for copy in copies:
         copy.wait()
-
-
-def stacked(parts):
-    rows, cols = parts[0].shape
-    return pl.pallas_call(
-        stack_kernel,
-        out_shape=jax.ShapeDtypeStruct((len(parts) + LATE, rows, cols), jnp.bfloat16),
-        in_specs=[pl.BlockSpec(memory_space=pl.ANY)] * len(parts),
-        out_specs=pl.BlockSpec(memory_space=pltpu.VMEM),
-        scratch_shapes=[pltpu.SemaphoreType.DMA((len(parts),))],
-        compiler_params=pltpu.CompilerParams(vmem_limit_bytes=4 * MIB),
-        cost_estimate=pl.CostEstimate(flops=0, bytes_accessed=4 * MIB, transcendentals=0),
-        name="stacked",
-    )(*parts)
-
-
-def place_of(slot, far):
-    row, col = lax.axis_index("row"), lax.axis_index("col")
-    z_lo, x = row // (X * CORE), (row // CORE) % X
-    y, z_hi = col // Z_HI, col % Z_HI
-    block = lax.rem(y + slot, Y) * Z_HI + (1 - z_hi if far else z_hi)
-    return (block // X + z_lo) % Z_LO * X + lax.rem(block % X - x + X, X)
-
-
-def near_kernel(*refs):
-    left, late, (_, sum_ref, stack_ref, acc, sem) = refs[:Y], refs[Y:Y + LATE], refs[Y + LATE:]
-    depth = stack_ref.shape[2] // 2
-    first = stack_ref.shape[0] - LATE
-    copies = [pltpu.make_async_copy(part, stack_ref.at[first + i], sem.at[i]) for i, part in enumerate(late)]
-    for copy in copies:
-        copy.start()
-    for copy in copies:
-        copy.wait()
-    for slot in range(Y):
-        both = jnp.concatenate([left[slot][:, :depth], left[slot][:, depth:]])
-        term = jnp.dot(both, stack_ref[place_of(slot, False)], preferred_element_type=jnp.float32)
-        if slot == 0:
+    for i, (left_slot, right_slot) in enumerate(product_terms((0, 0))):
+        block = left_stack[left_slot]
+        both = jnp.concatenate([block[:, :depth], block[:, depth:]])
+        term = jnp.dot(both, stack_ref[right_slot], preferred_element_type=jnp.float32)
+        if i == 0:
             acc[...] = term
-        elif slot < Y - 1:
-            acc[...] += term
         else:
             sum_ref[...] = acc[...] + term
 
 
-def near_product(left, right, stack):
+def near_product(left, right):
     rows, cols = left[0].shape
     vmem = pl.BlockSpec(memory_space=pltpu.VMEM)
+    stack = jax.ShapeDtypeStruct((2 * X, rows, cols), jnp.bfloat16)
     return pl.pallas_call(
         near_kernel,
-        out_shape=[
-            jax.ShapeDtypeStruct((2 * rows, cols), jnp.float32),
-            jax.ShapeDtypeStruct(stack.shape, stack.dtype)],
-        in_specs=[vmem] * Y + [pl.BlockSpec(memory_space=pl.ANY)] * LATE + [vmem],
-        out_specs=[vmem] * 2,
+        out_shape=[jax.ShapeDtypeStruct((2 * rows, cols), jnp.float32), stack, stack],
+        in_specs=[pl.BlockSpec(memory_space=pl.ANY)] * (X + Y),
+        out_specs=[vmem] * 3,
         scratch_shapes=[
             pltpu.VMEM((2 * rows, cols), jnp.float32),
-            pltpu.SemaphoreType.DMA((LATE,)),
+            pltpu.SemaphoreType.DMA((Y,)),
+            pltpu.SemaphoreType.DMA((X,)),
         ],
-        input_output_aliases={Y + LATE: 1},
         compiler_params=pltpu.CompilerParams(vmem_limit_bytes=10 * MIB),
         cost_estimate=pl.CostEstimate(
-            flops=4 * Y * rows * cols * cols // 2, bytes_accessed=12 * MIB, transcendentals=0),
+            flops=4 * 2 * rows * cols * cols // 2, bytes_accessed=12 * MIB, transcendentals=0),
         name="near_product",
-    )(*left, *right, stack)
-
-
-def far_kernel(own, *refs):
-    left, (sum_ref, stack_ref, out_ref, acc) = refs[:Y], refs[Y:]
-    depth = stack_ref.shape[2] // 2
+    )(*left, *right)
+
+
+def far_kernel(own, parts, *refs):
+    incoming, refs = refs[:parts], refs[parts:]
+    if parts:
+        sum_ref, _, _, out_ref, right_stack, left_stack, acc, sem_left, sem_right = refs
+        copies = copies_into(left_stack, Y, incoming[:Y], sem_left)
+        copies += copies_into(right_stack, X, incoming[Y:], sem_right)
+        for copy in copies:
+            copy.start()
+        for copy in copies:
+            copy.wait()
+    else:
+        sum_ref, right_stack, left_stack, out_ref, acc = refs
+    depth = right_stack.shape[2] // 2
     rows = out_ref.shape[0]
     first = 0 if own else 1
-    for slot in range(Y):
+    terms = product_terms((0, 1)) + product_terms((1, 0)) + product_terms((1, 1))
+    for i, (left_slot, right_slot) in enumerate(terms):
+        block = left_stack[left_slot]
         term = jnp.dot(
-            left[slot][:, first * depth:(first + 1) * depth], stack_ref[place_of(slot, True)],
-            preferred_element_type=jnp.float32)
-        if slot == 0:
+            block[:, first * depth:(first + 1) * depth], right_stack[right_slot], preferred_element_type=jnp.float32)
+        if i == 0:
             acc[...] = term + sum_ref[first * rows:(first + 1) * rows, :]
-        elif slot < Y - 1:
+        elif i < len(terms) - 1:
             acc[...] += term
         else:
             out_ref[...] = acc[...] + term
 
 
-def far_product(left, total, stack, own):
-    rows, cols = left[0].shape
+def far_product(incoming, total, right_stack, left_stack, own):
+    rows, cols = right_stack.shape[1:]
+    parts = len(incoming)
     vmem = pl.BlockSpec(memory_space=pltpu.VMEM)
+    stack = jax.ShapeDtypeStruct(right_stack.shape, right_stack.dtype)
+    out = jax.ShapeDtypeStruct((rows, cols), jnp.float32)
+    sems = [pltpu.SemaphoreType.DMA((Y,)), pltpu.SemaphoreType.DMA((X,))]
     return pl.pallas_call(
-        lambda *refs: far_kernel(own, *refs),
-        out_shape=jax.ShapeDtypeStruct((rows, cols), jnp.float32),
-        in_specs=[vmem] * (Y + 2),
-        out_specs=vmem,
-        scratch_shapes=[pltpu.VMEM((rows, cols), jnp.float32)],
+        lambda *refs: far_kernel(own, parts, *refs),
+        out_shape=[out, stack, stack] if parts else out,
+        in_specs=[pl.BlockSpec(memory_space=pl.ANY)] * parts + [vmem] * 3,
+        out_specs=[vmem] * 3 if parts else vmem,
+        scratch_shapes=[pltpu.VMEM((rows, cols), jnp.float32)] + (sems if parts else []),
+        input_output_aliases={parts + 1: 1, parts + 2: 2} if parts else {},
         compiler_params=pltpu.CompilerParams(vmem_limit_bytes=6 * MIB),
         cost_estimate=pl.CostEstimate(
-            flops=2 * Y * rows * cols * cols // 2, bytes_accessed=12 * MIB, transcendentals=0),
+            flops=2 * 6 * rows * cols * cols // 2, bytes_accessed=12 * MIB, transcendentals=0),
         name="far_product",
-    )(*left, total, stack)
+    )(*incoming, total, right_stack, left_stack)
 
 
 def encode(block, payload_ref):
@@ -285,7 +282,7 @@
         lane < half,
         jnp.where(core == 0, amplitudes, jnp.roll(amplitudes, half, axis=1)),
         jnp.where(core == 0, jnp.roll(other, half, axis=1), other))
-    near, far, early, late = gather(left, integrals, other)
+    near, far, right_near, right_far = gather(left, integrals, other)
 
     row_count, col_count = lax.axis_size("row"), lax.axis_size("col")
     row, col = lax.axis_index("row"), lax.axis_index("col")
@@ -294,11 +291,11 @@
     row_gap = lookup(occ_energy, row_occ) - lookup(vir_energy, row_vir)
     col_gap = lookup(occ_energy, col_occ) - lookup(vir_energy, col_vir)
 
-    stack, row_gap, col_gap = lax.optimization_barrier((stacked(early), row_gap, col_gap))
-    total, stack = near_product(near, late, stack)
-    give = far_product(far, total, stack, False)
+    total, right_stack, left_stack = near_product(near, right_near)
+    total, row_gap, col_gap = lax.optimization_barrier((total, row_gap, col_gap))
+    give, right_stack, left_stack = far_product((*far, *right_far), total, right_stack, left_stack, False)
     got = send(give, across_core)
-    keep = far_product(far, total, stack, True)
+    keep = far_product((), total, right_stack, left_stack, True)
     product, to_same, to_cross = join(keep, got)
     same = send(to_same, mirrored(0))
     cross = send(send(to_cross, detour), after_detour)

time: 123 us -> 121 us (0.984)
  waiting for transfers between devices: 65.3 us -> 59 us
  starting transfers between devices: 33.2 us -> 37.5 us
  other arithmetic: 3.26 us -> 1.99 us
    ppermute x20, waiting for transfers between devices: 65.3 us -> 59 us  [send(): return lax.ppermute(block, AXES, pairs)]
    ppermute x20, starting transfers between devices: 33.2 us -> 37.5 us  [send(): return lax.ppermute(block, AXES, pairs)]
    pallas_call x1, Pallas kernels: 5.41 us -> 3.98 us  [near_product(): pl.pallas_call(near_kernel, out_shape=[jax.ShapeDtypeStruct((2 * rows, co...]
    pallas_call x3 -> x2, Pallas kernels: 6.38 us -> 7.79 us  [far_product(): pl.pallas_call(lambda *refs: far_kernel(own, parts, *refs), out_shape=[ou...]
    concatenate x1 -> x0, other arithmetic: 1.27 us -> none  [gather(): jnp.concatenate([send(left_up[:half], along_y(1)), send(left_down[half:],...]
  transfers between devices with their start and end apart: 20 -> 20, of which waited for: 9 -> 11; matrix products, arithmetic and copies ran while one was open for 6% -> 6% of each run, Pallas kernels for 8% -> 6%
where the time goes in v6:
time: 121 us; the launch traced here: 120 us
  waiting for transfers between devices  59 us (49%)
  starting transfers between devices  37.5 us (31%)
  Pallas kernels  15.2 us (13%)
  local copies, waits for them, and re-layouts  6.52 us (5%)
  other arithmetic  1.99 us (2%)
    ppermute x20, waiting for transfers between devices, send(): return lax.ppermute(block, AXES, pairs)  59 us
    ppermute x20, starting transfers between devices, send(): return lax.ppermute(block, AXES, pairs)  37.5 us
    pallas_call x2, Pallas kernels, far_product(): pl.pallas_call(lambda *refs: far_kernel(own, parts, *refs), out_shape=[ou...  7.79 us
    pallas_call x1, Pallas kernels, near_product(): pl.pallas_call(near_kernel, out_shape=[jax.ShapeDtypeStruct((2 * rows, co...  3.98 us
    pallas_call x1, Pallas kernels, combine(): pl.pallas_call(combine_kernel, out_shape=jax.ShapeDtypeStruct((rows, cols...  2.53 us
  transfers between devices with their start and end apart: 20, of which 11 were waited for; matrix products, arithmetic and copies ran while one was open for 6% of the time, Pallas kernels for 6%

profile of v6, /device:TPU:25, one launch (start us, length us, event | category | flops | bytes accessed | tf_op | source)
XLA Modules:
  0.0 120.5 jit_solution(13405095079426777958)
XLA Ops:
  0.7 1.7 %collective-permute-start.7 = (bf16[448,896]{1,0:T(8,128)(2,1)}, bf16[448,896]{1,0:T(8,128)(2,1)}, u32[]{:S(2)}, u32[]{:S(2)}) collective-permute-start(bf16[448,896]{1,0:T(8,128)(2,1)} %refs_4_.1), channel_id=1, source_target_pairs={{0,64},{1,65},{2,66},{3,67},{4,68},{5,69},{6,70},{7,71},{8,72},{9,... | collective-permute-start | bytes 2408456 | tf_op jit(solution)/shard_map/ppermute | solution.py:29
  2.3 1.5 %fusion.2 = (bf16[448,448]{1,0:T(8,128)(2,1)S(1)}, bf16[448,448]{1,0:T(8,128)(2,1)S(1)}) fusion(bf16[448,896]{1,0:T(8,128)(2,1)} %param.6), kind=kLoop, calls=%fused_computation.21 | loop fusion | bytes 1605632 | tf_op jit(solution)/shard_map/jit(_roll_static)/slice | solution.py:283
  3.8 2.5 %collective-permute-start.6 = (bf16[448,896]{1,0:T(8,128)(2,1)S(1)}, bf16[448,896]{1,0:T(8,128)(2,1)S(1)}, u32[]{:S(2)}, u32[]{:S(2)}) collective-permute-start(bf16[448,896]{1,0:T(8,128)(2,1)S(1)} %copy-done), channel_id=1, source_target_pairs={{0,48},{1,49},{2,50},{3,51},{4,52},{5,53},{6,54},{7,55},{8,56},{9,... | collective-permute-start | bytes 2408456 | tf_op jit(solution)/shard_map/ppermute | solution.py:29
  7.5 1.5 %collective-permute-start.1 = (bf16[448,896]{1,0:T(8,128)(2,1)S(1)}, bf16[448,896]{1,0:T(8,128)(2,1)S(1)}, u32[]{:S(2)}, u32[]{:S(2)}) collective-permute-start(bf16[448,896]{1,0:T(8,128)(2,1)S(1)} %fusion.refs_0_), channel_id=1, source_target_pairs={{0,6},{1,7},{2,0},{3,1},{4,2},{5,3},{6,4},{7,5},{8,14},{9,15},{10,... | collective-permute-start | bytes 2408456 | tf_op jit(solution)/shard_map/ppermute | solution.py:29
  8.9 11.9 %collective-permute-done.7.refs_4_ = bf16[448,896]{1,0:T(8,128)(2,1)} collective-permute-done((bf16[448,896]{1,0:T(8,128)(2,1)}, bf16[448,896]{1,0:T(8,128)(2,1)}, u32[]{:S(2)}, u32[]{:S(2)}) %collective-permute-start.7) | collective-permute-done | bytes 802848 | tf_op jit(solution)/shard_map/ppermute | solution.py:29
  20.8 3.3 %collective-permute-start.9 = (bf16[448,896]{1,0:T(8,128)(2,1)S(1)}, bf16[448,896]{1,0:T(8,128)(2,1)}, u32[]{:S(2)}, u32[]{:S(2)}) collective-permute-start(bf16[448,896]{1,0:T(8,128)(2,1)S(1)} %fusion.refs_0_), channel_id=1, source_target_pairs={{0,1},{1,0},{2,3},{3,2},{4,5},{5,4},{6,7},{7,6},{8,9},{9,8},{10,11... | collective-permute-start | bytes 2408456 | tf_op jit(solution)/shard_map/ppermute | solution.py:29
  25.0 1.5 %collective-permute-done.5.refs_7_ = bf16[448,896]{1,0:T(8,128)(2,1)} collective-permute-done((bf16[448,896]{1,0:T(8,128)(2,1)S(1)}, bf16[448,896]{1,0:T(8,128)(2,1)}, u32[]{:S(2)}, u32[]{:S(2)}) %collective-permute-start.5) | collective-permute-done | bytes 802848 | tf_op jit(solution)/shard_map/ppermute | solution.py:29
  26.5 2.7 %collective-permute-start.13 = (bf16[448,896]{1,0:T(8,128)(2,1)}, bf16[448,896]{1,0:T(8,128)(2,1)}, u32[]{:S(2)}, u32[]{:S(2)}) collective-permute-start(bf16[448,896]{1,0:T(8,128)(2,1)} %collective-permute-done.7.refs_4_), channel_id=1, source_target_pairs={{0,48},{1,49},{2,50},{3,51},{4,52},{5,53},{6,54},{7,55},{8,56},{9,... | collective-permute-start | bytes 2408456 | tf_op jit(solution)/shard_map/ppermute | solution.py:29
  30.8 1.5 %collective-permute-start.4 = (bf16[224,896]{1,0:T(8,128)(2,1)}, bf16[224,896]{1,0:T(8,128)(2,1)}, u32[]{:S(2)}, u32[]{:S(2)}) collective-permute-start(bf16[224,896]{1,0:T(8,128)(2,1)} %slice.29), channel_id=1, source_target_pairs={{0,6},{1,7},{2,0},{3,1},{4,2},{5,3},{6,4},{7,5},{8,14},{9,15},{10,... | collective-permute-start | bytes 1204232 | tf_op jit(solution)/shard_map/ppermute | solution.py:29
  32.6 9.0 %collective-permute-done.9.refs_0_ = bf16[448,896]{1,0:T(8,128)(2,1)} collective-permute-done((bf16[448,896]{1,0:T(8,128)(2,1)S(1)}, bf16[448,896]{1,0:T(8,128)(2,1)}, u32[]{:S(2)}, u32[]{:S(2)}) %collective-permute-start.9) | collective-permute-done | bytes 802848 | tf_op jit(solution)/shard_map/ppermute | solution.py:29
  41.6 1.5 %collective-permute-start.10 = (bf16[448,896]{1,0:T(8,128)(2,1)}, bf16[448,896]{1,0:T(8,128)(2,1)S(1)}, u32[]{:S(2)}, u32[]{:S(2)}) collective-permute-start(bf16[448,896]{1,0:T(8,128)(2,1)} %collective-permute-done.9.refs_0_), channel_id=1, source_target_pairs={{0,6},{1,7},{2,0},{3,1},{4,2},{5,3},{6,4},{7,5},{8,14},{9,15},{10,... | collective-permute-start | bytes 2408456 | tf_op jit(solution)/shard_map/ppermute | solution.py:29
  43.1 1.0 constant_dynamic-update-slice_fusion.1
  44.1 1.0 constant_dynamic-update-slice_fusion.refs_2_
  45.1 2.7 %collective-permute-start.11 = (bf16[448,896]{1,0:T(8,128)(2,1)S(1)}, bf16[448,896]{1,0:T(8,128)(2,1)S(1)}, u32[]{:S(2)}, u32[]{:S(2)}) collective-permute-start(bf16[448,896]{1,0:T(8,128)(2,1)S(1)} %constant_dynamic-update-slice_fusion.refs_2_), channel_id=1, source_target_pairs={{0,1},{1,0},{2,3},{3,2},{4,5},{5,4},{6,7},{7,6},{8,9},{9,8},{10,11... | collective-permute-start | bytes 2408456 | tf_op jit(solution)/shard_map/ppermute | solution.py:29
  47.9 1.2 %collective-permute-start.15 = (bf16[448,896]{1,0:T(8,128)(2,1)}, bf16[448,896]{1,0:T(8,128)(2,1)S(1)}, u32[]{:S(2)}, u32[]{:S(2)}) collective-permute-start(bf16[448,896]{1,0:T(8,128)(2,1)} %collective-permute-done.7.refs_4_), channel_id=1, source_target_pairs={{0,16},{1,17},{2,18},{3,19},{4,20},{5,21},{6,22},{7,23},{8,24},{9,... | collective-permute-start | bytes 2408456 | tf_op jit(solution)/shard_map/ppermute | solution.py:29
  49.1 1.5 %collective-permute-start.14 = (bf16[448,896]{1,0:T(8,128)(2,1)}, bf16[448,896]{1,0:T(8,128)(2,1)S(1)}, u32[]{:S(2)}, u32[]{:S(2)}) collective-permute-start(bf16[448,896]{1,0:T(8,128)(2,1)} %collective-permute-done.13.refs_5_), channel_id=1, source_target_pairs={{0,48},{1,49},{2,50},{3,51},{4,52},{5,53},{6,54},{7,55},{8,56},{9,... | collective-permute-start | bytes 2408456 | tf_op jit(solution)/shard_map/ppermute | solution.py:29
  51.7 4.0 %near_product.1 = (f32[896,896]{1,0:T(8,128)S(1)}, bf16[8,448,896]{2,1,0:T(8,128)(2,1)S(1)}, bf16[8,448,896]{2,1,0:T(8,128)(2,1)S(1)}) custom-call(bf16[448,896]{1,0:T(8,128)(2,1)S(1)} %fusion.refs_0_, bf16[448,896]{1,0:T(8,128)(2,1)S(1)} %collective-permute-done.1.refs_1_, bf16[448,896]{1,0:T(8,128)(2,1)S(1)} %constant_dynamic-update-slice_fusion.refs_2_, ...), custom_call_target="tpu_custom_call" | custom-call | flops 1438646272 | bytes 12582912 | tf_op jit(solution)/shard_map/near_product/pallas_call | solution.py:147
  55.7 4.1 %collective-permute-done.12.refs_3_ = bf16[448,896]{1,0:T(8,128)(2,1)S(1)} collective-permute-done((bf16[448,896]{1,0:T(8,128)(2,1)}, bf16[448,896]{1,0:T(8,128)(2,1)S(1)}, u32[]{:S(2)}, u32[]{:S(2)}) %collective-permute-start.12) | collective-permute-done | bytes 802848 | tf_op jit(solution)/shard_map/ppermute | solution.py:29
  59.8 1.0 collective-permute-done.10.refs_1_
  60.8 3.4 %collective-permute-done.11.refs_2_ = bf16[448,896]{1,0:T(8,128)(2,1)S(1)} collective-permute-done((bf16[448,896]{1,0:T(8,128)(2,1)S(1)}, bf16[448,896]{1,0:T(8,128)(2,1)S(1)}, u32[]{:S(2)}, u32[]{:S(2)}) %collective-permute-start.11) | collective-permute-done | bytes 802848 | tf_op jit(solution)/shard_map/ppermute | solution.py:29
  64.1 2.0 %collective-permute-done.15.refs_7_ = bf16[448,896]{1,0:T(8,128)(2,1)S(1)} collective-permute-done((bf16[448,896]{1,0:T(8,128)(2,1)}, bf16[448,896]{1,0:T(8,128)(2,1)S(1)}, u32[]{:S(2)}, u32[]{:S(2)}) %collective-permute-start.15) | collective-permute-done | bytes 802848 | tf_op jit(solution)/shard_map/ppermute | solution.py:29
  66.1 4.8 %far_product.2 = (f32[448,896]{1,0:T(8,128)S(1)}, bf16[8,448,896]{2,1,0:T(8,128)(2,1)S(1)}, bf16[8,448,896]{2,1,0:T(8,128)(2,1)S(1)}) custom-call(bf16[448,896]{1,0:T(8,128)(2,1)} %collective-permute-done.9.refs_0_, bf16[448,896]{1,0:T(8,128)(2,1)S(1)} %collective-permute-done.10.refs_1_, ...), custom_call_target="tpu_custom_call", output_to_operand_aliasing={{1}: (9, {}), {2}: (10, {})} | custom-call | flops 2157969408 | bytes 12582912 | tf_op jit(solution)/shard_map/far_product/pallas_call | solution.py:199
  70.9 3.6 %collective-permute-start.16 = (f32[448,896]{1,0:T(8,128)S(1)}, f32[448,896]{1,0:T(8,128)S(1)}, u32[]{:S(2)}, u32[]{:S(2)}) collective-permute-start(f32[448,896]{1,0:T(8,128)S(1)} %get-tuple-element.35), channel_id=1, source_target_pairs={{0,8},{1,9},{2,10},{3,11},{4,12},{5,13},{6,14},{7,15},{8,0},{9,1},... | collective-permute-start | bytes 4816904 | tf_op jit(solution)/shard_map/ppermute | solution.py:29
  74.5 3.0 %far_product.3.keep_ref = f32[448,896]{1,0:T(8,128)S(1)} custom-call(f32[896,896]{1,0:T(8,128)S(1)} %get-tuple-element.27.refs_8_.refs_0_, bf16[8,448,896]{2,1,0:T(8,128)(2,1)S(1)} %get-tuple-element.33.refs_1_, bf16[8,448,896]{2,1,0:T(8,128)(2,1)S(1)} %get-tuple-element.34.refs_2_), custom_call_target="tpu_custom_call" | custom-call | flops 2157969408 | bytes 12582912 | tf_op jit(solution)/shard_map/far_product/pallas_call | solution.py:199
  77.6 0.9 join.1
  78.5 3.1 %collective-permute-start.18 = (s16[240,896]{1,0:T(8,128)(2,1)S(1)}, s16[240,896]{1,0:T(8,128)(2,1)}, u32[]{:S(2)}, u32[]{:S(2)}) collective-permute-start(s16[240,896]{1,0:T(8,128)(2,1)S(1)} %get-tuple-element.38), channel_id=1, source_target_pairs={{0,0},{1,80},{2,18},{3,66},{4,4},{5,84},{6,22},{7,70},{8,8},{9,88}... | collective-permute-start | bytes 1290248 | tf_op jit(solution)/shard_map/ppermute | solution.py:29
  81.6 6.0 %collective-permute-start.17 = (s16[240,896]{1,0:T(8,128)(2,1)S(1)}, s16[240,896]{1,0:T(8,128)(2,1)S(1)}, u32[]{:S(2)}, u32[]{:S(2)}) collective-permute-start(s16[240,896]{1,0:T(8,128)(2,1)S(1)} %get-tuple-element.37), channel_id=1, source_target_pairs={{0,0},{1,16},{2,32},{3,48},{4,64},{5,80},{6,96},{7,112},{8,8},{9,2... | collective-permute-start | bytes 1290248 | tf_op jit(solution)/shard_map/ppermute | solution.py:29
  87.6 5.2 %collective-permute-done.18 = s16[240,896]{1,0:T(8,128)(2,1)} collective-permute-done((s16[240,896]{1,0:T(8,128)(2,1)S(1)}, s16[240,896]{1,0:T(8,128)(2,1)}, u32[]{:S(2)}, u32[]{:S(2)}) %collective-permute-start.18) | collective-permute-done | bytes 430112 | tf_op jit(solution)/shard_map/ppermute | solution.py:29
  92.8 4.0 %collective-permute-start.19 = (s16[240,896]{1,0:T(8,128)(2,1)}, s16[240,896]{1,0:T(8,128)(2,1)S(1)}, u32[]{:S(2)}, u32[]{:S(2)}) collective-permute-start(s16[240,896]{1,0:T(8,128)(2,1)} %collective-permute-done.18), channel_id=1, source_target_pairs={{0,8},{1,13},{2,60},{3,57},{4,72},{5,77},{6,124},{7,121},{8,0},{9,... | collective-permute-start | bytes 1290248 | tf_op jit(solution)/shard_map/ppermute | solution.py:29
  97.0 7.6 %collective-permute-done.17.same_ref = s16[240,896]{1,0:T(8,128)(2,1)S(1)} collective-permute-done((s16[240,896]{1,0:T(8,128)(2,1)S(1)}, s16[240,896]{1,0:T(8,128)(2,1)S(1)}, u32[]{:S(2)}, u32[]{:S(2)}) %collective-permute-start.17) | collective-permute-done | bytes 430112 | tf_op jit(solution)/shard_map/ppermute | solution.py:29
  104.6 13.3 %collective-permute-done.19.cross_ref = s16[240,896]{1,0:T(8,128)(2,1)S(1)} collective-permute-done((s16[240,896]{1,0:T(8,128)(2,1)}, s16[240,896]{1,0:T(8,128)(2,1)S(1)}, u32[]{:S(2)}, u32[]{:S(2)}) %collective-permute-start.19) | collective-permute-done | bytes 430112 | tf_op jit(solution)/shard_map/ppermute | solution.py:29
  117.9 2.5 %combine.1 = f32[448,896]{1,0:T(8,128)} custom-call(f32[448,896]{1,0:T(8,128)S(1)} %get-tuple-element.36.product_ref, s16[240,896]{1,0:T(8,128)(2,1)S(1)} %collective-permute-done.17.same_ref, s16[240,896]{1,0:T(8,128)(2,1)S(1)} %collective-permute-done.19.cross_ref, f32[448,1]{1,0:T(8,128)S(1)} %copy.10.row_gap_ref, f32[1,896]{1,0:T(1,128)S(1)} %broadcast_in_dim.87.col_gap_ref), custom_call_target="tpu_custom_call" | custom-call | flops 1605632 | bytes 4816896 | tf_op jit(solution)/shard_map/combine/pallas_call | solution.py:264
  (53 shorter events, 5.9 us)
Async XLA Ops:
  0.0 3.8 %copy-start = (bf16[448,896]{1,0:T(8,128)(2,1)S(1)}, bf16[448,896]{1,0:T(8,128)(2,1)}, u32[]{:S(2)}) copy-start(bf16[448,896]{1,0:T(8,128)(2,1)} %refs_4_.1) | copy-start | bytes 2408452
  0.0 3.8 %collective-permute-start = (bf16[448,896]{1,0:T(8,128)(2,1)}, bf16[448,896]{1,0:T(8,128)(2,1)S(1)}, u32[]{:S(2)}, u32[]{:S(2)}) collective-permute-start(bf16[448,896]{1,0:T(8,128)(2,1)} %param.6), channel_id=1, source_target_pairs={{0,8},{1,9},{2,10},{3,11},{4,12},{5,13},{6,14},{7,15},{8,0},{9,1},... | collective-permute-start | bytes 2408456 | tf_op jit(solution)/shard_map/ppermute | solution.py:29
  0.7 20.1 %collective-permute-start.7 = (bf16[448,896]{1,0:T(8,128)(2,1)}, bf16[448,896]{1,0:T(8,128)(2,1)}, u32[]{:S(2)}, u32[]{:S(2)}) collective-permute-start(bf16[448,896]{1,0:T(8,128)(2,1)} %refs_4_.1), channel_id=1, source_target_pairs={{0,64},{1,65},{2,66},{3,67},{4,68},{5,69},{6,70},{7,71},{8,72},{9,... | collective-permute-start | bytes 2408456 | tf_op jit(solution)/shard_map/ppermute | solution.py:29
  2.3 4.2 %copy-start.3 = (bf16[448,896]{1,0:T(8,128)(2,1)S(1)}, bf16[448,896]{1,0:T(8,128)(2,1)}, u32[]{:S(2)}) copy-start(bf16[448,896]{1,0:T(8,128)(2,1)} %param.6) | copy-start | bytes 2408452
  3.8 20.2 %collective-permute-start.6 = (bf16[448,896]{1,0:T(8,128)(2,1)S(1)}, bf16[448,896]{1,0:T(8,128)(2,1)S(1)}, u32[]{:S(2)}, u32[]{:S(2)}) collective-permute-start(bf16[448,896]{1,0:T(8,128)(2,1)S(1)} %copy-done), channel_id=1, source_target_pairs={{0,48},{1,49},{2,50},{3,51},{4,52},{5,53},{6,54},{7,55},{8,56},{9,... | collective-permute-start | bytes 2408456 | tf_op jit(solution)/shard_map/ppermute | solution.py:29
  6.4 20.1 %collective-permute-start.5 = (bf16[448,896]{1,0:T(8,128)(2,1)S(1)}, bf16[448,896]{1,0:T(8,128)(2,1)}, u32[]{:S(2)}, u32[]{:S(2)}) collective-permute-start(bf16[448,896]{1,0:T(8,128)(2,1)S(1)} %copy-done), channel_id=1, source_target_pairs={{0,16},{1,17},{2,18},{3,19},{4,20},{5,21},{6,22},{7,23},{8,24},{9,... | collective-permute-start | bytes 2408456 | tf_op jit(solution)/shard_map/ppermute | solution.py:29
  6.6 25.6 %copy-start.4 = (s32[7168]{0:T(1024)S(1)}, s32[7168]{0:T(1024)}, u32[]{:S(2)}) copy-start(s32[7168]{0:T(1024)} %param.10) | copy-start | bytes 86020
  6.6 25.7 %copy-start.5 = (s32[7168]{0:T(1024)S(1)}, s32[7168]{0:T(1024)}, u32[]{:S(2)}) copy-start(s32[7168]{0:T(1024)} %param.11) | copy-start | bytes 86020
  7.4 25.1 %copy-start.7 = (f32[80]{0:T(128)S(1)}, f32[80]{0:T(128)}, u32[]{:S(2)}) copy-start(f32[80]{0:T(128)} %param.8) | copy-start | bytes 964
  7.4 43.2 %copy-start.6 = (f32[1000]{0:T(1024)S(1)}, f32[1000]{0:T(1024)}, u32[]{:S(2)}) copy-start(f32[1000]{0:T(1024)} %param.9) | copy-start | bytes 12004
  7.4 21.8 %collective-permute-start.2 = (bf16[448,896]{1,0:T(8,128)(2,1)S(1)}, bf16[448,896]{1,0:T(8,128)(2,1)S(1)}, u32[]{:S(2)}, u32[]{:S(2)}) collective-permute-start(bf16[448,896]{1,0:T(8,128)(2,1)S(1)} %fusion.refs_0_), channel_id=1, source_target_pairs={{0,2},{1,3},{2,4},{3,5},{4,6},{5,7},{6,0},{7,1},{8,10},{9,11},{10,... | collective-permute-start | bytes 2408456 | tf_op jit(solution)/shard_map/ppermute | solution.py:29
  7.5 22.5 %collective-permute-start.1 = (bf16[448,896]{1,0:T(8,128)(2,1)S(1)}, bf16[448,896]{1,0:T(8,128)(2,1)S(1)}, u32[]{:S(2)}, u32[]{:S(2)}) collective-permute-start(bf16[448,896]{1,0:T(8,128)(2,1)S(1)} %fusion.refs_0_), channel_id=1, source_target_pairs={{0,6},{1,7},{2,0},{3,1},{4,2},{5,3},{6,4},{7,5},{8,14},{9,15},{10,... | collective-permute-start | bytes 2408456 | tf_op jit(solution)/shard_map/ppermute | solution.py:29
  20.8 20.8 %collective-permute-start.9 = (bf16[448,896]{1,0:T(8,128)(2,1)S(1)}, bf16[448,896]{1,0:T(8,128)(2,1)}, u32[]{:S(2)}, u32[]{:S(2)}) collective-permute-start(bf16[448,896]{1,0:T(8,128)(2,1)S(1)} %fusion.refs_0_), channel_id=1, source_target_pairs={{0,1},{1,0},{2,3},{3,2},{4,5},{5,4},{6,7},{7,6},{8,9},{9,8},{10,11... | collective-permute-start | bytes 2408456 | tf_op jit(solution)/shard_map/ppermute | solution.py:29
  24.1 0.9 copy-start.1
  26.5 21.4 %collective-permute-start.8 = (bf16[448,896]{1,0:T(8,128)(2,1)}, bf16[448,896]{1,0:T(8,128)(2,1)}, u32[]{:S(2)}, u32[]{:S(2)}) collective-permute-start(bf16[448,896]{1,0:T(8,128)(2,1)} %collective-permute-done.5.refs_7_), channel_id=1, source_target_pairs={{0,16},{1,17},{2,18},{3,19},{4,20},{5,21},{6,22},{7,23},{8,24},{9,... | collective-permute-start | bytes 2408456 | tf_op jit(solution)/shard_map/ppermute | solution.py:29
  26.5 22.6 %collective-permute-start.13 = (bf16[448,896]{1,0:T(8,128)(2,1)}, bf16[448,896]{1,0:T(8,128)(2,1)}, u32[]{:S(2)}, u32[]{:S(2)}) collective-permute-start(bf16[448,896]{1,0:T(8,128)(2,1)} %collective-permute-done.7.refs_4_), channel_id=1, source_target_pairs={{0,48},{1,49},{2,50},{3,51},{4,52},{5,53},{6,54},{7,55},{8,56},{9,... | collective-permute-start | bytes 2408456 | tf_op jit(solution)/shard_map/ppermute | solution.py:29
  30.0 11.6 %collective-permute-start.3 = (bf16[224,896]{1,0:T(8,128)(2,1)}, bf16[224,896]{1,0:T(8,128)(2,1)}, u32[]{:S(2)}, u32[]{:S(2)}) collective-permute-start(bf16[224,896]{1,0:T(8,128)(2,1)} %slice.28), channel_id=1, source_target_pairs={{0,2},{1,3},{2,4},{3,5},{4,6},{5,7},{6,0},{7,1},{8,10},{9,11},{10,... | collective-permute-start | bytes 1204232 | tf_op jit(solution)/shard_map/ppermute | solution.py:29
  30.8 13.3 %collective-permute-start.4 = (bf16[224,896]{1,0:T(8,128)(2,1)}, bf16[224,896]{1,0:T(8,128)(2,1)}, u32[]{:S(2)}, u32[]{:S(2)}) collective-permute-start(bf16[224,896]{1,0:T(8,128)(2,1)} %slice.29), channel_id=1, source_target_pairs={{0,6},{1,7},{2,0},{3,1},{4,2},{5,3},{6,4},{7,5},{8,14},{9,15},{10,... | collective-permute-start | bytes 1204232 | tf_op jit(solution)/shard_map/ppermute | solution.py:29
  32.4 19.3 %copy-start.2 = (bf16[448,896]{1,0:T(8,128)(2,1)S(1)}, bf16[448,896]{1,0:T(8,128)(2,1)}, u32[]{:S(2)}) copy-start(bf16[448,896]{1,0:T(8,128)(2,1)} %copy-done.1) | copy-start | bytes 2408452
  41.6 18.2 %collective-permute-start.12 = (bf16[448,896]{1,0:T(8,128)(2,1)}, bf16[448,896]{1,0:T(8,128)(2,1)S(1)}, u32[]{:S(2)}, u32[]{:S(2)}) collective-permute-start(bf16[448,896]{1,0:T(8,128)(2,1)} %collective-permute-done.9.refs_0_), channel_id=1, source_target_pairs={{0,2},{1,3},{2,4},{3,5},{4,6},{5,7},{6,0},{7,1},{8,10},{9,11},{10,... | collective-permute-start | bytes 2408456 | tf_op jit(solution)/shard_map/ppermute | solution.py:29
  41.6 19.2 %collective-permute-start.10 = (bf16[448,896]{1,0:T(8,128)(2,1)}, bf16[448,896]{1,0:T(8,128)(2,1)S(1)}, u32[]{:S(2)}, u32[]{:S(2)}) collective-permute-start(bf16[448,896]{1,0:T(8,128)(2,1)} %collective-permute-done.9.refs_0_), channel_id=1, source_target_pairs={{0,6},{1,7},{2,0},{3,1},{4,2},{5,3},{6,4},{7,5},{8,14},{9,15},{10,... | collective-permute-start | bytes 2408456 | tf_op jit(solution)/shard_map/ppermute | solution.py:29
  45.1 19.0 %collective-permute-start.11 = (bf16[448,896]{1,0:T(8,128)(2,1)S(1)}, bf16[448,896]{1,0:T(8,128)(2,1)S(1)}, u32[]{:S(2)}, u32[]{:S(2)}) collective-permute-start(bf16[448,896]{1,0:T(8,128)(2,1)S(1)} %constant_dynamic-update-slice_fusion.refs_2_), channel_id=1, source_target_pairs={{0,1},{1,0},{2,3},{3,2},{4,5},{5,4},{6,7},{7,6},{8,9},{9,8},{10,11... | collective-permute-start | bytes 2408456 | tf_op jit(solution)/shard_map/ppermute | solution.py:29
  47.9 18.2 %collective-permute-start.15 = (bf16[448,896]{1,0:T(8,128)(2,1)}, bf16[448,896]{1,0:T(8,128)(2,1)S(1)}, u32[]{:S(2)}, u32[]{:S(2)}) collective-permute-start(bf16[448,896]{1,0:T(8,128)(2,1)} %collective-permute-done.7.refs_4_), channel_id=1, source_target_pairs={{0,16},{1,17},{2,18},{3,19},{4,20},{5,21},{6,22},{7,23},{8,24},{9,... | collective-permute-start | bytes 2408456 | tf_op jit(solution)/shard_map/ppermute | solution.py:29
  49.1 17.0 %collective-permute-start.14 = (bf16[448,896]{1,0:T(8,128)(2,1)}, bf16[448,896]{1,0:T(8,128)(2,1)S(1)}, u32[]{:S(2)}, u32[]{:S(2)}) collective-permute-start(bf16[448,896]{1,0:T(8,128)(2,1)} %collective-permute-done.13.refs_5_), channel_id=1, source_target_pairs={{0,48},{1,49},{2,50},{3,51},{4,52},{5,53},{6,54},{7,55},{8,56},{9,... | collective-permute-start | bytes 2408456 | tf_op jit(solution)/shard_map/ppermute | solution.py:29
  70.9 6.7 %collective-permute-start.16 = (f32[448,896]{1,0:T(8,128)S(1)}, f32[448,896]{1,0:T(8,128)S(1)}, u32[]{:S(2)}, u32[]{:S(2)}) collective-permute-start(f32[448,896]{1,0:T(8,128)S(1)} %get-tuple-element.35), channel_id=1, source_target_pairs={{0,8},{1,9},{2,10},{3,11},{4,12},{5,13},{6,14},{7,15},{8,0},{9,1},... | collective-permute-start | bytes 4816904 | tf_op jit(solution)/shard_map/ppermute | solution.py:29
  78.5 14.3 %collective-permute-start.18 = (s16[240,896]{1,0:T(8,128)(2,1)S(1)}, s16[240,896]{1,0:T(8,128)(2,1)}, u32[]{:S(2)}, u32[]{:S(2)}) collective-permute-start(s16[240,896]{1,0:T(8,128)(2,1)S(1)} %get-tuple-element.38), channel_id=1, source_target_pairs={{0,0},{1,80},{2,18},{3,66},{4,4},{5,84},{6,22},{7,70},{8,8},{9,88}... | collective-permute-start | bytes 1290248 | tf_op jit(solution)/shard_map/ppermute | solution.py:29
  81.6 23.0 %collective-permute-start.17 = (s16[240,896]{1,0:T(8,128)(2,1)S(1)}, s16[240,896]{1,0:T(8,128)(2,1)S(1)}, u32[]{:S(2)}, u32[]{:S(2)}) collective-permute-start(s16[240,896]{1,0:T(8,128)(2,1)S(1)} %get-tuple-element.37), channel_id=1, source_target_pairs={{0,0},{1,16},{2,32},{3,48},{4,64},{5,80},{6,96},{7,112},{8,8},{9,2... | collective-permute-start | bytes 1290248 | tf_op jit(solution)/shard_map/ppermute | solution.py:29
  92.8 25.1 %collective-permute-start.19 = (s16[240,896]{1,0:T(8,128)(2,1)}, s16[240,896]{1,0:T(8,128)(2,1)S(1)}, u32[]{:S(2)}, u32[]{:S(2)}) collective-permute-start(s16[240,896]{1,0:T(8,128)(2,1)} %collective-permute-done.18), channel_id=1, source_target_pairs={{0,8},{1,13},{2,60},{3,57},{4,72},{5,77},{6,124},{7,121},{8,0},{9,... | collective-permute-start | bytes 1290248 | tf_op jit(solution)/shard_map/ppermute | solution.py:29

commit v7 on v6

--- a/solution.py
+++ b/solution.py
@@ -49,22 +49,38 @@
     return z_lo, x, 1 - core, y, z_hi
 
 
-def mirrored(flip):
-    def target(z_lo, x, core, y, z_hi):
-        chip_row, chip_col = z_lo * X + x, y * Z_HI + z_hi
-        return chip_col // X, chip_col % X, core ^ flip, chip_row // Z_HI, chip_row % Z_HI
-
-    return target
+def chip_index(z_lo, x, y, z_hi):
+    return ((z_hi * Z_LO + z_lo) * Y + y) * X + x
+
+
+def at_chip(index, core):
+    x, y, z = index % X, index // X % Y, index // (X * Y)
+    return z % Z_LO, x, core, y, z // Z_LO
+
+
+def mirrored(z_lo, x, core, y, z_hi):
+    chip_row, chip_col = z_lo * X + x, y * Z_HI + z_hi
+    return chip_col // X, chip_col % X, core, chip_row // Z_HI, chip_row % Z_HI
+
+
+VIA = (
+    (0, 49, 53, 51, 4, 37, 6, 35, 12, 52, 43, 55, 13, 61, 14, 63,
+     3, 21, 1, 47, 7, 41, 2, 48, 24, 40, 29, 11, 25, 45, 46, 62,
+     17, 33, 54, 36, 16, 34, 22, 39, 5, 9, 26, 23, 28, 50, 30, 15,
+     8, 44, 18, 32, 27, 10, 19, 38, 56, 57, 42, 60, 20, 58, 31, 59),
+    (16, 36, 18, 7, 1, 50, 54, 26, 17, 5, 25, 59, 28, 2, 22, 3,
+     8, 32, 12, 23, 20, 38, 19, 42, 24, 9, 27, 44, 31, 10, 30, 15,
+     0, 61, 11, 34, 55, 33, 37, 39, 47, 52, 58, 40, 35, 45, 43, 56,
+     53, 13, 14, 49, 4, 41, 6, 48, 21, 57, 29, 62, 60, 51, 46, 63),
+)
 
 
 def detour(z_lo, x, core, y, z_hi):
-    x_bit = x // 2 ^ y % 2 ^ z_hi
-    return x % 2 ^ z_hi ^ z_lo, x // 2 * 2 + x_bit, core, y, x % 2
+    return at_chip(VIA[core][chip_index(z_lo, x, y, z_hi)], core)
 
 
 def after_detour(z_lo, x, core, y, z_hi):
-    start = next(place for place in places() if detour(*place) == (z_lo, x, core, y, z_hi))
-    return mirrored(1)(*start)
+    return mirrored(*at_chip(VIA[core].index(chip_index(z_lo, x, y, z_hi)), core))
 
 
 def after(block, *earlier):
@@ -173,20 +189,28 @@
             copy.wait()
     else:
         sum_ref, right_stack, left_stack, out_ref, acc = refs
+    core = lax.axis_index("row") % CORE
     depth = right_stack.shape[2] // 2
     rows = out_ref.shape[0]
-    first = 0 if own else 1
     terms = product_terms((0, 1)) + product_terms((1, 0)) + product_terms((1, 1))
-    for i, (left_slot, right_slot) in enumerate(terms):
-        block = left_stack[left_slot]
-        term = jnp.dot(
-            block[:, first * depth:(first + 1) * depth], right_stack[right_slot], preferred_element_type=jnp.float32)
-        if i == 0:
-            acc[...] = term + sum_ref[first * rows:(first + 1) * rows, :]
-        elif i < len(terms) - 1:
-            acc[...] += term
-        else:
-            out_ref[...] = acc[...] + term
+
+    def run(columns):
+        for half in range(2):
+            acc[half] = sum_ref[half * rows:(half + 1) * rows, columns]
+        for left_slot, right_slot in terms:
+            block, right = left_stack[left_slot], right_stack[right_slot][:, columns]
+            for half in range(2):
+                acc[half] += jnp.dot(
+                    block[:, half * depth:(half + 1) * depth], right, preferred_element_type=jnp.float32)
+        out_ref[...] = jnp.concatenate([acc[0], acc[1]], axis=1)
+
+    @pl.when(core == (0 if own else 1))
+    def _():
+        run(slice(0, depth))
+
+    @pl.when(core == (1 if own else 0))
+    def _():
+        run(slice(depth, 2 * depth))
 
 
 def far_product(incoming, total, right_stack, left_stack, own):
@@ -201,9 +225,9 @@
         out_shape=[out, stack, stack] if parts else out,
         in_specs=[pl.BlockSpec(memory_space=pl.ANY)] * parts + [vmem] * 3,
         out_specs=[vmem] * 3 if parts else vmem,
-        scratch_shapes=[pltpu.VMEM((rows, cols), jnp.float32)] + (sems if parts else []),
+        scratch_shapes=[pltpu.VMEM((2, rows, cols // 2), jnp.float32)] + (sems if parts else []),
         input_output_aliases={parts + 1: 1, parts + 2: 2} if parts else {},
-        compiler_params=pltpu.CompilerParams(vmem_limit_bytes=6 * MIB),
+        compiler_params=pltpu.CompilerParams(vmem_limit_bytes=10 * MIB),
         cost_estimate=pl.CostEstimate(
             flops=2 * 6 * rows * cols * cols // 2, bytes_accessed=12 * MIB, transcendentals=0),
         name="far_product",
@@ -211,56 +235,55 @@
 
 
 def encode(block, payload_ref):
-    part = block.shape[0] // 2
-    packed = jnp.concatenate([block[:part], block[part:]], axis=1)
-    top = jnp.maximum(jnp.max(jnp.abs(packed), axis=0, keepdims=True), 1e-30)
+    part = block.shape[0]
+    top = jnp.maximum(jnp.max(jnp.abs(block), axis=0, keepdims=True), 1e-30)
     power = jnp.ceil(jnp.log2(top) + 1e-3)
-    payload_ref[:part, :] = jnp.round(packed * jnp.exp2(LEVELS - power)).astype(jnp.int32).astype(jnp.int16)
-    payload_ref[part:, :] = jnp.broadcast_to(power, (16, packed.shape[1])).astype(jnp.int32).astype(jnp.int16)
+    payload_ref[:part, :] = jnp.round(block * jnp.exp2(LEVELS - power)).astype(jnp.int32).astype(jnp.int16)
+    payload_ref[part:, :] = jnp.broadcast_to(power, (16, block.shape[1])).astype(jnp.int32).astype(jnp.int16)
 
 
 def decode(payload_ref):
     part = payload_ref.shape[0] - 16
     power = payload_ref[part:, :].astype(jnp.int32).astype(jnp.float32)[:1]
-    packed = payload_ref[:part, :].astype(jnp.int32).astype(jnp.float32) * jnp.exp2(power - LEVELS)
-    width = packed.shape[1] // 2
-    return jnp.concatenate([packed[:, :width], packed[:, width:]])
-
-
-def join_kernel(keep_ref, got_ref, out_ref, same_ref, cross_ref):
-    core = lax.axis_index("row") % CORE
-    out_ref[...] = keep_ref[...] + got_ref[...]
-    half = out_ref.shape[1] // 2
-    low, high = out_ref[:, :half], out_ref[:, half:]
-    encode(jnp.where(core == 0, low, high), same_ref)
-    encode(jnp.where(core == 0, high, low), cross_ref)
+    return payload_ref[:part, :].astype(jnp.int32).astype(jnp.float32) * jnp.exp2(power - LEVELS)
+
+
+def join_kernel(keep_ref, got_ref, own_ref, other_ref, payload_ref):
+    half = keep_ref.shape[1] // 2
+    own = keep_ref[:, :half] + got_ref[:, half:]
+    other = keep_ref[:, half:] + got_ref[:, :half]
+    own_ref[...] = own
+    other_ref[...] = other
+    encode(jnp.concatenate([own, other], axis=1), payload_ref)
 
 
 def join(keep, got):
     rows, cols = keep.shape
-    payload = jax.ShapeDtypeStruct((rows // 2 + 16, cols), jnp.int16)
+    half = jax.ShapeDtypeStruct((rows, cols // 2), jnp.float32)
     vmem = pl.BlockSpec(memory_space=pltpu.VMEM)
     return pl.pallas_call(
         join_kernel,
-        out_shape=[jax.ShapeDtypeStruct((rows, cols), jnp.float32), payload, payload],
+        out_shape=[half, half, jax.ShapeDtypeStruct((rows + 16, cols), jnp.int16)],
         in_specs=[vmem] * 2,
         out_specs=[vmem] * 3,
-        compiler_params=pltpu.CompilerParams(vmem_limit_bytes=6 * MIB),
+        compiler_params=pltpu.CompilerParams(vmem_limit_bytes=8 * MIB),
         cost_estimate=pl.CostEstimate(flops=4 * rows * cols, bytes_accessed=12 * rows * cols, transcendentals=0),
         name="join",
     )(keep, got)
 
 
-def combine_kernel(product_ref, same_ref, cross_ref, row_gap_ref, col_gap_ref, out_ref):
+def combine_kernel(own_ref, side_ref, payload_ref, row_gap_ref, col_gap_ref, out_ref):
     core = lax.axis_index("row") % CORE
-    same, cross = decode(same_ref).T, decode(cross_ref).T
-    mirror = jnp.concatenate(
-        [jnp.where(core == 0, same, cross), jnp.where(core == 0, cross, same)], axis=1)
-    out_ref[...] = (product_ref[...] + mirror) / (row_gap_ref[...] + col_gap_ref[...])
-
-
-def combine(product, same, cross, row_gap, col_gap):
-    rows, cols = product.shape
+    mirror = decode(payload_ref)
+    half = mirror.shape[1] // 2
+    own = own_ref[...] + mirror[:, :half].T
+    other = side_ref[...] + mirror[:, half:].T
+    both = jnp.concatenate([jnp.where(core == 0, own, other), jnp.where(core == 0, other, own)], axis=1)
+    out_ref[...] = both / (row_gap_ref[...] + col_gap_ref[...])
+
+
+def combine(own, side, payload, row_gap, col_gap):
+    rows, cols = row_gap.shape[0], col_gap.shape[0]
     return pl.pallas_call(
         combine_kernel,
         out_shape=jax.ShapeDtypeStruct((rows, cols), jnp.float32),
@@ -269,7 +292,7 @@
         compiler_params=pltpu.CompilerParams(vmem_limit_bytes=8 * MIB),
         cost_estimate=pl.CostEstimate(flops=4 * rows * cols, bytes_accessed=12 * rows * cols, transcendentals=0),
         name="combine",
-    )(product, same, cross, row_gap[:, None], col_gap[None, :])
+    )(own, side, payload, row_gap[:, None], col_gap[None, :])
 
 
 def shards(amplitudes, integrals, occ_energy, vir_energy, pair_occ, pair_vir):
@@ -296,11 +319,10 @@
     give, right_stack, left_stack = far_product((*far, *right_far), total, right_stack, left_stack, False)
     got = send(give, across_core)
     keep = far_product((), total, right_stack, left_stack, True)
-    product, to_same, to_cross = join(keep, got)
-    same = send(to_same, mirrored(0))
-    cross = send(send(to_cross, detour), after_detour)
-
-    return combine(product, same, cross, row_gap, col_gap)
+    own, other, payload = join(keep, got)
+    payload = send(send(payload, detour), after_detour)
+    side = send(other, across_core)
+    return combine(own, side, payload, row_gap, col_gap)
 
 
 def solution(mesh):

time: 121 us -> 119 us (0.983)
  the two profiles are of different devices: /device:TPU:25 before, /device:TPU:16 now
where the time goes in v7:
time: 119 us
  waiting for transfers between devices  62.8 us (53%)
  starting transfers between devices  29.7 us (25%)
  Pallas kernels  17.2 us (14%)
  local copies, waits for them, and re-layouts  6.52 us (5%)
  other arithmetic  1.99 us (2%)
    ppermute x20, waiting for transfers between devices, send(): return lax.ppermute(block, AXES, pairs)  62.8 us
    ppermute x20, starting transfers between devices, send(): return lax.ppermute(block, AXES, pairs)  29.7 us
    pallas_call x2, Pallas kernels, far_product(): pl.pallas_call(lambda *refs: far_kernel(own, parts, *refs), out_shape=[ou...  8.85 us
    pallas_call x1, Pallas kernels, near_product(): pl.pallas_call(near_kernel, out_shape=[jax.ShapeDtypeStruct((2 * rows, co...  3.98 us
    pallas_call x1, Pallas kernels, combine(): pl.pallas_call(combine_kernel, out_shape=jax.ShapeDtypeStruct((rows, cols...  2.51 us
  transfers between devices with their start and end apart: 20, of which 10 were waited for; matrix products, arithmetic and copies ran while one was open for 6% of the time, Pallas kernels for 6%

profile of v7, /device:TPU:16, one launch (start us, length us, event | category | flops | bytes accessed | tf_op | source)
XLA Modules:
  0.0 118.5 jit_solution(17736067190437413219)
XLA Ops:
  0.0 2.0 %collective-permute-start.7 = (bf16[448,896]{1,0:T(8,128)(2,1)}, bf16[448,896]{1,0:T(8,128)(2,1)}, u32[]{:S(2)}, u32[]{:S(2)}) collective-permute-start(bf16[448,896]{1,0:T(8,128)(2,1)} %refs_4_.1), channel_id=1, source_target_pairs={{0,64},{1,65},{2,66},{3,67},{4,68},{5,69},{6,70},{7,71},{8,72},{9,... | collective-permute-start | bytes 2408456 | tf_op jit(solution)/shard_map/ppermute | solution.py:29
  2.0 1.5 %fusion.2 = (bf16[448,448]{1,0:T(8,128)(2,1)S(1)}, bf16[448,448]{1,0:T(8,128)(2,1)S(1)}) fusion(bf16[448,896]{1,0:T(8,128)(2,1)} %param.6), kind=kLoop, calls=%fused_computation.21 | loop fusion | bytes 1605632 | tf_op jit(solution)/shard_map/jit(_roll_static)/slice | solution.py:306
  3.5 2.8 %collective-permute-start.6 = (bf16[448,896]{1,0:T(8,128)(2,1)S(1)}, bf16[448,896]{1,0:T(8,128)(2,1)S(1)}, u32[]{:S(2)}, u32[]{:S(2)}) collective-permute-start(bf16[448,896]{1,0:T(8,128)(2,1)S(1)} %copy-done), channel_id=1, source_target_pairs={{0,48},{1,49},{2,50},{3,51},{4,52},{5,53},{6,54},{7,55},{8,56},{9,... | collective-permute-start | bytes 2408456 | tf_op jit(solution)/shard_map/ppermute | solution.py:29
  7.4 1.4 %collective-permute-start.2 = (bf16[448,896]{1,0:T(8,128)(2,1)S(1)}, bf16[448,896]{1,0:T(8,128)(2,1)S(1)}, u32[]{:S(2)}, u32[]{:S(2)}) collective-permute-start(bf16[448,896]{1,0:T(8,128)(2,1)S(1)} %fusion.refs_0_), channel_id=1, source_target_pairs={{0,2},{1,3},{2,4},{3,5},{4,6},{5,7},{6,0},{7,1},{8,10},{9,11},{10,... | collective-permute-start | bytes 2408456 | tf_op jit(solution)/shard_map/ppermute | solution.py:29
  9.4 11.4 %collective-permute-done.7.refs_4_ = bf16[448,896]{1,0:T(8,128)(2,1)} collective-permute-done((bf16[448,896]{1,0:T(8,128)(2,1)}, bf16[448,896]{1,0:T(8,128)(2,1)}, u32[]{:S(2)}, u32[]{:S(2)}) %collective-permute-start.7) | collective-permute-done | bytes 802848 | tf_op jit(solution)/shard_map/ppermute | solution.py:29
  20.8 3.7 %collective-permute-start.9 = (bf16[448,896]{1,0:T(8,128)(2,1)S(1)}, bf16[448,896]{1,0:T(8,128)(2,1)}, u32[]{:S(2)}, u32[]{:S(2)}) collective-permute-start(bf16[448,896]{1,0:T(8,128)(2,1)S(1)} %fusion.refs_0_), channel_id=1, source_target_pairs={{0,1},{1,0},{2,3},{3,2},{4,5},{5,4},{6,7},{7,6},{8,9},{9,8},{10,11... | collective-permute-start | bytes 2408456 | tf_op jit(solution)/shard_map/ppermute | solution.py:29
  24.5 0.9 copy-done.1
  25.4 1.9 %collective-permute-done.5.refs_7_ = bf16[448,896]{1,0:T(8,128)(2,1)} collective-permute-done((bf16[448,896]{1,0:T(8,128)(2,1)S(1)}, bf16[448,896]{1,0:T(8,128)(2,1)}, u32[]{:S(2)}, u32[]{:S(2)}) %collective-permute-start.5) | collective-permute-done | bytes 802848 | tf_op jit(solution)/shard_map/ppermute | solution.py:29
  27.3 3.2 %collective-permute-start.13 = (bf16[448,896]{1,0:T(8,128)(2,1)}, bf16[448,896]{1,0:T(8,128)(2,1)}, u32[]{:S(2)}, u32[]{:S(2)}) collective-permute-start(bf16[448,896]{1,0:T(8,128)(2,1)} %collective-permute-done.7.refs_4_), channel_id=1, source_target_pairs={{0,48},{1,49},{2,50},{3,51},{4,52},{5,53},{6,54},{7,55},{8,56},{9,... | collective-permute-start | bytes 2408456 | tf_op jit(solution)/shard_map/ppermute | solution.py:29
  31.3 1.3 %collective-permute-start.3 = (bf16[224,896]{1,0:T(8,128)(2,1)}, bf16[224,896]{1,0:T(8,128)(2,1)}, u32[]{:S(2)}, u32[]{:S(2)}) collective-permute-start(bf16[224,896]{1,0:T(8,128)(2,1)} %slice.28), channel_id=1, source_target_pairs={{0,2},{1,3},{2,4},{3,5},{4,6},{5,7},{6,0},{7,1},{8,10},{9,11},{10,... | collective-permute-start | bytes 1204232 | tf_op jit(solution)/shard_map/ppermute | solution.py:29
  32.6 0.8 slice.29
  34.5 7.8 %collective-permute-done.9.refs_0_ = bf16[448,896]{1,0:T(8,128)(2,1)} collective-permute-done((bf16[448,896]{1,0:T(8,128)(2,1)S(1)}, bf16[448,896]{1,0:T(8,128)(2,1)}, u32[]{:S(2)}, u32[]{:S(2)}) %collective-permute-start.9) | collective-permute-done | bytes 802848 | tf_op jit(solution)/shard_map/ppermute | solution.py:29
  42.3 1.3 %collective-permute-start.12 = (bf16[448,896]{1,0:T(8,128)(2,1)}, bf16[448,896]{1,0:T(8,128)(2,1)S(1)}, u32[]{:S(2)}, u32[]{:S(2)}) collective-permute-start(bf16[448,896]{1,0:T(8,128)(2,1)} %collective-permute-done.9.refs_0_), channel_id=1, source_target_pairs={{0,2},{1,3},{2,4},{3,5},{4,6},{5,7},{6,0},{7,1},{8,10},{9,11},{10,... | collective-permute-start | bytes 2408456 | tf_op jit(solution)/shard_map/ppermute | solution.py:29
  44.4 1.0 constant_dynamic-update-slice_fusion.1
  45.4 1.0 constant_dynamic-update-slice_fusion.refs_2_
  46.5 3.3 %collective-permute-start.11 = (bf16[448,896]{1,0:T(8,128)(2,1)S(1)}, bf16[448,896]{1,0:T(8,128)(2,1)S(1)}, u32[]{:S(2)}, u32[]{:S(2)}) collective-permute-start(bf16[448,896]{1,0:T(8,128)(2,1)S(1)} %constant_dynamic-update-slice_fusion.refs_2_), channel_id=1, source_target_pairs={{0,1},{1,0},{2,3},{3,2},{4,5},{5,4},{6,7},{7,6},{8,9},{9,8},{10,11... | collective-permute-start | bytes 2408456 | tf_op jit(solution)/shard_map/ppermute | solution.py:29
  49.8 1.5 %collective-permute-start.15 = (bf16[448,896]{1,0:T(8,128)(2,1)}, bf16[448,896]{1,0:T(8,128)(2,1)S(1)}, u32[]{:S(2)}, u32[]{:S(2)}) collective-permute-start(bf16[448,896]{1,0:T(8,128)(2,1)} %collective-permute-done.7.refs_4_), channel_id=1, source_target_pairs={{0,16},{1,17},{2,18},{3,19},{4,20},{5,21},{6,22},{7,23},{8,24},{9,... | collective-permute-start | bytes 2408456 | tf_op jit(solution)/shard_map/ppermute | solution.py:29
  51.3 1.7 %collective-permute-start.14 = (bf16[448,896]{1,0:T(8,128)(2,1)}, bf16[448,896]{1,0:T(8,128)(2,1)S(1)}, u32[]{:S(2)}, u32[]{:S(2)}) collective-permute-start(bf16[448,896]{1,0:T(8,128)(2,1)} %collective-permute-done.13.refs_5_), channel_id=1, source_target_pairs={{0,48},{1,49},{2,50},{3,51},{4,52},{5,53},{6,54},{7,55},{8,56},{9,... | collective-permute-start | bytes 2408456 | tf_op jit(solution)/shard_map/ppermute | solution.py:29
  54.1 4.0 %near_product.1 = (f32[896,896]{1,0:T(8,128)S(1)}, bf16[8,448,896]{2,1,0:T(8,128)(2,1)S(1)}, bf16[8,448,896]{2,1,0:T(8,128)(2,1)S(1)}) custom-call(bf16[448,896]{1,0:T(8,128)(2,1)S(1)} %fusion.refs_0_, bf16[448,896]{1,0:T(8,128)(2,1)S(1)} %collective-permute-done.1.refs_1_, bf16[448,896]{1,0:T(8,128)(2,1)S(1)} %constant_dynamic-update-slice_fusion.refs_2_, ...), custom_call_target="tpu_custom_call" | custom-call | flops 1438646272 | bytes 12582912 | tf_op jit(solution)/shard_map/near_product/pallas_call | solution.py:163
  58.1 3.3 %collective-permute-done.12.refs_3_ = bf16[448,896]{1,0:T(8,128)(2,1)S(1)} collective-permute-done((bf16[448,896]{1,0:T(8,128)(2,1)}, bf16[448,896]{1,0:T(8,128)(2,1)S(1)}, u32[]{:S(2)}, u32[]{:S(2)}) %collective-permute-start.12) | collective-permute-done | bytes 802848 | tf_op jit(solution)/shard_map/ppermute | solution.py:29
  61.4 1.0 collective-permute-done.10.refs_1_
  62.4 3.9 %collective-permute-done.11.refs_2_ = bf16[448,896]{1,0:T(8,128)(2,1)S(1)} collective-permute-done((bf16[448,896]{1,0:T(8,128)(2,1)S(1)}, bf16[448,896]{1,0:T(8,128)(2,1)S(1)}, u32[]{:S(2)}, u32[]{:S(2)}) %collective-permute-start.11) | collective-permute-done | bytes 802848 | tf_op jit(solution)/shard_map/ppermute | solution.py:29
  66.4 2.6 %collective-permute-done.15.refs_7_ = bf16[448,896]{1,0:T(8,128)(2,1)S(1)} collective-permute-done((bf16[448,896]{1,0:T(8,128)(2,1)}, bf16[448,896]{1,0:T(8,128)(2,1)S(1)}, u32[]{:S(2)}, u32[]{:S(2)}) %collective-permute-start.15) | collective-permute-done | bytes 802848 | tf_op jit(solution)/shard_map/ppermute | solution.py:29
  68.9 5.3 %far_product.2 = (f32[448,896]{1,0:T(8,128)S(1)}, bf16[8,448,896]{2,1,0:T(8,128)(2,1)S(1)}, bf16[8,448,896]{2,1,0:T(8,128)(2,1)S(1)}) custom-call(bf16[448,896]{1,0:T(8,128)(2,1)} %collective-permute-done.9.refs_0_, bf16[448,896]{1,0:T(8,128)(2,1)S(1)} %collective-permute-done.10.refs_1_, ...), custom_call_target="tpu_custom_call", output_to_operand_aliasing={{1}: (9, {}), {2}: (10, {})} | custom-call | flops 2157969408 | bytes 12582912 | tf_op jit(solution)/shard_map/far_product/pallas_call | solution.py:223
  74.4 3.5 %far_product.3.keep_ref = f32[448,896]{1,0:T(8,128)S(1)} custom-call(f32[896,896]{1,0:T(8,128)S(1)} %get-tuple-element.27.refs_8_.refs_0_, bf16[8,448,896]{2,1,0:T(8,128)(2,1)S(1)} %get-tuple-element.33.refs_1_, bf16[8,448,896]{2,1,0:T(8,128)(2,1)S(1)} %get-tuple-element.34.refs_2_), custom_call_target="tpu_custom_call" | custom-call | flops 2157969408 | bytes 12582912 | tf_op jit(solution)/shard_map/far_product/pallas_call | solution.py:223
  77.9 1.8 %join.1 = (f32[448,448]{1,0:T(8,128)S(1)}, f32[448,448]{1,0:T(8,128)}, s16[464,896]{1,0:T(8,128)(2,1)S(1)}) custom-call(f32[448,896]{1,0:T(8,128)S(1)} %far_product.3.keep_ref, f32[448,896]{1,0:T(8,128)S(1)} %collective-permute-done.16.got_ref), custom_call_target="tpu_custom_call" | custom-call | flops 1605632 | bytes 4816896 | tf_op jit(solution)/shard_map/join/pallas_call | solution.py:264
  79.8 3.2 %collective-permute-start.18 = (s16[464,896]{1,0:T(8,128)(2,1)S(1)}, s16[464,896]{1,0:T(8,128)(2,1)}, u32[]{:S(2)}, u32[]{:S(2)}) collective-permute-start(s16[464,896]{1,0:T(8,128)(2,1)S(1)} %get-tuple-element.38), channel_id=1, source_target_pairs={{0,0},{1,80},{2,2},{3,64},{4,6},{5,18},{6,22},{7,70},{8,72},{9,8},... | collective-permute-start | bytes 2494472 | tf_op jit(solution)/shard_map/ppermute | solution.py:29
  82.9 14.9 %collective-permute-done.18 = s16[464,896]{1,0:T(8,128)(2,1)} collective-permute-done((s16[464,896]{1,0:T(8,128)(2,1)S(1)}, s16[464,896]{1,0:T(8,128)(2,1)}, u32[]{:S(2)}, u32[]{:S(2)}) %collective-permute-start.18) | collective-permute-done | bytes 831520 | tf_op jit(solution)/shard_map/ppermute | solution.py:29
  97.8 1.9 %collective-permute-start.19 = (s16[464,896]{1,0:T(8,128)(2,1)}, s16[464,896]{1,0:T(8,128)(2,1)S(1)}, u32[]{:S(2)}, u32[]{:S(2)}) collective-permute-start(s16[464,896]{1,0:T(8,128)(2,1)} %collective-permute-done.18), channel_id=1, source_target_pairs={{0,0},{1,23},{2,32},{3,19},{4,20},{5,69},{6,64},{7,21},{8,24},{9,1... | collective-permute-start | bytes 2494472 | tf_op jit(solution)/shard_map/ppermute | solution.py:29
  100.0 2.5 %collective-permute-done.17.side_ref = f32[448,448]{1,0:T(8,128)S(1)} collective-permute-done((f32[448,448]{1,0:T(8,128)}, f32[448,448]{1,0:T(8,128)S(1)}, u32[]{:S(2)}, u32[]{:S(2)}) %collective-permute-start.17) | collective-permute-done | bytes 802848 | tf_op jit(solution)/shard_map/ppermute | solution.py:29
  102.5 13.5 %collective-permute-done.19.payload_ref = s16[464,896]{1,0:T(8,128)(2,1)S(1)} collective-permute-done((s16[464,896]{1,0:T(8,128)(2,1)}, s16[464,896]{1,0:T(8,128)(2,1)S(1)}, u32[]{:S(2)}, u32[]{:S(2)}) %collective-permute-start.19) | collective-permute-done | bytes 831520 | tf_op jit(solution)/shard_map/ppermute | solution.py:29
  116.0 2.5 %combine.1 = f32[448,896]{1,0:T(8,128)} custom-call(f32[448,448]{1,0:T(8,128)S(1)} %get-tuple-element.36.own_ref, f32[448,448]{1,0:T(8,128)S(1)} %collective-permute-done.17.side_ref, s16[464,896]{1,0:T(8,128)(2,1)S(1)} %collective-permute-done.19.payload_ref, f32[448,1]{1,0:T(8,128)S(1)} %copy.10.row_gap_ref, f32[1,896]{1,0:T(1,128)S(1)} %broadcast_in_dim.87.col_gap_ref), custom_call_target="tpu_custom_call" | custom-call | flops 1605632 | bytes 4816896 | tf_op jit(solution)/shard_map/combine/pallas_call | solution.py:287
  (53 shorter events, 5.8 us)
Async XLA Ops:
  0.0 3.5 %copy-start = (bf16[448,896]{1,0:T(8,128)(2,1)S(1)}, bf16[448,896]{1,0:T(8,128)(2,1)}, u32[]{:S(2)}) copy-start(bf16[448,896]{1,0:T(8,128)(2,1)} %refs_4_.1) | copy-start | bytes 2408452
  0.0 3.5 %collective-permute-start = (bf16[448,896]{1,0:T(8,128)(2,1)}, bf16[448,896]{1,0:T(8,128)(2,1)S(1)}, u32[]{:S(2)}, u32[]{:S(2)}) collective-permute-start(bf16[448,896]{1,0:T(8,128)(2,1)} %param.6), channel_id=1, source_target_pairs={{0,8},{1,9},{2,10},{3,11},{4,12},{5,13},{6,14},{7,15},{8,0},{9,1},... | collective-permute-start | bytes 2408456 | tf_op jit(solution)/shard_map/ppermute | solution.py:29
  0.0 20.8 %collective-permute-start.7 = (bf16[448,896]{1,0:T(8,128)(2,1)}, bf16[448,896]{1,0:T(8,128)(2,1)}, u32[]{:S(2)}, u32[]{:S(2)}) collective-permute-start(bf16[448,896]{1,0:T(8,128)(2,1)} %refs_4_.1), channel_id=1, source_target_pairs={{0,64},{1,65},{2,66},{3,67},{4,68},{5,69},{6,70},{7,71},{8,72},{9,... | collective-permute-start | bytes 2408456 | tf_op jit(solution)/shard_map/ppermute | solution.py:29
  2.0 4.5 %copy-start.3 = (bf16[448,896]{1,0:T(8,128)(2,1)S(1)}, bf16[448,896]{1,0:T(8,128)(2,1)}, u32[]{:S(2)}) copy-start(bf16[448,896]{1,0:T(8,128)(2,1)} %param.6) | copy-start | bytes 2408452
  3.5 21.0 %collective-permute-start.6 = (bf16[448,896]{1,0:T(8,128)(2,1)S(1)}, bf16[448,896]{1,0:T(8,128)(2,1)S(1)}, u32[]{:S(2)}, u32[]{:S(2)}) collective-permute-start(bf16[448,896]{1,0:T(8,128)(2,1)S(1)} %copy-done), channel_id=1, source_target_pairs={{0,48},{1,49},{2,50},{3,51},{4,52},{5,53},{6,54},{7,55},{8,56},{9,... | collective-permute-start | bytes 2408456 | tf_op jit(solution)/shard_map/ppermute | solution.py:29
  6.3 21.0 %collective-permute-start.5 = (bf16[448,896]{1,0:T(8,128)(2,1)S(1)}, bf16[448,896]{1,0:T(8,128)(2,1)}, u32[]{:S(2)}, u32[]{:S(2)}) collective-permute-start(bf16[448,896]{1,0:T(8,128)(2,1)S(1)} %copy-done), channel_id=1, source_target_pairs={{0,16},{1,17},{2,18},{3,19},{4,20},{5,21},{6,22},{7,23},{8,24},{9,... | collective-permute-start | bytes 2408456 | tf_op jit(solution)/shard_map/ppermute | solution.py:29
  6.5 27.6 %copy-start.4 = (s32[7168]{0:T(1024)S(1)}, s32[7168]{0:T(1024)}, u32[]{:S(2)}) copy-start(s32[7168]{0:T(1024)} %param.10) | copy-start | bytes 86020
  6.6 27.7 %copy-start.5 = (s32[7168]{0:T(1024)S(1)}, s32[7168]{0:T(1024)}, u32[]{:S(2)}) copy-start(s32[7168]{0:T(1024)} %param.11) | copy-start | bytes 86020
  7.3 27.1 %copy-start.7 = (f32[80]{0:T(128)S(1)}, f32[80]{0:T(128)}, u32[]{:S(2)}) copy-start(f32[80]{0:T(128)} %param.8) | copy-start | bytes 964
  7.3 45.7 %copy-start.6 = (f32[1000]{0:T(1024)S(1)}, f32[1000]{0:T(1024)}, u32[]{:S(2)}) copy-start(f32[1000]{0:T(1024)} %param.9) | copy-start | bytes 12004
  7.4 23.2 %collective-permute-start.2 = (bf16[448,896]{1,0:T(8,128)(2,1)S(1)}, bf16[448,896]{1,0:T(8,128)(2,1)S(1)}, u32[]{:S(2)}, u32[]{:S(2)}) collective-permute-start(bf16[448,896]{1,0:T(8,128)(2,1)S(1)} %fusion.refs_0_), channel_id=1, source_target_pairs={{0,2},{1,3},{2,4},{3,5},{4,6},{5,7},{6,0},{7,1},{8,10},{9,11},{10,... | collective-permute-start | bytes 2408456 | tf_op jit(solution)/shard_map/ppermute | solution.py:29
  8.7 23.9 %collective-permute-start.1 = (bf16[448,896]{1,0:T(8,128)(2,1)S(1)}, bf16[448,896]{1,0:T(8,128)(2,1)S(1)}, u32[]{:S(2)}, u32[]{:S(2)}) collective-permute-start(bf16[448,896]{1,0:T(8,128)(2,1)S(1)} %fusion.refs_0_), channel_id=1, source_target_pairs={{0,6},{1,7},{2,0},{3,1},{4,2},{5,3},{6,4},{7,5},{8,14},{9,15},{10,... | collective-permute-start | bytes 2408456 | tf_op jit(solution)/shard_map/ppermute | solution.py:29
  20.8 21.5 %collective-permute-start.9 = (bf16[448,896]{1,0:T(8,128)(2,1)S(1)}, bf16[448,896]{1,0:T(8,128)(2,1)}, u32[]{:S(2)}, u32[]{:S(2)}) collective-permute-start(bf16[448,896]{1,0:T(8,128)(2,1)S(1)} %fusion.refs_0_), channel_id=1, source_target_pairs={{0,1},{1,0},{2,3},{3,2},{4,5},{5,4},{6,7},{7,6},{8,9},{9,8},{10,11... | collective-permute-start | bytes 2408456 | tf_op jit(solution)/shard_map/ppermute | solution.py:29
  24.5 0.9 copy-start.1
  27.3 22.5 %collective-permute-start.8 = (bf16[448,896]{1,0:T(8,128)(2,1)}, bf16[448,896]{1,0:T(8,128)(2,1)}, u32[]{:S(2)}, u32[]{:S(2)}) collective-permute-start(bf16[448,896]{1,0:T(8,128)(2,1)} %collective-permute-done.5.refs_7_), channel_id=1, source_target_pairs={{0,16},{1,17},{2,18},{3,19},{4,20},{5,21},{6,22},{7,23},{8,24},{9,... | collective-permute-start | bytes 2408456 | tf_op jit(solution)/shard_map/ppermute | solution.py:29
  27.3 24.0 %collective-permute-start.13 = (bf16[448,896]{1,0:T(8,128)(2,1)}, bf16[448,896]{1,0:T(8,128)(2,1)}, u32[]{:S(2)}, u32[]{:S(2)}) collective-permute-start(bf16[448,896]{1,0:T(8,128)(2,1)} %collective-permute-done.7.refs_4_), channel_id=1, source_target_pairs={{0,48},{1,49},{2,50},{3,51},{4,52},{5,53},{6,54},{7,55},{8,56},{9,... | collective-permute-start | bytes 2408456 | tf_op jit(solution)/shard_map/ppermute | solution.py:29
  31.3 12.3 %collective-permute-start.3 = (bf16[224,896]{1,0:T(8,128)(2,1)}, bf16[224,896]{1,0:T(8,128)(2,1)}, u32[]{:S(2)}, u32[]{:S(2)}) collective-permute-start(bf16[224,896]{1,0:T(8,128)(2,1)} %slice.28), channel_id=1, source_target_pairs={{0,2},{1,3},{2,4},{3,5},{4,6},{5,7},{6,0},{7,1},{8,10},{9,11},{10,... | collective-permute-start | bytes 1204232 | tf_op jit(solution)/shard_map/ppermute | solution.py:29
  33.4 12.0 %collective-permute-start.4 = (bf16[224,896]{1,0:T(8,128)(2,1)}, bf16[224,896]{1,0:T(8,128)(2,1)}, u32[]{:S(2)}, u32[]{:S(2)}) collective-permute-start(bf16[224,896]{1,0:T(8,128)(2,1)} %slice.29), channel_id=1, source_target_pairs={{0,6},{1,7},{2,0},{3,1},{4,2},{5,3},{6,4},{7,5},{8,14},{9,15},{10,... | collective-permute-start | bytes 1204232 | tf_op jit(solution)/shard_map/ppermute | solution.py:29
  34.3 19.8 %copy-start.2 = (bf16[448,896]{1,0:T(8,128)(2,1)S(1)}, bf16[448,896]{1,0:T(8,128)(2,1)}, u32[]{:S(2)}) copy-start(bf16[448,896]{1,0:T(8,128)(2,1)} %copy-done.1) | copy-start | bytes 2408452
  42.3 19.1 %collective-permute-start.12 = (bf16[448,896]{1,0:T(8,128)(2,1)}, bf16[448,896]{1,0:T(8,128)(2,1)S(1)}, u32[]{:S(2)}, u32[]{:S(2)}) collective-permute-start(bf16[448,896]{1,0:T(8,128)(2,1)} %collective-permute-done.9.refs_0_), channel_id=1, source_target_pairs={{0,2},{1,3},{2,4},{3,5},{4,6},{5,7},{6,0},{7,1},{8,10},{9,11},{10,... | collective-permute-start | bytes 2408456 | tf_op jit(solution)/shard_map/ppermute | solution.py:29
  43.6 18.8 %collective-permute-start.10 = (bf16[448,896]{1,0:T(8,128)(2,1)}, bf16[448,896]{1,0:T(8,128)(2,1)S(1)}, u32[]{:S(2)}, u32[]{:S(2)}) collective-permute-start(bf16[448,896]{1,0:T(8,128)(2,1)} %collective-permute-done.9.refs_0_), channel_id=1, source_target_pairs={{0,6},{1,7},{2,0},{3,1},{4,2},{5,3},{6,4},{7,5},{8,14},{9,15},{10,... | collective-permute-start | bytes 2408456 | tf_op jit(solution)/shard_map/ppermute | solution.py:29
  46.5 19.9 %collective-permute-start.11 = (bf16[448,896]{1,0:T(8,128)(2,1)S(1)}, bf16[448,896]{1,0:T(8,128)(2,1)S(1)}, u32[]{:S(2)}, u32[]{:S(2)}) collective-permute-start(bf16[448,896]{1,0:T(8,128)(2,1)S(1)} %constant_dynamic-update-slice_fusion.refs_2_), channel_id=1, source_target_pairs={{0,1},{1,0},{2,3},{3,2},{4,5},{5,4},{6,7},{7,6},{8,9},{9,8},{10,11... | collective-permute-start | bytes 2408456 | tf_op jit(solution)/shard_map/ppermute | solution.py:29
  49.8 19.1 %collective-permute-start.15 = (bf16[448,896]{1,0:T(8,128)(2,1)}, bf16[448,896]{1,0:T(8,128)(2,1)S(1)}, u32[]{:S(2)}, u32[]{:S(2)}) collective-permute-start(bf16[448,896]{1,0:T(8,128)(2,1)} %collective-permute-done.7.refs_4_), channel_id=1, source_target_pairs={{0,16},{1,17},{2,18},{3,19},{4,20},{5,21},{6,22},{7,23},{8,24},{9,... | collective-permute-start | bytes 2408456 | tf_op jit(solution)/shard_map/ppermute | solution.py:29
  51.3 17.7 %collective-permute-start.14 = (bf16[448,896]{1,0:T(8,128)(2,1)}, bf16[448,896]{1,0:T(8,128)(2,1)S(1)}, u32[]{:S(2)}, u32[]{:S(2)}) collective-permute-start(bf16[448,896]{1,0:T(8,128)(2,1)} %collective-permute-done.13.refs_5_), channel_id=1, source_target_pairs={{0,48},{1,49},{2,50},{3,51},{4,52},{5,53},{6,54},{7,55},{8,56},{9,... | collective-permute-start | bytes 2408456 | tf_op jit(solution)/shard_map/ppermute | solution.py:29
  74.3 3.6 %collective-permute-start.16 = (f32[448,896]{1,0:T(8,128)S(1)}, f32[448,896]{1,0:T(8,128)S(1)}, u32[]{:S(2)}, u32[]{:S(2)}) collective-permute-start(f32[448,896]{1,0:T(8,128)S(1)} %get-tuple-element.35), channel_id=1, source_target_pairs={{0,8},{1,9},{2,10},{3,11},{4,12},{5,13},{6,14},{7,15},{8,0},{9,1},... | collective-permute-start | bytes 4816904 | tf_op jit(solution)/shard_map/ppermute | solution.py:29
  79.8 18.1 %collective-permute-start.18 = (s16[464,896]{1,0:T(8,128)(2,1)S(1)}, s16[464,896]{1,0:T(8,128)(2,1)}, u32[]{:S(2)}, u32[]{:S(2)}) collective-permute-start(s16[464,896]{1,0:T(8,128)(2,1)S(1)} %get-tuple-element.38), channel_id=1, source_target_pairs={{0,0},{1,80},{2,2},{3,64},{4,6},{5,18},{6,22},{7,70},{8,72},{9,8},... | collective-permute-start | bytes 2494472 | tf_op jit(solution)/shard_map/ppermute | solution.py:29
  97.8 18.2 %collective-permute-start.19 = (s16[464,896]{1,0:T(8,128)(2,1)}, s16[464,896]{1,0:T(8,128)(2,1)S(1)}, u32[]{:S(2)}, u32[]{:S(2)}) collective-permute-start(s16[464,896]{1,0:T(8,128)(2,1)} %collective-permute-done.18), channel_id=1, source_target_pairs={{0,0},{1,23},{2,32},{3,19},{4,20},{5,69},{6,64},{7,21},{8,24},{9,1... | collective-permute-start | bytes 2494472 | tf_op jit(solution)/shard_map/ppermute | solution.py:29
  99.7 2.8 %collective-permute-start.17 = (f32[448,448]{1,0:T(8,128)}, f32[448,448]{1,0:T(8,128)S(1)}, u32[]{:S(2)}, u32[]{:S(2)}) collective-permute-start(f32[448,448]{1,0:T(8,128)} %get-tuple-element.37), channel_id=1, source_target_pairs={{0,8},{1,9},{2,10},{3,11},{4,12},{5,13},{6,14},{7,15},{8,0},{9,1},... | collective-permute-start | bytes 2408456 | tf_op jit(solution)/shard_map/ppermute | solution.py:29

commit v8 on v7

--- a/solution.py
+++ b/solution.py
@@ -103,8 +103,9 @@
     left_z_up, left_z_down = send(left_z, along_y(1)), send(left_z, along_y(-1))
     left_z_two = send(left_two, across_z_hi)
     near = [left, left_down, left_two, left_up]
-    far = [left_z, left_z_down, left_z_two, left_z_up]
-    return near, far, [right, right_down, right_two, right_up], [right_z, right_z_down, right_z_two, right_z_up]
+    far = [left_z_down, left_z_two, left_z_up]
+    return (
+        [*near, left_z], far, [right, right_down, right_two, right_up, right_z, right_z_down], [right_z_two, right_z_up])
 
 
 def block_of(values, index, count):
@@ -138,8 +139,9 @@
     return terms
 
 
-def near_kernel(*refs):
-    left, right, (sum_ref, stack_ref, left_stack, acc, sem_left, sem_right) = refs[:Y], refs[Y:Y + X], refs[Y + X:]
+def near_kernel(left_count, right_count, *refs):
+    left, right, refs = refs[:left_count], refs[left_count:left_count + right_count], refs[left_count + right_count:]
+    sum_ref, stack_ref, left_stack, acc, sem_left, sem_right = refs
     depth = stack_ref.shape[2] // 2
     copies = copies_into(left_stack, 0, left, sem_left) + copies_into(stack_ref, 0, right, sem_right)
     for copy in copies:
@@ -161,14 +163,14 @@
     vmem = pl.BlockSpec(memory_space=pltpu.VMEM)
     stack = jax.ShapeDtypeStruct((2 * X, rows, cols), jnp.bfloat16)
     return pl.pallas_call(
-        near_kernel,
+        lambda *refs: near_kernel(len(left), len(right), *refs),
         out_shape=[jax.ShapeDtypeStruct((2 * rows, cols), jnp.float32), stack, stack],
-        in_specs=[pl.BlockSpec(memory_space=pl.ANY)] * (X + Y),
+        in_specs=[pl.BlockSpec(memory_space=pl.ANY)] * (len(left) + len(right)),
         out_specs=[vmem] * 3,
         scratch_shapes=[
             pltpu.VMEM((2 * rows, cols), jnp.float32),
-            pltpu.SemaphoreType.DMA((Y,)),
-            pltpu.SemaphoreType.DMA((X,)),
+            pltpu.SemaphoreType.DMA((len(left),)),
+            pltpu.SemaphoreType.DMA((len(right),)),
         ],
         compiler_params=pltpu.CompilerParams(vmem_limit_bytes=10 * MIB),
         cost_estimate=pl.CostEstimate(
@@ -177,27 +179,32 @@
     )(*left, *right)
 
 
-def far_kernel(own, parts, *refs):
+def far_kernel(own, left_count, right_count, *refs):
+    parts = left_count + right_count
     incoming, refs = refs[:parts], refs[parts:]
+    left_copies = []
     if parts:
         sum_ref, _, _, out_ref, right_stack, left_stack, acc, sem_left, sem_right = refs
-        copies = copies_into(left_stack, Y, incoming[:Y], sem_left)
-        copies += copies_into(right_stack, X, incoming[Y:], sem_right)
-        for copy in copies:
+        left_copies = copies_into(left_stack, 2 * Y - left_count, incoming[:left_count], sem_left)
+        right_copies = copies_into(right_stack, 2 * X - right_count, incoming[left_count:], sem_right)
+        for copy in right_copies + left_copies:
             copy.start()
-        for copy in copies:
+        for copy in right_copies:
             copy.wait()
     else:
         sum_ref, right_stack, left_stack, out_ref, acc = refs
     core = lax.axis_index("row") % CORE
     depth = right_stack.shape[2] // 2
     rows = out_ref.shape[0]
-    terms = product_terms((0, 1)) + product_terms((1, 0)) + product_terms((1, 1))
+    near_terms, far_terms = product_terms((0, 1)), product_terms((1, 0)) + product_terms((1, 1))
 
     def run(columns):
         for half in range(2):
             acc[half] = sum_ref[half * rows:(half + 1) * rows, columns]
-        for left_slot, right_slot in terms:
+        for i, (left_slot, right_slot) in enumerate(near_terms + far_terms):
+            if i == len(near_terms):
+                for copy in left_copies:
+                    copy.wait()
             block, right = left_stack[left_slot], right_stack[right_slot][:, columns]
             for half in range(2):
                 acc[half] += jnp.dot(
@@ -213,15 +220,15 @@
         run(slice(depth, 2 * depth))
 
 
-def far_product(incoming, total, right_stack, left_stack, own):
+def far_product(left, right, total, right_stack, left_stack, own):
     rows, cols = right_stack.shape[1:]
-    parts = len(incoming)
+    parts = len(left) + len(right)
     vmem = pl.BlockSpec(memory_space=pltpu.VMEM)
     stack = jax.ShapeDtypeStruct(right_stack.shape, right_stack.dtype)
     out = jax.ShapeDtypeStruct((rows, cols), jnp.float32)
-    sems = [pltpu.SemaphoreType.DMA((Y,)), pltpu.SemaphoreType.DMA((X,))]
+    sems = [pltpu.SemaphoreType.DMA((max(len(left), 1),)), pltpu.SemaphoreType.DMA((max(len(right), 1),))]
     return pl.pallas_call(
-        lambda *refs: far_kernel(own, parts, *refs),
+        lambda *refs: far_kernel(own, len(left), len(right), *refs),
         out_shape=[out, stack, stack] if parts else out,
         in_specs=[pl.BlockSpec(memory_space=pl.ANY)] * parts + [vmem] * 3,
         out_specs=[vmem] * 3 if parts else vmem,
@@ -231,7 +238,7 @@
         cost_estimate=pl.CostEstimate(
             flops=2 * 6 * rows * cols * cols // 2, bytes_accessed=12 * MIB, transcendentals=0),
         name="far_product",
-    )(*incoming, total, right_stack, left_stack)
+    )(*left, *right, total, right_stack, left_stack)
 
 
 def encode(block, payload_ref):
@@ -248,33 +255,37 @@
     return payload_ref[:part, :].astype(jnp.int32).astype(jnp.float32) * jnp.exp2(power - LEVELS)
 
 
-def join_kernel(keep_ref, got_ref, own_ref, other_ref, payload_ref):
+def join_kernel(keep_ref, got_ref, own_ref, other_ref, *payload_refs):
     half = keep_ref.shape[1] // 2
-    own = keep_ref[:, :half] + got_ref[:, half:]
-    other = keep_ref[:, half:] + got_ref[:, :half]
-    own_ref[...] = own
-    other_ref[...] = other
-    encode(jnp.concatenate([own, other], axis=1), payload_ref)
+    part = keep_ref.shape[0] // len(payload_refs)
+    for i, payload_ref in enumerate(payload_refs):
+        rows = slice(i * part, (i + 1) * part)
+        own = keep_ref[rows, :half] + got_ref[rows, half:]
+        other = keep_ref[rows, half:] + got_ref[rows, :half]
+        own_ref[rows, :] = own
+        other_ref[rows, :] = other
+        encode(jnp.concatenate([own, other], axis=1), payload_ref)
 
 
 def join(keep, got):
     rows, cols = keep.shape
     half = jax.ShapeDtypeStruct((rows, cols // 2), jnp.float32)
+    payload = jax.ShapeDtypeStruct((rows // 2 + 16, cols), jnp.int16)
     vmem = pl.BlockSpec(memory_space=pltpu.VMEM)
     return pl.pallas_call(
         join_kernel,
-        out_shape=[half, half, jax.ShapeDtypeStruct((rows + 16, cols), jnp.int16)],
+        out_shape=[half, half, payload, payload],
         in_specs=[vmem] * 2,
-        out_specs=[vmem] * 3,
+        out_specs=[vmem] * 4,
         compiler_params=pltpu.CompilerParams(vmem_limit_bytes=8 * MIB),
         cost_estimate=pl.CostEstimate(flops=4 * rows * cols, bytes_accessed=12 * rows * cols, transcendentals=0),
         name="join",
     )(keep, got)
 
 
-def combine_kernel(own_ref, side_ref, payload_ref, row_gap_ref, col_gap_ref, out_ref):
+def combine_kernel(own_ref, side_ref, top_ref, bottom_ref, row_gap_ref, col_gap_ref, out_ref):
     core = lax.axis_index("row") % CORE
-    mirror = decode(payload_ref)
+    mirror = jnp.concatenate([decode(top_ref), decode(bottom_ref)])
     half = mirror.shape[1] // 2
     own = own_ref[...] + mirror[:, :half].T
     other = side_ref[...] + mirror[:, half:].T
@@ -282,17 +293,17 @@
     out_ref[...] = both / (row_gap_ref[...] + col_gap_ref[...])
 
 
-def combine(own, side, payload, row_gap, col_gap):
+def combine(own, side, payloads, row_gap, col_gap):
     rows, cols = row_gap.shape[0], col_gap.shape[0]
     return pl.pallas_call(
         combine_kernel,
         out_shape=jax.ShapeDtypeStruct((rows, cols), jnp.float32),
-        in_specs=[pl.BlockSpec(memory_space=pltpu.VMEM)] * 5,
+        in_specs=[pl.BlockSpec(memory_space=pltpu.VMEM)] * 6,
         out_specs=pl.BlockSpec(memory_space=pltpu.VMEM),
         compiler_params=pltpu.CompilerParams(vmem_limit_bytes=8 * MIB),
         cost_estimate=pl.CostEstimate(flops=4 * rows * cols, bytes_accessed=12 * rows * cols, transcendentals=0),
         name="combine",
-    )(own, side, payload, row_gap[:, None], col_gap[None, :])
+    )(own, side, *payloads, row_gap[:, None], col_gap[None, :])
 
 
 def shards(amplitudes, integrals, occ_energy, vir_energy, pair_occ, pair_vir):
@@ -316,13 +327,13 @@
 
     total, right_stack, left_stack = near_product(near, right_near)
     total, row_gap, col_gap = lax.optimization_barrier((total, row_gap, col_gap))
-    give, right_stack, left_stack = far_product((*far, *right_far), total, right_stack, left_stack, False)
+    give, right_stack, left_stack = far_product(far, right_far, total, right_stack, left_stack, False)
     got = send(give, across_core)
-    keep = far_product((), total, right_stack, left_stack, True)
-    own, other, payload = join(keep, got)
-    payload = send(send(payload, detour), after_detour)
+    keep = far_product((), (), total, right_stack, left_stack, True)
+    own, other, *payloads = join(keep, got)
+    payloads = [send(send(payload, detour), after_detour) for payload in payloads]
     side = send(other, across_core)
-    return combine(own, side, payload, row_gap, col_gap)
+    return combine(own, side, payloads, row_gap, col_gap)
 
 
 def solution(mesh):

time: 119 us -> 114 us (0.958)
  waiting for transfers between devices: 62.8 us -> 52.1 us
  starting transfers between devices: 29.7 us -> 35.8 us
    ppermute x20 -> x22, waiting for transfers between devices: 62.8 us -> 52.1 us  [send(): return lax.ppermute(block, AXES, pairs)]
    ppermute x20 -> x22, starting transfers between devices: 29.7 us -> 35.8 us  [send(): return lax.ppermute(block, AXES, pairs)]
  transfers between devices with their start and end apart: 20 -> 22, of which waited for: 10 -> 11; matrix products, arithmetic and copies ran while one was open for 6% -> 7% of each run, Pallas kernels for 6% -> 7%
where the time goes in v8:
time: 114 us; the launch traced here: 113 us
  waiting for transfers between devices  52.1 us (46%)
  starting transfers between devices  35.8 us (31%)
  Pallas kernels  16.8 us (15%)
  local copies, waits for them, and re-layouts  6.54 us (6%)
  other arithmetic  1.99 us (2%)
    ppermute x22, waiting for transfers between devices, send(): return lax.ppermute(block, AXES, pairs)  52.1 us
    ppermute x22, starting transfers between devices, send(): return lax.ppermute(block, AXES, pairs)  35.8 us
    pallas_call x2, Pallas kernels, far_product(): pl.pallas_call(lambda *refs: far_kernel(own, len(left), len(right), *refs...  7.92 us
    pallas_call x1, Pallas kernels, near_product(): pl.pallas_call(lambda *refs: near_kernel(len(left), len(right), *refs), o...  4.61 us
    pallas_call x1, Pallas kernels, combine(): pl.pallas_call(combine_kernel, out_shape=jax.ShapeDtypeStruct((rows, cols...  2.51 us
  transfers between devices with their start and end apart: 22, of which 11 were waited for; matrix products, arithmetic and copies ran while one was open for 7% of the time, Pallas kernels for 7%

profile of v8, /device:TPU:16, one launch (start us, length us, event | category | flops | bytes accessed | tf_op | source)
XLA Modules:
  0.0 113.5 jit_solution(15376553647929296476)
XLA Ops:
  0.0 2.0 %collective-permute-start.5 = (bf16[448,896]{1,0:T(8,128)(2,1)}, bf16[448,896]{1,0:T(8,128)(2,1)}, u32[]{:S(2)}, u32[]{:S(2)}) collective-permute-start(bf16[448,896]{1,0:T(8,128)(2,1)} %refs_5_.1), channel_id=1, source_target_pairs={{0,64},{1,65},{2,66},{3,67},{4,68},{5,69},{6,70},{7,71},{8,72},{9,... | collective-permute-start | bytes 2408456 | tf_op jit(solution)/shard_map/ppermute | solution.py:29
  2.0 1.5 %fusion.2 = (bf16[448,448]{1,0:T(8,128)(2,1)S(1)}, bf16[448,448]{1,0:T(8,128)(2,1)S(1)}) fusion(bf16[448,896]{1,0:T(8,128)(2,1)} %param.6), kind=kLoop, calls=%fused_computation.21 | loop fusion | bytes 1605632 | tf_op jit(solution)/shard_map/jit(_roll_static)/slice | solution.py:317
  3.5 2.8 %collective-permute-start.8 = (bf16[448,896]{1,0:T(8,128)(2,1)S(1)}, bf16[448,896]{1,0:T(8,128)(2,1)S(1)}, u32[]{:S(2)}, u32[]{:S(2)}) collective-permute-start(bf16[448,896]{1,0:T(8,128)(2,1)S(1)} %copy-done), channel_id=1, source_target_pairs={{0,48},{1,49},{2,50},{3,51},{4,52},{5,53},{6,54},{7,55},{8,56},{9,... | collective-permute-start | bytes 2408456 | tf_op jit(solution)/shard_map/ppermute | solution.py:29
  7.4 1.4 %collective-permute-start.2 = (bf16[448,896]{1,0:T(8,128)(2,1)S(1)}, bf16[448,896]{1,0:T(8,128)(2,1)S(1)}, u32[]{:S(2)}, u32[]{:S(2)}) collective-permute-start(bf16[448,896]{1,0:T(8,128)(2,1)S(1)} %fusion.refs_0_), channel_id=1, source_target_pairs={{0,2},{1,3},{2,4},{3,5},{4,6},{5,7},{6,0},{7,1},{8,10},{9,11},{10,... | collective-permute-start | bytes 2408456 | tf_op jit(solution)/shard_map/ppermute | solution.py:29
  9.4 11.4 %collective-permute-done.5.refs_9_ = bf16[448,896]{1,0:T(8,128)(2,1)} collective-permute-done((bf16[448,896]{1,0:T(8,128)(2,1)}, bf16[448,896]{1,0:T(8,128)(2,1)}, u32[]{:S(2)}, u32[]{:S(2)}) %collective-permute-start.5) | collective-permute-done | bytes 802848 | tf_op jit(solution)/shard_map/ppermute | solution.py:29
  20.8 3.7 %collective-permute-start.6 = (bf16[448,896]{1,0:T(8,128)(2,1)S(1)}, bf16[448,896]{1,0:T(8,128)(2,1)}, u32[]{:S(2)}, u32[]{:S(2)}) collective-permute-start(bf16[448,896]{1,0:T(8,128)(2,1)S(1)} %fusion.refs_0_), channel_id=1, source_target_pairs={{0,1},{1,0},{2,3},{3,2},{4,5},{5,4},{6,7},{7,6},{8,9},{9,8},{10,11... | collective-permute-start | bytes 2408456 | tf_op jit(solution)/shard_map/ppermute | solution.py:29
  25.4 1.9 %collective-permute-done.7.refs_8_ = bf16[448,896]{1,0:T(8,128)(2,1)} collective-permute-done((bf16[448,896]{1,0:T(8,128)(2,1)S(1)}, bf16[448,896]{1,0:T(8,128)(2,1)}, u32[]{:S(2)}, u32[]{:S(2)}) %collective-permute-start.7) | collective-permute-done | bytes 802848 | tf_op jit(solution)/shard_map/ppermute | solution.py:29
  27.3 3.2 %collective-permute-start.10 = (bf16[448,896]{1,0:T(8,128)(2,1)}, bf16[448,896]{1,0:T(8,128)(2,1)}, u32[]{:S(2)}, u32[]{:S(2)}) collective-permute-start(bf16[448,896]{1,0:T(8,128)(2,1)} %collective-permute-done.5.refs_9_), channel_id=1, source_target_pairs={{0,48},{1,49},{2,50},{3,51},{4,52},{5,53},{6,54},{7,55},{8,56},{9,... | collective-permute-start | bytes 2408456 | tf_op jit(solution)/shard_map/ppermute | solution.py:29
  31.3 1.3 %collective-permute-start.3 = (bf16[224,896]{1,0:T(8,128)(2,1)}, bf16[224,896]{1,0:T(8,128)(2,1)}, u32[]{:S(2)}, u32[]{:S(2)}) collective-permute-start(bf16[224,896]{1,0:T(8,128)(2,1)} %slice.28), channel_id=1, source_target_pairs={{0,2},{1,3},{2,4},{3,5},{4,6},{5,7},{6,0},{7,1},{8,10},{9,11},{10,... | collective-permute-start | bytes 1204232 | tf_op jit(solution)/shard_map/ppermute | solution.py:29
  34.6 7.8 %collective-permute-done.6.refs_4_ = bf16[448,896]{1,0:T(8,128)(2,1)} collective-permute-done((bf16[448,896]{1,0:T(8,128)(2,1)S(1)}, bf16[448,896]{1,0:T(8,128)(2,1)}, u32[]{:S(2)}, u32[]{:S(2)}) %collective-permute-start.6) | collective-permute-done | bytes 802848 | tf_op jit(solution)/shard_map/ppermute | solution.py:29
  42.3 1.3 %collective-permute-start.13 = (bf16[448,896]{1,0:T(8,128)(2,1)}, bf16[448,896]{1,0:T(8,128)(2,1)S(1)}, u32[]{:S(2)}, u32[]{:S(2)}) collective-permute-start(bf16[448,896]{1,0:T(8,128)(2,1)} %collective-permute-done.6.refs_4_), channel_id=1, source_target_pairs={{0,2},{1,3},{2,4},{3,5},{4,6},{5,7},{6,0},{7,1},{8,10},{9,11},{10,... | collective-permute-start | bytes 2408456 | tf_op jit(solution)/shard_map/ppermute | solution.py:29
  44.4 1.0 constant_dynamic-update-slice_fusion.1
  45.4 1.0 constant_dynamic-update-slice_fusion.refs_2_
  46.5 3.3 %collective-permute-start.12 = (bf16[448,896]{1,0:T(8,128)(2,1)S(1)}, bf16[448,896]{1,0:T(8,128)(2,1)S(1)}, u32[]{:S(2)}, u32[]{:S(2)}) collective-permute-start(bf16[448,896]{1,0:T(8,128)(2,1)S(1)} %constant_dynamic-update-slice_fusion.refs_2_), channel_id=1, source_target_pairs={{0,1},{1,0},{2,3},{3,2},{4,5},{5,4},{6,7},{7,6},{8,9},{9,8},{10,11... | collective-permute-start | bytes 2408456 | tf_op jit(solution)/shard_map/ppermute | solution.py:29
  49.8 1.5 %collective-permute-start.15 = (bf16[448,896]{1,0:T(8,128)(2,1)}, bf16[448,896]{1,0:T(8,128)(2,1)S(1)}, u32[]{:S(2)}, u32[]{:S(2)}) collective-permute-start(bf16[448,896]{1,0:T(8,128)(2,1)} %collective-permute-done.5.refs_9_), channel_id=1, source_target_pairs={{0,16},{1,17},{2,18},{3,19},{4,20},{5,21},{6,22},{7,23},{8,24},{9,... | collective-permute-start | bytes 2408456 | tf_op jit(solution)/shard_map/ppermute | solution.py:29
  51.3 1.7 %collective-permute-start.14 = (bf16[448,896]{1,0:T(8,128)(2,1)}, bf16[448,896]{1,0:T(8,128)(2,1)S(1)}, u32[]{:S(2)}, u32[]{:S(2)}) collective-permute-start(bf16[448,896]{1,0:T(8,128)(2,1)} %collective-permute-done.10.refs_10_), channel_id=1, source_target_pairs={{0,48},{1,49},{2,50},{3,51},{4,52},{5,53},{6,54},{7,55},{8,56},{9,... | collective-permute-start | bytes 2408456 | tf_op jit(solution)/shard_map/ppermute | solution.py:29
  54.1 4.6 %near_product.1 = (f32[896,896]{1,0:T(8,128)S(1)}, bf16[8,448,896]{2,1,0:T(8,128)(2,1)S(1)}, bf16[8,448,896]{2,1,0:T(8,128)(2,1)S(1)}) custom-call(bf16[448,896]{1,0:T(8,128)(2,1)S(1)} %fusion.refs_0_, bf16[448,896]{1,0:T(8,128)(2,1)S(1)} %collective-permute-done.1.refs_1_, bf16[448,896]{1,0:T(8,128)(2,1)S(1)} %constant_dynamic-update-slice_fusion.refs_2_, ...), custom_call_target="tpu_custom_call" | custom-call | flops 1438646272 | bytes 12582912 | tf_op jit(solution)/shard_map/near_product/pallas_call | solution.py:165
  58.7 2.7 %collective-permute-done.13.refs_2_ = bf16[448,896]{1,0:T(8,128)(2,1)S(1)} collective-permute-done((bf16[448,896]{1,0:T(8,128)(2,1)}, bf16[448,896]{1,0:T(8,128)(2,1)S(1)}, u32[]{:S(2)}, u32[]{:S(2)}) %collective-permute-start.13) | collective-permute-done | bytes 802848 | tf_op jit(solution)/shard_map/ppermute | solution.py:29
  62.4 3.9 %collective-permute-done.12.refs_1_ = bf16[448,896]{1,0:T(8,128)(2,1)S(1)} collective-permute-done((bf16[448,896]{1,0:T(8,128)(2,1)S(1)}, bf16[448,896]{1,0:T(8,128)(2,1)S(1)}, u32[]{:S(2)}, u32[]{:S(2)}) %collective-permute-start.12) | collective-permute-done | bytes 802848 | tf_op jit(solution)/shard_map/ppermute | solution.py:29
  66.4 2.6 %collective-permute-done.15.refs_4_ = bf16[448,896]{1,0:T(8,128)(2,1)S(1)} collective-permute-done((bf16[448,896]{1,0:T(8,128)(2,1)}, bf16[448,896]{1,0:T(8,128)(2,1)S(1)}, u32[]{:S(2)}, u32[]{:S(2)}) %collective-permute-start.15) | collective-permute-done | bytes 802848 | tf_op jit(solution)/shard_map/ppermute | solution.py:29
  68.9 4.4 %far_product.2 = (f32[448,896]{1,0:T(8,128)S(1)}, bf16[8,448,896]{2,1,0:T(8,128)(2,1)S(1)}, bf16[8,448,896]{2,1,0:T(8,128)(2,1)S(1)}) custom-call(bf16[448,896]{1,0:T(8,128)(2,1)S(1)} %collective-permute-done.11.refs_0_, bf16[448,896]{1,0:T(8,128)(2,1)S(1)} %collective-permute-done.12.refs_1_, ...), custom_call_target="tpu_custom_call", output_to_operand_aliasing={{1}: (6, {}), {2}: (7, {})} | custom-call | flops 2157969408 | bytes 12582912 | tf_op jit(solution)/shard_map/far_product/pallas_call | solution.py:230
  73.4 3.5 %far_product.3.keep_ref = f32[448,896]{1,0:T(8,128)S(1)} custom-call(f32[896,896]{1,0:T(8,128)S(1)} %get-tuple-element.30.refs_5_.refs_0_, bf16[8,448,896]{2,1,0:T(8,128)(2,1)S(1)} %get-tuple-element.34.refs_1_, bf16[8,448,896]{2,1,0:T(8,128)(2,1)S(1)} %get-tuple-element.35.refs_2_), custom_call_target="tpu_custom_call" | custom-call | flops 2157969408 | bytes 12582912 | tf_op jit(solution)/shard_map/far_product/pallas_call | solution.py:230
  77.0 1.7 %join.1 = (f32[448,448]{1,0:T(8,128)S(1)}, f32[448,448]{1,0:T(8,128)}, s16[240,896]{1,0:T(8,128)(2,1)S(1)}, s16[240,896]{1,0:T(8,128)(2,1)S(1)}) custom-call(f32[448,896]{1,0:T(8,128)S(1)} %far_product.3.keep_ref, f32[448,896]{1,0:T(8,128)S(1)} %collective-permute-done.16.got_ref), custom_call_target="tpu_custom_call" | custom-call | flops 1605632 | bytes 4816896 | tf_op jit(solution)/shard_map/join/pallas_call | solution.py:275
  78.7 3.2 %collective-permute-start.18 = (s16[240,896]{1,0:T(8,128)(2,1)S(1)}, s16[240,896]{1,0:T(8,128)(2,1)}, u32[]{:S(2)}, u32[]{:S(2)}) collective-permute-start(s16[240,896]{1,0:T(8,128)(2,1)S(1)} %get-tuple-element.39), channel_id=1, source_target_pairs={{0,0},{1,80},{2,2},{3,64},{4,6},{5,18},{6,22},{7,70},{8,72},{9,8},... | collective-permute-start | bytes 1290248 | tf_op jit(solution)/shard_map/ppermute | solution.py:29
  81.9 3.4 %collective-permute-start.20 = (s16[240,896]{1,0:T(8,128)(2,1)S(1)}, s16[240,896]{1,0:T(8,128)(2,1)}, u32[]{:S(2)}, u32[]{:S(2)}) collective-permute-start(s16[240,896]{1,0:T(8,128)(2,1)S(1)} %get-tuple-element.40), channel_id=1, source_target_pairs={{0,0},{1,80},{2,2},{3,64},{4,6},{5,18},{6,22},{7,70},{8,72},{9,8},... | collective-permute-start | bytes 1290248 | tf_op jit(solution)/shard_map/ppermute | solution.py:29
  86.1 6.3 %collective-permute-done.18 = s16[240,896]{1,0:T(8,128)(2,1)} collective-permute-done((s16[240,896]{1,0:T(8,128)(2,1)S(1)}, s16[240,896]{1,0:T(8,128)(2,1)}, u32[]{:S(2)}, u32[]{:S(2)}) %collective-permute-start.18) | collective-permute-done | bytes 430112 | tf_op jit(solution)/shard_map/ppermute | solution.py:29
  92.5 1.9 %collective-permute-start.19 = (s16[240,896]{1,0:T(8,128)(2,1)}, s16[240,896]{1,0:T(8,128)(2,1)S(1)}, u32[]{:S(2)}, u32[]{:S(2)}) collective-permute-start(s16[240,896]{1,0:T(8,128)(2,1)} %collective-permute-done.18), channel_id=1, source_target_pairs={{0,0},{1,23},{2,32},{3,19},{4,20},{5,69},{6,64},{7,21},{8,24},{9,1... | collective-permute-start | bytes 1290248 | tf_op jit(solution)/shard_map/ppermute | solution.py:29
  94.4 2.7 %collective-permute-done.20 = s16[240,896]{1,0:T(8,128)(2,1)} collective-permute-done((s16[240,896]{1,0:T(8,128)(2,1)S(1)}, s16[240,896]{1,0:T(8,128)(2,1)}, u32[]{:S(2)}, u32[]{:S(2)}) %collective-permute-start.20) | collective-permute-done | bytes 430112 | tf_op jit(solution)/shard_map/ppermute | solution.py:29
  97.1 1.9 %collective-permute-start.21 = (s16[240,896]{1,0:T(8,128)(2,1)}, s16[240,896]{1,0:T(8,128)(2,1)S(1)}, u32[]{:S(2)}, u32[]{:S(2)}) collective-permute-start(s16[240,896]{1,0:T(8,128)(2,1)} %collective-permute-done.20), channel_id=1, source_target_pairs={{0,0},{1,23},{2,32},{3,19},{4,20},{5,69},{6,64},{7,21},{8,24},{9,1... | collective-permute-start | bytes 1290248 | tf_op jit(solution)/shard_map/ppermute | solution.py:29
  99.2 7.2 %collective-permute-done.19.top_ref = s16[240,896]{1,0:T(8,128)(2,1)S(1)} collective-permute-done((s16[240,896]{1,0:T(8,128)(2,1)}, s16[240,896]{1,0:T(8,128)(2,1)S(1)}, u32[]{:S(2)}, u32[]{:S(2)}) %collective-permute-start.19) | collective-permute-done | bytes 430112 | tf_op jit(solution)/shard_map/ppermute | solution.py:29
  106.4 4.6 %collective-permute-done.21.bottom_ref = s16[240,896]{1,0:T(8,128)(2,1)S(1)} collective-permute-done((s16[240,896]{1,0:T(8,128)(2,1)}, s16[240,896]{1,0:T(8,128)(2,1)S(1)}, u32[]{:S(2)}, u32[]{:S(2)}) %collective-permute-start.21) | collective-permute-done | bytes 430112 | tf_op jit(solution)/shard_map/ppermute | solution.py:29
  111.0 2.5 %combine.1 = f32[448,896]{1,0:T(8,128)} custom-call(f32[448,448]{1,0:T(8,128)S(1)} %get-tuple-element.37.own_ref, f32[448,448]{1,0:T(8,128)S(1)} %collective-permute-done.17.side_ref, s16[240,896]{1,0:T(8,128)(2,1)S(1)} %collective-permute-done.19.top_ref, s16[240,896]{1,0:T(8,128)(2,1)S(1)} %collective-permute-done.21.bottom_ref, ...), custom_call_target="tpu_custom_call" | custom-call | flops 1605632 | bytes 4816896 | tf_op jit(solution)/shard_map/combine/pallas_call | solution.py:298
  (57 shorter events, 9.2 us)
Async XLA Ops:
  0.0 3.5 %copy-start = (bf16[448,896]{1,0:T(8,128)(2,1)S(1)}, bf16[448,896]{1,0:T(8,128)(2,1)}, u32[]{:S(2)}) copy-start(bf16[448,896]{1,0:T(8,128)(2,1)} %refs_5_.1) | copy-start | bytes 2408452
  0.0 3.5 %collective-permute-start = (bf16[448,896]{1,0:T(8,128)(2,1)}, bf16[448,896]{1,0:T(8,128)(2,1)S(1)}, u32[]{:S(2)}, u32[]{:S(2)}) collective-permute-start(bf16[448,896]{1,0:T(8,128)(2,1)} %param.6), channel_id=1, source_target_pairs={{0,8},{1,9},{2,10},{3,11},{4,12},{5,13},{6,14},{7,15},{8,0},{9,1},... | collective-permute-start | bytes 2408456 | tf_op jit(solution)/shard_map/ppermute | solution.py:29
  0.0 20.8 %collective-permute-start.5 = (bf16[448,896]{1,0:T(8,128)(2,1)}, bf16[448,896]{1,0:T(8,128)(2,1)}, u32[]{:S(2)}, u32[]{:S(2)}) collective-permute-start(bf16[448,896]{1,0:T(8,128)(2,1)} %refs_5_.1), channel_id=1, source_target_pairs={{0,64},{1,65},{2,66},{3,67},{4,68},{5,69},{6,70},{7,71},{8,72},{9,... | collective-permute-start | bytes 2408456 | tf_op jit(solution)/shard_map/ppermute | solution.py:29
  2.0 4.5 %copy-start.3 = (bf16[448,896]{1,0:T(8,128)(2,1)S(1)}, bf16[448,896]{1,0:T(8,128)(2,1)}, u32[]{:S(2)}) copy-start(bf16[448,896]{1,0:T(8,128)(2,1)} %param.6) | copy-start | bytes 2408452
  3.5 21.0 %collective-permute-start.8 = (bf16[448,896]{1,0:T(8,128)(2,1)S(1)}, bf16[448,896]{1,0:T(8,128)(2,1)S(1)}, u32[]{:S(2)}, u32[]{:S(2)}) collective-permute-start(bf16[448,896]{1,0:T(8,128)(2,1)S(1)} %copy-done), channel_id=1, source_target_pairs={{0,48},{1,49},{2,50},{3,51},{4,52},{5,53},{6,54},{7,55},{8,56},{9,... | collective-permute-start | bytes 2408456 | tf_op jit(solution)/shard_map/ppermute | solution.py:29
  6.3 21.0 %collective-permute-start.7 = (bf16[448,896]{1,0:T(8,128)(2,1)S(1)}, bf16[448,896]{1,0:T(8,128)(2,1)}, u32[]{:S(2)}, u32[]{:S(2)}) collective-permute-start(bf16[448,896]{1,0:T(8,128)(2,1)S(1)} %copy-done), channel_id=1, source_target_pairs={{0,16},{1,17},{2,18},{3,19},{4,20},{5,21},{6,22},{7,23},{8,24},{9,... | collective-permute-start | bytes 2408456 | tf_op jit(solution)/shard_map/ppermute | solution.py:29
  6.5 27.6 %copy-start.4 = (s32[7168]{0:T(1024)S(1)}, s32[7168]{0:T(1024)}, u32[]{:S(2)}) copy-start(s32[7168]{0:T(1024)} %param.10) | copy-start | bytes 86020
  6.6 27.7 %copy-start.5 = (s32[7168]{0:T(1024)S(1)}, s32[7168]{0:T(1024)}, u32[]{:S(2)}) copy-start(s32[7168]{0:T(1024)} %param.11) | copy-start | bytes 86020
  7.3 27.1 %copy-start.7 = (f32[80]{0:T(128)S(1)}, f32[80]{0:T(128)}, u32[]{:S(2)}) copy-start(f32[80]{0:T(128)} %param.8) | copy-start | bytes 964
  7.3 45.7 %copy-start.6 = (f32[1000]{0:T(1024)S(1)}, f32[1000]{0:T(1024)}, u32[]{:S(2)}) copy-start(f32[1000]{0:T(1024)} %param.9) | copy-start | bytes 12004
  7.4 23.2 %collective-permute-start.2 = (bf16[448,896]{1,0:T(8,128)(2,1)S(1)}, bf16[448,896]{1,0:T(8,128)(2,1)S(1)}, u32[]{:S(2)}, u32[]{:S(2)}) collective-permute-start(bf16[448,896]{1,0:T(8,128)(2,1)S(1)} %fusion.refs_0_), channel_id=1, source_target_pairs={{0,2},{1,3},{2,4},{3,5},{4,6},{5,7},{6,0},{7,1},{8,10},{9,11},{10,... | collective-permute-start | bytes 2408456 | tf_op jit(solution)/shard_map/ppermute | solution.py:29
  8.7 23.9 %collective-permute-start.1 = (bf16[448,896]{1,0:T(8,128)(2,1)S(1)}, bf16[448,896]{1,0:T(8,128)(2,1)S(1)}, u32[]{:S(2)}, u32[]{:S(2)}) collective-permute-start(bf16[448,896]{1,0:T(8,128)(2,1)S(1)} %fusion.refs_0_), channel_id=1, source_target_pairs={{0,6},{1,7},{2,0},{3,1},{4,2},{5,3},{6,4},{7,5},{8,14},{9,15},{10,... | collective-permute-start | bytes 2408456 | tf_op jit(solution)/shard_map/ppermute | solution.py:29
  20.8 21.5 %collective-permute-start.6 = (bf16[448,896]{1,0:T(8,128)(2,1)S(1)}, bf16[448,896]{1,0:T(8,128)(2,1)}, u32[]{:S(2)}, u32[]{:S(2)}) collective-permute-start(bf16[448,896]{1,0:T(8,128)(2,1)S(1)} %fusion.refs_0_), channel_id=1, source_target_pairs={{0,1},{1,0},{2,3},{3,2},{4,5},{5,4},{6,7},{7,6},{8,9},{9,8},{10,11... | collective-permute-start | bytes 2408456 | tf_op jit(solution)/shard_map/ppermute | solution.py:29
  24.5 0.9 copy-start.1
  27.3 22.5 %collective-permute-start.9 = (bf16[448,896]{1,0:T(8,128)(2,1)}, bf16[448,896]{1,0:T(8,128)(2,1)}, u32[]{:S(2)}, u32[]{:S(2)}) collective-permute-start(bf16[448,896]{1,0:T(8,128)(2,1)} %collective-permute-done.7.refs_8_), channel_id=1, source_target_pairs={{0,16},{1,17},{2,18},{3,19},{4,20},{5,21},{6,22},{7,23},{8,24},{9,... | collective-permute-start | bytes 2408456 | tf_op jit(solution)/shard_map/ppermute | solution.py:29
  27.3 24.0 %collective-permute-start.10 = (bf16[448,896]{1,0:T(8,128)(2,1)}, bf16[448,896]{1,0:T(8,128)(2,1)}, u32[]{:S(2)}, u32[]{:S(2)}) collective-permute-start(bf16[448,896]{1,0:T(8,128)(2,1)} %collective-permute-done.5.refs_9_), channel_id=1, source_target_pairs={{0,48},{1,49},{2,50},{3,51},{4,52},{5,53},{6,54},{7,55},{8,56},{9,... | collective-permute-start | bytes 2408456 | tf_op jit(solution)/shard_map/ppermute | solution.py:29
  31.3 12.3 %collective-permute-start.3 = (bf16[224,896]{1,0:T(8,128)(2,1)}, bf16[224,896]{1,0:T(8,128)(2,1)}, u32[]{:S(2)}, u32[]{:S(2)}) collective-permute-start(bf16[224,896]{1,0:T(8,128)(2,1)} %slice.28), channel_id=1, source_target_pairs={{0,2},{1,3},{2,4},{3,5},{4,6},{5,7},{6,0},{7,1},{8,10},{9,11},{10,... | collective-permute-start | bytes 1204232 | tf_op jit(solution)/shard_map/ppermute | solution.py:29
  33.4 12.0 %collective-permute-start.4 = (bf16[224,896]{1,0:T(8,128)(2,1)}, bf16[224,896]{1,0:T(8,128)(2,1)}, u32[]{:S(2)}, u32[]{:S(2)}) collective-permute-start(bf16[224,896]{1,0:T(8,128)(2,1)} %slice.29), channel_id=1, source_target_pairs={{0,6},{1,7},{2,0},{3,1},{4,2},{5,3},{6,4},{7,5},{8,14},{9,15},{10,... | collective-permute-start | bytes 1204232 | tf_op jit(solution)/shard_map/ppermute | solution.py:29
  34.4 19.7 %copy-start.2 = (bf16[448,896]{1,0:T(8,128)(2,1)S(1)}, bf16[448,896]{1,0:T(8,128)(2,1)}, u32[]{:S(2)}) copy-start(bf16[448,896]{1,0:T(8,128)(2,1)} %copy-done.1) | copy-start | bytes 2408452
  42.3 19.1 %collective-permute-start.13 = (bf16[448,896]{1,0:T(8,128)(2,1)}, bf16[448,896]{1,0:T(8,128)(2,1)S(1)}, u32[]{:S(2)}, u32[]{:S(2)}) collective-permute-start(bf16[448,896]{1,0:T(8,128)(2,1)} %collective-permute-done.6.refs_4_), channel_id=1, source_target_pairs={{0,2},{1,3},{2,4},{3,5},{4,6},{5,7},{6,0},{7,1},{8,10},{9,11},{10,... | collective-permute-start | bytes 2408456 | tf_op jit(solution)/shard_map/ppermute | solution.py:29
  43.6 18.8 %collective-permute-start.11 = (bf16[448,896]{1,0:T(8,128)(2,1)}, bf16[448,896]{1,0:T(8,128)(2,1)S(1)}, u32[]{:S(2)}, u32[]{:S(2)}) collective-permute-start(bf16[448,896]{1,0:T(8,128)(2,1)} %collective-permute-done.6.refs_4_), channel_id=1, source_target_pairs={{0,6},{1,7},{2,0},{3,1},{4,2},{5,3},{6,4},{7,5},{8,14},{9,15},{10,... | collective-permute-start | bytes 2408456 | tf_op jit(solution)/shard_map/ppermute | solution.py:29
  46.5 19.9 %collective-permute-start.12 = (bf16[448,896]{1,0:T(8,128)(2,1)S(1)}, bf16[448,896]{1,0:T(8,128)(2,1)S(1)}, u32[]{:S(2)}, u32[]{:S(2)}) collective-permute-start(bf16[448,896]{1,0:T(8,128)(2,1)S(1)} %constant_dynamic-update-slice_fusion.refs_2_), channel_id=1, source_target_pairs={{0,1},{1,0},{2,3},{3,2},{4,5},{5,4},{6,7},{7,6},{8,9},{9,8},{10,11... | collective-permute-start | bytes 2408456 | tf_op jit(solution)/shard_map/ppermute | solution.py:29
  49.8 19.1 %collective-permute-start.15 = (bf16[448,896]{1,0:T(8,128)(2,1)}, bf16[448,896]{1,0:T(8,128)(2,1)S(1)}, u32[]{:S(2)}, u32[]{:S(2)}) collective-permute-start(bf16[448,896]{1,0:T(8,128)(2,1)} %collective-permute-done.5.refs_9_), channel_id=1, source_target_pairs={{0,16},{1,17},{2,18},{3,19},{4,20},{5,21},{6,22},{7,23},{8,24},{9,... | collective-permute-start | bytes 2408456 | tf_op jit(solution)/shard_map/ppermute | solution.py:29
  51.3 17.7 %collective-permute-start.14 = (bf16[448,896]{1,0:T(8,128)(2,1)}, bf16[448,896]{1,0:T(8,128)(2,1)S(1)}, u32[]{:S(2)}, u32[]{:S(2)}) collective-permute-start(bf16[448,896]{1,0:T(8,128)(2,1)} %collective-permute-done.10.refs_10_), channel_id=1, source_target_pairs={{0,48},{1,49},{2,50},{3,51},{4,52},{5,53},{6,54},{7,55},{8,56},{9,... | collective-permute-start | bytes 2408456 | tf_op jit(solution)/shard_map/ppermute | solution.py:29
  73.4 3.6 %collective-permute-start.16 = (f32[448,896]{1,0:T(8,128)S(1)}, f32[448,896]{1,0:T(8,128)S(1)}, u32[]{:S(2)}, u32[]{:S(2)}) collective-permute-start(f32[448,896]{1,0:T(8,128)S(1)} %get-tuple-element.36), channel_id=1, source_target_pairs={{0,8},{1,9},{2,10},{3,11},{4,12},{5,13},{6,14},{7,15},{8,0},{9,1},... | collective-permute-start | bytes 4816904 | tf_op jit(solution)/shard_map/ppermute | solution.py:29
  78.7 13.8 %collective-permute-start.18 = (s16[240,896]{1,0:T(8,128)(2,1)S(1)}, s16[240,896]{1,0:T(8,128)(2,1)}, u32[]{:S(2)}, u32[]{:S(2)}) collective-permute-start(s16[240,896]{1,0:T(8,128)(2,1)S(1)} %get-tuple-element.39), channel_id=1, source_target_pairs={{0,0},{1,80},{2,2},{3,64},{4,6},{5,18},{6,22},{7,70},{8,72},{9,8},... | collective-permute-start | bytes 1290248 | tf_op jit(solution)/shard_map/ppermute | solution.py:29
  81.9 15.2 %collective-permute-start.20 = (s16[240,896]{1,0:T(8,128)(2,1)S(1)}, s16[240,896]{1,0:T(8,128)(2,1)}, u32[]{:S(2)}, u32[]{:S(2)}) collective-permute-start(s16[240,896]{1,0:T(8,128)(2,1)S(1)} %get-tuple-element.40), channel_id=1, source_target_pairs={{0,0},{1,80},{2,2},{3,64},{4,6},{5,18},{6,22},{7,70},{8,72},{9,8},... | collective-permute-start | bytes 1290248 | tf_op jit(solution)/shard_map/ppermute | solution.py:29
  85.3 13.9 %collective-permute-start.17 = (f32[448,448]{1,0:T(8,128)}, f32[448,448]{1,0:T(8,128)S(1)}, u32[]{:S(2)}, u32[]{:S(2)}) collective-permute-start(f32[448,448]{1,0:T(8,128)} %get-tuple-element.38), channel_id=1, source_target_pairs={{0,8},{1,9},{2,10},{3,11},{4,12},{5,13},{6,14},{7,15},{8,0},{9,1},... | collective-permute-start | bytes 2408456 | tf_op jit(solution)/shard_map/ppermute | solution.py:29
  92.5 13.9 %collective-permute-start.19 = (s16[240,896]{1,0:T(8,128)(2,1)}, s16[240,896]{1,0:T(8,128)(2,1)S(1)}, u32[]{:S(2)}, u32[]{:S(2)}) collective-permute-start(s16[240,896]{1,0:T(8,128)(2,1)} %collective-permute-done.18), channel_id=1, source_target_pairs={{0,0},{1,23},{2,32},{3,19},{4,20},{5,69},{6,64},{7,21},{8,24},{9,1... | collective-permute-start | bytes 1290248 | tf_op jit(solution)/shard_map/ppermute | solution.py:29
  97.1 13.9 %collective-permute-start.21 = (s16[240,896]{1,0:T(8,128)(2,1)}, s16[240,896]{1,0:T(8,128)(2,1)S(1)}, u32[]{:S(2)}, u32[]{:S(2)}) collective-permute-start(s16[240,896]{1,0:T(8,128)(2,1)} %collective-permute-done.20), channel_id=1, source_target_pairs={{0,0},{1,23},{2,32},{3,19},{4,20},{5,69},{6,64},{7,21},{8,24},{9,1... | collective-permute-start | bytes 1290248 | tf_op jit(solution)/shard_map/ppermute | solution.py:29

commit v9 on v8

--- a/solution.py
+++ b/solution.py
@@ -64,14 +64,14 @@
 
 
 VIA = (
-    (0, 49, 53, 51, 4, 37, 6, 35, 12, 52, 43, 55, 13, 61, 14, 63,
-     3, 21, 1, 47, 7, 41, 2, 48, 24, 40, 29, 11, 25, 45, 46, 62,
-     17, 33, 54, 36, 16, 34, 22, 39, 5, 9, 26, 23, 28, 50, 30, 15,
-     8, 44, 18, 32, 27, 10, 19, 38, 56, 57, 42, 60, 20, 58, 31, 59),
-    (16, 36, 18, 7, 1, 50, 54, 26, 17, 5, 25, 59, 28, 2, 22, 3,
-     8, 32, 12, 23, 20, 38, 19, 42, 24, 9, 27, 44, 31, 10, 30, 15,
-     0, 61, 11, 34, 55, 33, 37, 39, 47, 52, 58, 40, 35, 45, 43, 56,
-     53, 13, 14, 49, 4, 41, 6, 48, 21, 57, 29, 62, 60, 51, 46, 63),
+    (4, 16, 3, 35, 1, 22, 6, 54, 24, 52, 27, 55, 17, 61, 9, 63,
+     28, 45, 19, 31, 5, 38, 10, 18, 23, 8, 43, 12, 29, 42, 14, 15,
+     49, 33, 53, 34, 0, 20, 51, 39, 21, 46, 25, 56, 44, 32, 30, 58,
+     48, 37, 2, 50, 7, 36, 26, 59, 57, 13, 41, 62, 40, 60, 47, 11),
+    (0, 49, 5, 48, 51, 53, 6, 20, 21, 13, 9, 59, 31, 12, 26, 2,
+     7, 37, 1, 32, 11, 25, 3, 40, 24, 41, 29, 47, 27, 57, 30, 44,
+     16, 33, 18, 52, 55, 38, 22, 23, 36, 61, 42, 39, 19, 62, 34, 43,
+     4, 45, 17, 28, 56, 54, 50, 35, 8, 58, 10, 60, 15, 46, 14, 63),
 )
 
 
@@ -201,14 +201,16 @@
     def run(columns):
         for half in range(2):
             acc[half] = sum_ref[half * rows:(half + 1) * rows, columns]
-        for i, (left_slot, right_slot) in enumerate(near_terms + far_terms):
+        terms = near_terms + far_terms
+        for i in range(0, len(terms), 2):
             if i == len(near_terms):
                 for copy in left_copies:
                     copy.wait()
-            block, right = left_stack[left_slot], right_stack[right_slot][:, columns]
+            blocks = [left_stack[left_slot] for left_slot, _ in terms[i:i + 2]]
+            right = jnp.concatenate([right_stack[right_slot][:, columns] for _, right_slot in terms[i:i + 2]])
             for half in range(2):
-                acc[half] += jnp.dot(
-                    block[:, half * depth:(half + 1) * depth], right, preferred_element_type=jnp.float32)
+                both = jnp.concatenate([block[:, half * depth:(half + 1) * depth] for block in blocks], axis=1)
+                acc[half] += jnp.dot(both, right, preferred_element_type=jnp.float32)
         out_ref[...] = jnp.concatenate([acc[0], acc[1]], axis=1)
 
     @pl.when(core == (0 if own else 1))

time: 114 us -> 114 us (level)
  the two profiles are of different devices: /device:TPU:16 before, /device:TPU:24 now
where the time goes in v9:
time: 114 us; the launch traced here: 113 us
  waiting for transfers between devices  52.3 us (46%)
  starting transfers between devices  36 us (32%)
  Pallas kernels  16.5 us (14%)
  local copies, waits for them, and re-layouts  6.54 us (6%)
  other arithmetic  1.99 us (2%)
    ppermute x22, waiting for transfers between devices, send(): return lax.ppermute(block, AXES, pairs)  52.3 us
    ppermute x22, starting transfers between devices, send(): return lax.ppermute(block, AXES, pairs)  36 us
    pallas_call x2, Pallas kernels, far_product(): pl.pallas_call(lambda *refs: far_kernel(own, len(left), len(right), *refs...  7.61 us
    pallas_call x1, Pallas kernels, near_product(): pl.pallas_call(lambda *refs: near_kernel(len(left), len(right), *refs), o...  4.61 us
    pallas_call x1, Pallas kernels, combine(): pl.pallas_call(combine_kernel, out_shape=jax.ShapeDtypeStruct((rows, cols...  2.51 us
  transfers between devices with their start and end apart: 22, of which 12 were waited for; matrix products, arithmetic and copies ran while one was open for 7% of the time, Pallas kernels for 7%

profile of v9, /device:TPU:24, one launch (start us, length us, event | category | flops | bytes accessed | tf_op | source)
XLA Modules:
  0.0 113.5 jit_solution(16383599845440037086)
XLA Ops:
  0.0 2.0 %collective-permute-start.5 = (bf16[448,896]{1,0:T(8,128)(2,1)}, bf16[448,896]{1,0:T(8,128)(2,1)}, u32[]{:S(2)}, u32[]{:S(2)}) collective-permute-start(bf16[448,896]{1,0:T(8,128)(2,1)} %refs_5_.1), channel_id=1, source_target_pairs={{0,64},{1,65},{2,66},{3,67},{4,68},{5,69},{6,70},{7,71},{8,72},{9,... | collective-permute-start | bytes 2408456 | tf_op jit(solution)/shard_map/ppermute | solution.py:29
  2.0 1.5 %fusion.2 = (bf16[448,448]{1,0:T(8,128)(2,1)S(1)}, bf16[448,448]{1,0:T(8,128)(2,1)S(1)}) fusion(bf16[448,896]{1,0:T(8,128)(2,1)} %param.6), kind=kLoop, calls=%fused_computation.21 | loop fusion | bytes 1605632 | tf_op jit(solution)/shard_map/jit(_roll_static)/slice | solution.py:319
  3.5 2.8 %collective-permute-start.8 = (bf16[448,896]{1,0:T(8,128)(2,1)S(1)}, bf16[448,896]{1,0:T(8,128)(2,1)S(1)}, u32[]{:S(2)}, u32[]{:S(2)}) collective-permute-start(bf16[448,896]{1,0:T(8,128)(2,1)S(1)} %copy-done), channel_id=1, source_target_pairs={{0,48},{1,49},{2,50},{3,51},{4,52},{5,53},{6,54},{7,55},{8,56},{9,... | collective-permute-start | bytes 2408456 | tf_op jit(solution)/shard_map/ppermute | solution.py:29
  7.6 1.8 %collective-permute-start.1 = (bf16[448,896]{1,0:T(8,128)(2,1)S(1)}, bf16[448,896]{1,0:T(8,128)(2,1)S(1)}, u32[]{:S(2)}, u32[]{:S(2)}) collective-permute-start(bf16[448,896]{1,0:T(8,128)(2,1)S(1)} %fusion.refs_0_), channel_id=1, source_target_pairs={{0,6},{1,7},{2,0},{3,1},{4,2},{5,3},{6,4},{7,5},{8,14},{9,15},{10,... | collective-permute-start | bytes 2408456 | tf_op jit(solution)/shard_map/ppermute | solution.py:29
  9.4 11.4 %collective-permute-done.5.refs_9_ = bf16[448,896]{1,0:T(8,128)(2,1)} collective-permute-done((bf16[448,896]{1,0:T(8,128)(2,1)}, bf16[448,896]{1,0:T(8,128)(2,1)}, u32[]{:S(2)}, u32[]{:S(2)}) %collective-permute-start.5) | collective-permute-done | bytes 802848 | tf_op jit(solution)/shard_map/ppermute | solution.py:29
  20.8 3.7 %collective-permute-start.6 = (bf16[448,896]{1,0:T(8,128)(2,1)S(1)}, bf16[448,896]{1,0:T(8,128)(2,1)}, u32[]{:S(2)}, u32[]{:S(2)}) collective-permute-start(bf16[448,896]{1,0:T(8,128)(2,1)S(1)} %fusion.refs_0_), channel_id=1, source_target_pairs={{0,1},{1,0},{2,3},{3,2},{4,5},{5,4},{6,7},{7,6},{8,9},{9,8},{10,11... | collective-permute-start | bytes 2408456 | tf_op jit(solution)/shard_map/ppermute | solution.py:29
  25.4 1.9 %collective-permute-done.7.refs_8_ = bf16[448,896]{1,0:T(8,128)(2,1)} collective-permute-done((bf16[448,896]{1,0:T(8,128)(2,1)S(1)}, bf16[448,896]{1,0:T(8,128)(2,1)}, u32[]{:S(2)}, u32[]{:S(2)}) %collective-permute-start.7) | collective-permute-done | bytes 802848 | tf_op jit(solution)/shard_map/ppermute | solution.py:29
  27.3 3.2 %collective-permute-start.10 = (bf16[448,896]{1,0:T(8,128)(2,1)}, bf16[448,896]{1,0:T(8,128)(2,1)}, u32[]{:S(2)}, u32[]{:S(2)}) collective-permute-start(bf16[448,896]{1,0:T(8,128)(2,1)} %collective-permute-done.5.refs_9_), channel_id=1, source_target_pairs={{0,48},{1,49},{2,50},{3,51},{4,52},{5,53},{6,54},{7,55},{8,56},{9,... | collective-permute-start | bytes 2408456 | tf_op jit(solution)/shard_map/ppermute | solution.py:29
  32.4 1.8 %collective-permute-start.4 = (bf16[224,896]{1,0:T(8,128)(2,1)}, bf16[224,896]{1,0:T(8,128)(2,1)}, u32[]{:S(2)}, u32[]{:S(2)}) collective-permute-start(bf16[224,896]{1,0:T(8,128)(2,1)} %slice.29), channel_id=1, source_target_pairs={{0,6},{1,7},{2,0},{3,1},{4,2},{5,3},{6,4},{7,5},{8,14},{9,15},{10,... | collective-permute-start | bytes 1204232 | tf_op jit(solution)/shard_map/ppermute | solution.py:29
  34.6 7.8 %collective-permute-done.6.refs_4_ = bf16[448,896]{1,0:T(8,128)(2,1)} collective-permute-done((bf16[448,896]{1,0:T(8,128)(2,1)S(1)}, bf16[448,896]{1,0:T(8,128)(2,1)}, u32[]{:S(2)}, u32[]{:S(2)}) %collective-permute-start.6) | collective-permute-done | bytes 802848 | tf_op jit(solution)/shard_map/ppermute | solution.py:29
  42.6 1.8 %collective-permute-start.11 = (bf16[448,896]{1,0:T(8,128)(2,1)}, bf16[448,896]{1,0:T(8,128)(2,1)S(1)}, u32[]{:S(2)}, u32[]{:S(2)}) collective-permute-start(bf16[448,896]{1,0:T(8,128)(2,1)} %collective-permute-done.6.refs_4_), channel_id=1, source_target_pairs={{0,6},{1,7},{2,0},{3,1},{4,2},{5,3},{6,4},{7,5},{8,14},{9,15},{10,... | collective-permute-start | bytes 2408456 | tf_op jit(solution)/shard_map/ppermute | solution.py:29
  45.4 1.0 constant_dynamic-update-slice_fusion.refs_2_
  46.5 3.3 %collective-permute-start.12 = (bf16[448,896]{1,0:T(8,128)(2,1)S(1)}, bf16[448,896]{1,0:T(8,128)(2,1)S(1)}, u32[]{:S(2)}, u32[]{:S(2)}) collective-permute-start(bf16[448,896]{1,0:T(8,128)(2,1)S(1)} %constant_dynamic-update-slice_fusion.refs_2_), channel_id=1, source_target_pairs={{0,1},{1,0},{2,3},{3,2},{4,5},{5,4},{6,7},{7,6},{8,9},{9,8},{10,11... | collective-permute-start | bytes 2408456 | tf_op jit(solution)/shard_map/ppermute | solution.py:29
  49.8 1.5 %collective-permute-start.15 = (bf16[448,896]{1,0:T(8,128)(2,1)}, bf16[448,896]{1,0:T(8,128)(2,1)S(1)}, u32[]{:S(2)}, u32[]{:S(2)}) collective-permute-start(bf16[448,896]{1,0:T(8,128)(2,1)} %collective-permute-done.5.refs_9_), channel_id=1, source_target_pairs={{0,16},{1,17},{2,18},{3,19},{4,20},{5,21},{6,22},{7,23},{8,24},{9,... | collective-permute-start | bytes 2408456 | tf_op jit(solution)/shard_map/ppermute | solution.py:29
  51.3 1.7 %collective-permute-start.14 = (bf16[448,896]{1,0:T(8,128)(2,1)}, bf16[448,896]{1,0:T(8,128)(2,1)S(1)}, u32[]{:S(2)}, u32[]{:S(2)}) collective-permute-start(bf16[448,896]{1,0:T(8,128)(2,1)} %collective-permute-done.10.refs_10_), channel_id=1, source_target_pairs={{0,48},{1,49},{2,50},{3,51},{4,52},{5,53},{6,54},{7,55},{8,56},{9,... | collective-permute-start | bytes 2408456 | tf_op jit(solution)/shard_map/ppermute | solution.py:29
  54.1 4.6 %near_product.1 = (f32[896,896]{1,0:T(8,128)S(1)}, bf16[8,448,896]{2,1,0:T(8,128)(2,1)S(1)}, bf16[8,448,896]{2,1,0:T(8,128)(2,1)S(1)}) custom-call(bf16[448,896]{1,0:T(8,128)(2,1)S(1)} %fusion.refs_0_, bf16[448,896]{1,0:T(8,128)(2,1)S(1)} %collective-permute-done.1.refs_1_, bf16[448,896]{1,0:T(8,128)(2,1)S(1)} %constant_dynamic-update-slice_fusion.refs_2_, ...), custom_call_target="tpu_custom_call" | custom-call | flops 1438646272 | bytes 12582912 | tf_op jit(solution)/shard_map/near_product/pallas_call | solution.py:165
  58.7 2.7 %collective-permute-done.13.refs_2_ = bf16[448,896]{1,0:T(8,128)(2,1)S(1)} collective-permute-done((bf16[448,896]{1,0:T(8,128)(2,1)}, bf16[448,896]{1,0:T(8,128)(2,1)S(1)}, u32[]{:S(2)}, u32[]{:S(2)}) %collective-permute-start.13) | collective-permute-done | bytes 802848 | tf_op jit(solution)/shard_map/ppermute | solution.py:29
  61.4 1.2 %collective-permute-done.11.refs_0_ = bf16[448,896]{1,0:T(8,128)(2,1)S(1)} collective-permute-done((bf16[448,896]{1,0:T(8,128)(2,1)}, bf16[448,896]{1,0:T(8,128)(2,1)S(1)}, u32[]{:S(2)}, u32[]{:S(2)}) %collective-permute-start.11) | collective-permute-done | bytes 802848 | tf_op jit(solution)/shard_map/ppermute | solution.py:29
  62.6 3.7 %collective-permute-done.12.refs_1_ = bf16[448,896]{1,0:T(8,128)(2,1)S(1)} collective-permute-done((bf16[448,896]{1,0:T(8,128)(2,1)S(1)}, bf16[448,896]{1,0:T(8,128)(2,1)S(1)}, u32[]{:S(2)}, u32[]{:S(2)}) %collective-permute-start.12) | collective-permute-done | bytes 802848 | tf_op jit(solution)/shard_map/ppermute | solution.py:29
  66.4 2.6 %collective-permute-done.15.refs_4_ = bf16[448,896]{1,0:T(8,128)(2,1)S(1)} collective-permute-done((bf16[448,896]{1,0:T(8,128)(2,1)}, bf16[448,896]{1,0:T(8,128)(2,1)S(1)}, u32[]{:S(2)}, u32[]{:S(2)}) %collective-permute-start.15) | collective-permute-done | bytes 802848 | tf_op jit(solution)/shard_map/ppermute | solution.py:29
  68.9 4.3 %far_product.2 = (f32[448,896]{1,0:T(8,128)S(1)}, bf16[8,448,896]{2,1,0:T(8,128)(2,1)S(1)}, bf16[8,448,896]{2,1,0:T(8,128)(2,1)S(1)}) custom-call(bf16[448,896]{1,0:T(8,128)(2,1)S(1)} %collective-permute-done.11.refs_0_, bf16[448,896]{1,0:T(8,128)(2,1)S(1)} %collective-permute-done.12.refs_1_, ...), custom_call_target="tpu_custom_call", output_to_operand_aliasing={{1}: (6, {}), {2}: (7, {})} | custom-call | flops 2157969408 | bytes 12582912 | tf_op jit(solution)/shard_map/far_product/pallas_call | solution.py:232
  73.3 3.3 %far_product.3.keep_ref = f32[448,896]{1,0:T(8,128)S(1)} custom-call(f32[896,896]{1,0:T(8,128)S(1)} %get-tuple-element.30.refs_5_.refs_0_, bf16[8,448,896]{2,1,0:T(8,128)(2,1)S(1)} %get-tuple-element.34.refs_1_, bf16[8,448,896]{2,1,0:T(8,128)(2,1)S(1)} %get-tuple-element.35.refs_2_), custom_call_target="tpu_custom_call" | custom-call | flops 2157969408 | bytes 12582912 | tf_op jit(solution)/shard_map/far_product/pallas_call | solution.py:232
  76.8 1.7 %join.1 = (f32[448,448]{1,0:T(8,128)S(1)}, f32[448,448]{1,0:T(8,128)}, s16[240,896]{1,0:T(8,128)(2,1)S(1)}, s16[240,896]{1,0:T(8,128)(2,1)S(1)}) custom-call(f32[448,896]{1,0:T(8,128)S(1)} %far_product.3.keep_ref, f32[448,896]{1,0:T(8,128)S(1)} %collective-permute-done.16.got_ref), custom_call_target="tpu_custom_call" | custom-call | flops 1605632 | bytes 4816896 | tf_op jit(solution)/shard_map/join/pallas_call | solution.py:277
  78.5 4.8 %collective-permute-start.18 = (s16[240,896]{1,0:T(8,128)(2,1)S(1)}, s16[240,896]{1,0:T(8,128)(2,1)}, u32[]{:S(2)}, u32[]{:S(2)}) collective-permute-start(s16[240,896]{1,0:T(8,128)(2,1)S(1)} %get-tuple-element.39), channel_id=1, source_target_pairs={{0,2},{1,81},{2,16},{3,0},{4,68},{5,82},{6,80},{7,7},{8,8},{9,72},... | collective-permute-start | bytes 1290248 | tf_op jit(solution)/shard_map/ppermute | solution.py:29
  83.3 2.6 %collective-permute-start.20 = (s16[240,896]{1,0:T(8,128)(2,1)S(1)}, s16[240,896]{1,0:T(8,128)(2,1)}, u32[]{:S(2)}, u32[]{:S(2)}) collective-permute-start(s16[240,896]{1,0:T(8,128)(2,1)S(1)} %get-tuple-element.40), channel_id=1, source_target_pairs={{0,2},{1,81},{2,16},{3,0},{4,68},{5,82},{6,80},{7,7},{8,8},{9,72},... | collective-permute-start | bytes 1290248 | tf_op jit(solution)/shard_map/ppermute | solution.py:29
  86.1 5.5 %collective-permute-done.18 = s16[240,896]{1,0:T(8,128)(2,1)} collective-permute-done((s16[240,896]{1,0:T(8,128)(2,1)S(1)}, s16[240,896]{1,0:T(8,128)(2,1)}, u32[]{:S(2)}, u32[]{:S(2)}) %collective-permute-start.18) | collective-permute-done | bytes 430112 | tf_op jit(solution)/shard_map/ppermute | solution.py:29
  91.7 1.9 %collective-permute-start.19 = (s16[240,896]{1,0:T(8,128)(2,1)}, s16[240,896]{1,0:T(8,128)(2,1)S(1)}, u32[]{:S(2)}, u32[]{:S(2)}) collective-permute-start(s16[240,896]{1,0:T(8,128)(2,1)} %collective-permute-done.18), channel_id=1, source_target_pairs={{0,48},{1,113},{2,0},{3,53},{4,69},{5,116},{6,71},{7,112},{8,8},{9... | collective-permute-start | bytes 1290248 | tf_op jit(solution)/shard_map/ppermute | solution.py:29
  93.6 2.9 %collective-permute-done.20 = s16[240,896]{1,0:T(8,128)(2,1)} collective-permute-done((s16[240,896]{1,0:T(8,128)(2,1)S(1)}, s16[240,896]{1,0:T(8,128)(2,1)}, u32[]{:S(2)}, u32[]{:S(2)}) %collective-permute-start.20) | collective-permute-done | bytes 430112 | tf_op jit(solution)/shard_map/ppermute | solution.py:29
  96.5 1.9 %collective-permute-start.21 = (s16[240,896]{1,0:T(8,128)(2,1)}, s16[240,896]{1,0:T(8,128)(2,1)S(1)}, u32[]{:S(2)}, u32[]{:S(2)}) collective-permute-start(s16[240,896]{1,0:T(8,128)(2,1)} %collective-permute-done.20), channel_id=1, source_target_pairs={{0,48},{1,113},{2,0},{3,53},{4,69},{5,116},{6,71},{7,112},{8,8},{9... | collective-permute-start | bytes 1290248 | tf_op jit(solution)/shard_map/ppermute | solution.py:29
  98.6 7.6 %collective-permute-done.19.top_ref = s16[240,896]{1,0:T(8,128)(2,1)S(1)} collective-permute-done((s16[240,896]{1,0:T(8,128)(2,1)}, s16[240,896]{1,0:T(8,128)(2,1)S(1)}, u32[]{:S(2)}, u32[]{:S(2)}) %collective-permute-start.19) | collective-permute-done | bytes 430112 | tf_op jit(solution)/shard_map/ppermute | solution.py:29
  106.2 4.8 %collective-permute-done.21.bottom_ref = s16[240,896]{1,0:T(8,128)(2,1)S(1)} collective-permute-done((s16[240,896]{1,0:T(8,128)(2,1)}, s16[240,896]{1,0:T(8,128)(2,1)S(1)}, u32[]{:S(2)}, u32[]{:S(2)}) %collective-permute-start.21) | collective-permute-done | bytes 430112 | tf_op jit(solution)/shard_map/ppermute | solution.py:29
  111.0 2.5 %combine.1 = f32[448,896]{1,0:T(8,128)} custom-call(f32[448,448]{1,0:T(8,128)S(1)} %get-tuple-element.37.own_ref, f32[448,448]{1,0:T(8,128)S(1)} %collective-permute-done.17.side_ref, s16[240,896]{1,0:T(8,128)(2,1)S(1)} %collective-permute-done.19.top_ref, s16[240,896]{1,0:T(8,128)(2,1)S(1)} %collective-permute-done.21.bottom_ref, ...), custom_call_target="tpu_custom_call" | custom-call | flops 1605632 | bytes 4816896 | tf_op jit(solution)/shard_map/combine/pallas_call | solution.py:300
  (57 shorter events, 7.2 us)
Async XLA Ops:
  0.0 3.5 %copy-start = (bf16[448,896]{1,0:T(8,128)(2,1)S(1)}, bf16[448,896]{1,0:T(8,128)(2,1)}, u32[]{:S(2)}) copy-start(bf16[448,896]{1,0:T(8,128)(2,1)} %refs_5_.1) | copy-start | bytes 2408452
  0.0 3.5 %collective-permute-start = (bf16[448,896]{1,0:T(8,128)(2,1)}, bf16[448,896]{1,0:T(8,128)(2,1)S(1)}, u32[]{:S(2)}, u32[]{:S(2)}) collective-permute-start(bf16[448,896]{1,0:T(8,128)(2,1)} %param.6), channel_id=1, source_target_pairs={{0,8},{1,9},{2,10},{3,11},{4,12},{5,13},{6,14},{7,15},{8,0},{9,1},... | collective-permute-start | bytes 2408456 | tf_op jit(solution)/shard_map/ppermute | solution.py:29
  0.0 20.8 %collective-permute-start.5 = (bf16[448,896]{1,0:T(8,128)(2,1)}, bf16[448,896]{1,0:T(8,128)(2,1)}, u32[]{:S(2)}, u32[]{:S(2)}) collective-permute-start(bf16[448,896]{1,0:T(8,128)(2,1)} %refs_5_.1), channel_id=1, source_target_pairs={{0,64},{1,65},{2,66},{3,67},{4,68},{5,69},{6,70},{7,71},{8,72},{9,... | collective-permute-start | bytes 2408456 | tf_op jit(solution)/shard_map/ppermute | solution.py:29
  2.0 4.5 %copy-start.3 = (bf16[448,896]{1,0:T(8,128)(2,1)S(1)}, bf16[448,896]{1,0:T(8,128)(2,1)}, u32[]{:S(2)}) copy-start(bf16[448,896]{1,0:T(8,128)(2,1)} %param.6) | copy-start | bytes 2408452
  3.5 21.0 %collective-permute-start.8 = (bf16[448,896]{1,0:T(8,128)(2,1)S(1)}, bf16[448,896]{1,0:T(8,128)(2,1)S(1)}, u32[]{:S(2)}, u32[]{:S(2)}) collective-permute-start(bf16[448,896]{1,0:T(8,128)(2,1)S(1)} %copy-done), channel_id=1, source_target_pairs={{0,48},{1,49},{2,50},{3,51},{4,52},{5,53},{6,54},{7,55},{8,56},{9,... | collective-permute-start | bytes 2408456 | tf_op jit(solution)/shard_map/ppermute | solution.py:29
  6.3 21.0 %collective-permute-start.7 = (bf16[448,896]{1,0:T(8,128)(2,1)S(1)}, bf16[448,896]{1,0:T(8,128)(2,1)}, u32[]{:S(2)}, u32[]{:S(2)}) collective-permute-start(bf16[448,896]{1,0:T(8,128)(2,1)S(1)} %copy-done), channel_id=1, source_target_pairs={{0,16},{1,17},{2,18},{3,19},{4,20},{5,21},{6,22},{7,23},{8,24},{9,... | collective-permute-start | bytes 2408456 | tf_op jit(solution)/shard_map/ppermute | solution.py:29
  6.5 27.6 %copy-start.4 = (s32[7168]{0:T(1024)S(1)}, s32[7168]{0:T(1024)}, u32[]{:S(2)}) copy-start(s32[7168]{0:T(1024)} %param.10) | copy-start | bytes 86020
  6.6 27.7 %copy-start.5 = (s32[7168]{0:T(1024)S(1)}, s32[7168]{0:T(1024)}, u32[]{:S(2)}) copy-start(s32[7168]{0:T(1024)} %param.11) | copy-start | bytes 86020
  7.3 27.1 %copy-start.7 = (f32[80]{0:T(128)S(1)}, f32[80]{0:T(128)}, u32[]{:S(2)}) copy-start(f32[80]{0:T(128)} %param.8) | copy-start | bytes 964
  7.3 45.7 %copy-start.6 = (f32[1000]{0:T(1024)S(1)}, f32[1000]{0:T(1024)}, u32[]{:S(2)}) copy-start(f32[1000]{0:T(1024)} %param.9) | copy-start | bytes 12004
  7.4 23.2 %collective-permute-start.2 = (bf16[448,896]{1,0:T(8,128)(2,1)S(1)}, bf16[448,896]{1,0:T(8,128)(2,1)S(1)}, u32[]{:S(2)}, u32[]{:S(2)}) collective-permute-start(bf16[448,896]{1,0:T(8,128)(2,1)S(1)} %fusion.refs_0_), channel_id=1, source_target_pairs={{0,2},{1,3},{2,4},{3,5},{4,6},{5,7},{6,0},{7,1},{8,10},{9,11},{10,... | collective-permute-start | bytes 2408456 | tf_op jit(solution)/shard_map/ppermute | solution.py:29
  7.6 23.9 %collective-permute-start.1 = (bf16[448,896]{1,0:T(8,128)(2,1)S(1)}, bf16[448,896]{1,0:T(8,128)(2,1)S(1)}, u32[]{:S(2)}, u32[]{:S(2)}) collective-permute-start(bf16[448,896]{1,0:T(8,128)(2,1)S(1)} %fusion.refs_0_), channel_id=1, source_target_pairs={{0,6},{1,7},{2,0},{3,1},{4,2},{5,3},{6,4},{7,5},{8,14},{9,15},{10,... | collective-permute-start | bytes 2408456 | tf_op jit(solution)/shard_map/ppermute | solution.py:29
  20.8 21.5 %collective-permute-start.6 = (bf16[448,896]{1,0:T(8,128)(2,1)S(1)}, bf16[448,896]{1,0:T(8,128)(2,1)}, u32[]{:S(2)}, u32[]{:S(2)}) collective-permute-start(bf16[448,896]{1,0:T(8,128)(2,1)S(1)} %fusion.refs_0_), channel_id=1, source_target_pairs={{0,1},{1,0},{2,3},{3,2},{4,5},{5,4},{6,7},{7,6},{8,9},{9,8},{10,11... | collective-permute-start | bytes 2408456 | tf_op jit(solution)/shard_map/ppermute | solution.py:29
  24.5 0.9 copy-start.1
  27.3 22.5 %collective-permute-start.9 = (bf16[448,896]{1,0:T(8,128)(2,1)}, bf16[448,896]{1,0:T(8,128)(2,1)}, u32[]{:S(2)}, u32[]{:S(2)}) collective-permute-start(bf16[448,896]{1,0:T(8,128)(2,1)} %collective-permute-done.7.refs_8_), channel_id=1, source_target_pairs={{0,16},{1,17},{2,18},{3,19},{4,20},{5,21},{6,22},{7,23},{8,24},{9,... | collective-permute-start | bytes 2408456 | tf_op jit(solution)/shard_map/ppermute | solution.py:29
  27.3 24.0 %collective-permute-start.10 = (bf16[448,896]{1,0:T(8,128)(2,1)}, bf16[448,896]{1,0:T(8,128)(2,1)}, u32[]{:S(2)}, u32[]{:S(2)}) collective-permute-start(bf16[448,896]{1,0:T(8,128)(2,1)} %collective-permute-done.5.refs_9_), channel_id=1, source_target_pairs={{0,48},{1,49},{2,50},{3,51},{4,52},{5,53},{6,54},{7,55},{8,56},{9,... | collective-permute-start | bytes 2408456 | tf_op jit(solution)/shard_map/ppermute | solution.py:29
  31.3 11.2 %collective-permute-start.3 = (bf16[224,896]{1,0:T(8,128)(2,1)}, bf16[224,896]{1,0:T(8,128)(2,1)}, u32[]{:S(2)}, u32[]{:S(2)}) collective-permute-start(bf16[224,896]{1,0:T(8,128)(2,1)} %slice.28), channel_id=1, source_target_pairs={{0,2},{1,3},{2,4},{3,5},{4,6},{5,7},{6,0},{7,1},{8,10},{9,11},{10,... | collective-permute-start | bytes 1204232 | tf_op jit(solution)/shard_map/ppermute | solution.py:29
  32.4 13.0 %collective-permute-start.4 = (bf16[224,896]{1,0:T(8,128)(2,1)}, bf16[224,896]{1,0:T(8,128)(2,1)}, u32[]{:S(2)}, u32[]{:S(2)}) collective-permute-start(bf16[224,896]{1,0:T(8,128)(2,1)} %slice.29), channel_id=1, source_target_pairs={{0,6},{1,7},{2,0},{3,1},{4,2},{5,3},{6,4},{7,5},{8,14},{9,15},{10,... | collective-permute-start | bytes 1204232 | tf_op jit(solution)/shard_map/ppermute | solution.py:29
  34.4 19.7 %copy-start.2 = (bf16[448,896]{1,0:T(8,128)(2,1)S(1)}, bf16[448,896]{1,0:T(8,128)(2,1)}, u32[]{:S(2)}) copy-start(bf16[448,896]{1,0:T(8,128)(2,1)} %copy-done.1) | copy-start | bytes 2408452
  42.3 19.1 %collective-permute-start.13 = (bf16[448,896]{1,0:T(8,128)(2,1)}, bf16[448,896]{1,0:T(8,128)(2,1)S(1)}, u32[]{:S(2)}, u32[]{:S(2)}) collective-permute-start(bf16[448,896]{1,0:T(8,128)(2,1)} %collective-permute-done.6.refs_4_), channel_id=1, source_target_pairs={{0,2},{1,3},{2,4},{3,5},{4,6},{5,7},{6,0},{7,1},{8,10},{9,11},{10,... | collective-permute-start | bytes 2408456 | tf_op jit(solution)/shard_map/ppermute | solution.py:29
  42.6 20.1 %collective-permute-start.11 = (bf16[448,896]{1,0:T(8,128)(2,1)}, bf16[448,896]{1,0:T(8,128)(2,1)S(1)}, u32[]{:S(2)}, u32[]{:S(2)}) collective-permute-start(bf16[448,896]{1,0:T(8,128)(2,1)} %collective-permute-done.6.refs_4_), channel_id=1, source_target_pairs={{0,6},{1,7},{2,0},{3,1},{4,2},{5,3},{6,4},{7,5},{8,14},{9,15},{10,... | collective-permute-start | bytes 2408456 | tf_op jit(solution)/shard_map/ppermute | solution.py:29
  46.5 19.9 %collective-permute-start.12 = (bf16[448,896]{1,0:T(8,128)(2,1)S(1)}, bf16[448,896]{1,0:T(8,128)(2,1)S(1)}, u32[]{:S(2)}, u32[]{:S(2)}) collective-permute-start(bf16[448,896]{1,0:T(8,128)(2,1)S(1)} %constant_dynamic-update-slice_fusion.refs_2_), channel_id=1, source_target_pairs={{0,1},{1,0},{2,3},{3,2},{4,5},{5,4},{6,7},{7,6},{8,9},{9,8},{10,11... | collective-permute-start | bytes 2408456 | tf_op jit(solution)/shard_map/ppermute | solution.py:29
  49.8 19.1 %collective-permute-start.15 = (bf16[448,896]{1,0:T(8,128)(2,1)}, bf16[448,896]{1,0:T(8,128)(2,1)S(1)}, u32[]{:S(2)}, u32[]{:S(2)}) collective-permute-start(bf16[448,896]{1,0:T(8,128)(2,1)} %collective-permute-done.5.refs_9_), channel_id=1, source_target_pairs={{0,16},{1,17},{2,18},{3,19},{4,20},{5,21},{6,22},{7,23},{8,24},{9,... | collective-permute-start | bytes 2408456 | tf_op jit(solution)/shard_map/ppermute | solution.py:29
  51.3 17.7 %collective-permute-start.14 = (bf16[448,896]{1,0:T(8,128)(2,1)}, bf16[448,896]{1,0:T(8,128)(2,1)S(1)}, u32[]{:S(2)}, u32[]{:S(2)}) collective-permute-start(bf16[448,896]{1,0:T(8,128)(2,1)} %collective-permute-done.10.refs_10_), channel_id=1, source_target_pairs={{0,48},{1,49},{2,50},{3,51},{4,52},{5,53},{6,54},{7,55},{8,56},{9,... | collective-permute-start | bytes 2408456 | tf_op jit(solution)/shard_map/ppermute | solution.py:29
  73.2 3.5 %collective-permute-start.16 = (f32[448,896]{1,0:T(8,128)S(1)}, f32[448,896]{1,0:T(8,128)S(1)}, u32[]{:S(2)}, u32[]{:S(2)}) collective-permute-start(f32[448,896]{1,0:T(8,128)S(1)} %get-tuple-element.36), channel_id=1, source_target_pairs={{0,8},{1,9},{2,10},{3,11},{4,12},{5,13},{6,14},{7,15},{8,0},{9,1},... | collective-permute-start | bytes 4816904 | tf_op jit(solution)/shard_map/ppermute | solution.py:29
  78.5 13.2 %collective-permute-start.18 = (s16[240,896]{1,0:T(8,128)(2,1)S(1)}, s16[240,896]{1,0:T(8,128)(2,1)}, u32[]{:S(2)}, u32[]{:S(2)}) collective-permute-start(s16[240,896]{1,0:T(8,128)(2,1)S(1)} %get-tuple-element.39), channel_id=1, source_target_pairs={{0,2},{1,81},{2,16},{3,0},{4,68},{5,82},{6,80},{7,7},{8,8},{9,72},... | collective-permute-start | bytes 1290248 | tf_op jit(solution)/shard_map/ppermute | solution.py:29
  83.3 13.2 %collective-permute-start.20 = (s16[240,896]{1,0:T(8,128)(2,1)S(1)}, s16[240,896]{1,0:T(8,128)(2,1)}, u32[]{:S(2)}, u32[]{:S(2)}) collective-permute-start(s16[240,896]{1,0:T(8,128)(2,1)S(1)} %get-tuple-element.40), channel_id=1, source_target_pairs={{0,2},{1,81},{2,16},{3,0},{4,68},{5,82},{6,80},{7,7},{8,8},{9,72},... | collective-permute-start | bytes 1290248 | tf_op jit(solution)/shard_map/ppermute | solution.py:29
  85.9 12.7 %collective-permute-start.17 = (f32[448,448]{1,0:T(8,128)}, f32[448,448]{1,0:T(8,128)S(1)}, u32[]{:S(2)}, u32[]{:S(2)}) collective-permute-start(f32[448,448]{1,0:T(8,128)} %get-tuple-element.38), channel_id=1, source_target_pairs={{0,8},{1,9},{2,10},{3,11},{4,12},{5,13},{6,14},{7,15},{8,0},{9,1},... | collective-permute-start | bytes 2408456 | tf_op jit(solution)/shard_map/ppermute | solution.py:29
  91.7 14.5 %collective-permute-start.19 = (s16[240,896]{1,0:T(8,128)(2,1)}, s16[240,896]{1,0:T(8,128)(2,1)S(1)}, u32[]{:S(2)}, u32[]{:S(2)}) collective-permute-start(s16[240,896]{1,0:T(8,128)(2,1)} %collective-permute-done.18), channel_id=1, source_target_pairs={{0,48},{1,113},{2,0},{3,53},{4,69},{5,116},{6,71},{7,112},{8,8},{9... | collective-permute-start | bytes 1290248 | tf_op jit(solution)/shard_map/ppermute | solution.py:29
  96.5 14.5 %collective-permute-start.21 = (s16[240,896]{1,0:T(8,128)(2,1)}, s16[240,896]{1,0:T(8,128)(2,1)S(1)}, u32[]{:S(2)}, u32[]{:S(2)}) collective-permute-start(s16[240,896]{1,0:T(8,128)(2,1)} %collective-permute-done.20), channel_id=1, source_target_pairs={{0,48},{1,113},{2,0},{3,53},{4,69},{5,116},{6,71},{7,112},{8,8},{9... | collective-permute-start | bytes 1290248 | tf_op jit(solution)/shard_map/ppermute | solution.py:29
